TPU v7x, 32 devices: a whole 2x2x4 slice. The times are simulated.
32 devices in a mesh: replica: 8 (over z, x), shard: 4 (over y, core).
Axes of the slice: x: 2, y: 2, z: 4, core: 2. Of those that a mesh axis runs over, the one named last changes fastest.
Arguments:
- tokens: bfloat16 [8192, 768], P(('replica', 'shard')), may hold values from -6 to 6
- pass_ids: int32 [8192], P(('replica', 'shard')), may hold values from 0 to 4
- seg_ids: int32 [8192], P('replica'), may hold values from 0 to 19, never falling along the last dimension, each value on 1 to 800 neighbouring positions
- cotangent: bfloat16 [8192, 768], P(('replica', 'shard')), may hold values from -6 to 6
- pass_table: bfloat16 [768, 5], P('shard'), may hold values from -3 to 3
- norm1_gain: bfloat16 [768], P('shard'), may hold values from 0.5 to 1.5
- norm1_bias: bfloat16 [768], P('shard'), may hold values from -2 to 2
- qkv_weight: bfloat16 [768, 2304], P('shard'), may hold values from -0.21875 to 0.21875
- out_weight: bfloat16 [768, 768], P('shard'), may hold values from -0.875 to 0.875
- out_bias: bfloat16 [768], P('shard'), may hold values from -2 to 2
- norm2_gain: bfloat16 [768], P('shard'), may hold values from 0.5 to 1.5
- norm2_bias: bfloat16 [768], P('shard'), may hold values from -2 to 2
- up_weight: bfloat16 [768, 3072], P('shard'), may hold values from -0.21875 to 0.21875
- up_bias: bfloat16 [3072], P('shard'), may hold values from -3 to 3
- down_weight: bfloat16 [3072, 768], P('shard'), may hold values from -0.109375 to 0.109375
- down_bias: bfloat16 [768], P('shard'), may hold values from -2 to 2
Outputs:
- output: bfloat16 [8192, 768], P(('replica', 'shard'))
- tokens_grad: bfloat16 [8192, 768], P(('replica', 'shard'))
- pass_table_grad: float32 [768, 5], P('shard')
- norm1_gain_grad: float32 [768], P('shard')
- norm1_bias_grad: float32 [768], P('shard')
- qkv_weight_grad: float32 [768, 2304], P('shard')
- out_weight_grad: float32 [768, 768], P('shard')
- out_bias_grad: float32 [768], P('shard')
- norm2_gain_grad: float32 [768], P('shard')
- norm2_bias_grad: float32 [768], P('shard')
- up_weight_grad: float32 [768, 3072], P('shard')
- up_bias_grad: float32 [3072], P('shard')
- down_weight_grad: float32 [3072, 768], P('shard')
- down_bias_grad: float32 [768], P('shard')
All inputs are finite; a program needn't handle non-finite values.
Results may differ from a plain program's by a relative error of at most 0.014.
Values may be sent and summed in bfloat16 or wider, within the bound.
No kernel may reach another device: no remote copies, remote signals or barrier semaphores. Data moves between devices by JAX's collectives and lax.ppermute only.
A program may use at most 128 MiB of HBM per device.

v0:
```python
import functools

import jax
import jax.numpy as jnp
from jax import lax
from jax.experimental import pallas as pl
from jax.experimental.pallas import tpu as pltpu
from jax.sharding import PartitionSpec as P

HD = 64
epsilon = 1e-05
score_scale = 0.125
masked_score = -1e30
f32 = jnp.float32
bf16 = jnp.bfloat16

CORE = [(i, i ^ 1) for i in range(4)]
ROWY = [(i, i ^ 2) for i in range(4)]
BOTH = [(i, i ^ 3) for i in range(4)]


def contract(left, right, ld, rd):
    return lax.dot_general(left, right, (((ld,), (rd,)), ((), ())), preferred_element_type=f32)


def unit_of(values):
    centred = values - jnp.mean(values, -1, keepdims=True)
    inverse = lax.rsqrt(jnp.mean(centred * centred, -1, keepdims=True) + epsilon)
    return centred * inverse, inverse


def norm_back(grad_rows, unit_rows, inverse, gain):
    scaled = grad_rows * gain
    return inverse * (
        scaled
        - jnp.mean(scaled, -1, keepdims=True)
        - unit_rows * jnp.mean(scaled * unit_rows, -1, keepdims=True)
    )


def at_rows(index, size):
    return pl.ds(pl.multiple_of(index * size, size), size)


def pack_body(x_ref, ids_ref, table_ref, g1_ref, b1_ref, ob_ref, g2_ref, b2_ref, db_ref, out_ref):
    passes, part = table_ref.shape
    rows = ids_ref.shape[0]
    out_ref[0:rows] = x_ref[...]
    ext = jnp.zeros((16, out_ref.shape[1]), bf16)
    out_ref[rows:] = ext
    out_ref[rows:rows + passes, 0:part] = table_ref[...]
    for i, ref in enumerate((g1_ref, b1_ref, ob_ref, g2_ref, b2_ref, db_ref)):
        out_ref[rows + 5 + i:rows + 6 + i, 0:part] = ref[...].astype(f32).reshape(1, part).astype(bf16)
    out_ref[rows + 11:rows + 12, 0:rows] = ids_ref[...].astype(f32).reshape(1, rows).astype(bf16)


def norm_body(rank_ref, x0, x1, x2, x3,
              sin_ref, par_ref, nrm_ref, late_ref, unit_ref, inv_ref, ids_ref):
    rank = rank_ref[0]
    rows, width = sin_ref.shape
    part = width // 4
    ext = [b[rows:rows + 16, 0:part].astype(f32) for b in (x0, x1, x2, x3)]
    cols = []
    for j in range(4):
        acc = jnp.zeros_like(ext[0])
        for k in range(4):
            acc = jnp.where((rank ^ k) == j, ext[k], acc)
        cols.append(acc)
    par = jnp.concatenate(cols, axis=1)
    par_ref[...] = par
    table = par[0:8].astype(bf16)
    gain, bias = par[5:6], par[6:7]
    for k, b in enumerate((x0, x1, x2, x3)):
        ids = b[rows + 11:rows + 12, 0:rows].astype(f32)
        ids_ref[k:k + 1] = ids
        one = (lax.broadcasted_iota(jnp.int32, (8, rows), 0).astype(f32) == ids).astype(bf16)
        x = b[0:rows].astype(f32) + contract(one, table, 0, 0)
        if k == 0:
            sin_ref[...] = x
        unit, inverse = unit_of(x)
        at = at_rows(rank ^ k, rows)
        unit_ref[at] = unit.astype(bf16)
        inv_ref[at] = inverse
        normed = (unit * gain + bias).astype(bf16)
        nrm_ref[at] = normed
        late_ref[at] = normed


def front_body(rank_ref, segc_ref, segr_ref, nrm_ref, w0, w1, w2, w3, wout_ref,
               send_ref, keep_ref, far_ref, qkv_ref, ctx_ref, lse_ref, wq_ref, lse_s, head_s, ctx_s, top_s):
    rank = rank_ref[0]
    rows, width = keep_ref.shape
    part = width // 4
    for k, w in enumerate((w0[...], w1[...], w2[0:part], w3[...])):
        wq_ref[at_rows(rank ^ k, part)] = w
    qkv_ref[...] = jnp.dot(nrm_ref[...], wq_ref[...], preferred_element_type=f32).astype(bf16)
    heads = part // HD
    total_rows = nrm_ref.shape[0]
    for i in range(3 * heads):
        head = qkv_ref[:, i * HD:(i + 1) * HD]
        head_s[i] = head * jnp.asarray(score_scale, bf16) if i < heads else head

    def one_head(h, carry):
        q, key, val = head_s[h], head_s[heads + h], head_s[2 * heads + h]
        for i in range(total_rows // rows):
            lo, nk = i * rows, (i + 1) * rows
            sc = contract(q[lo:nk], key[:nk], 1, 1)
            qpos = lo + lax.broadcasted_iota(jnp.int32, (rows, nk), 0)
            kpos = lax.broadcasted_iota(jnp.int32, (rows, nk), 1)
            seen = (segc_ref[lo:nk] == segr_ref[:, :nk]) & (kpos <= qpos)
            sc = jnp.where(seen, sc, masked_score)
            top = jnp.max(sc, -1, keepdims=True)
            e = jnp.exp(sc - top)
            total = jnp.sum(e, -1, keepdims=True)
            prob = (e * (1.0 / total)).astype(bf16)
            ctx_s[h, lo:nk] = jnp.dot(prob, val[:nk], preferred_element_type=f32).astype(bf16)
            top_s[h, lo:nk] = top + jnp.log(total)
        return carry

    lax.fori_loop(0, heads, one_head, 0)
    for h in range(heads):
        ctx_ref[:, h * HD:(h + 1) * HD] = ctx_s[h]
        lse_s[:, h:h + 1] = top_s[h]
    lse_ref[...] = lse_s[...].T[0:8]
    for i, k in enumerate((1, 3)):
        send_ref[i * rows:(i + 1) * rows] = jnp.dot(
            ctx_ref[at_rows(rank ^ k, rows)], wout_ref[...], preferred_element_type=f32).astype(bf16)
    for ref, k in ((keep_ref, 0), (far_ref, 2)):
        ref[...] = jnp.dot(ctx_ref[at_rows(rank ^ k, rows)], wout_ref[...], preferred_element_type=f32)


def mid_body(sin_ref, par_ref, keep_ref, recv_ref, yrecv_ref, mid_ref, nrm_ref):
    rows = sin_ref.shape[0]
    mid = (sin_ref[...] + keep_ref[...] + recv_ref[0:rows].astype(f32)
           + yrecv_ref[...].astype(f32) + par_ref[7:8])
    mid_ref[...] = mid
    unit, _ = unit_of(mid)
    nrm_ref[...] = (unit * par_ref[8:9] + par_ref[9:10]).astype(bf16)


def gelu_pair(v):
    c0, c1 = 0.7978845608028654, 0.044715
    sq = v * v
    t = jnp.tanh(c0 * v * (1.0 + c1 * sq))
    half = 0.5 * (1.0 + t)
    return v * half, half + 0.5 * v * (1.0 - t * t) * (c0 * (1.0 + 3.0 * c1 * sq))


def feed_body(rank_ref, n0, n1, n2, n3, c0, g1, g2, g3, u0, pair_ref, ub_ref, dw_ref,
              send_ref, keep_ref, far_ref, act_ref, pg_ref, wu_s):
    rank = rank_ref[0]
    rows, width = n0.shape
    part = width // 4
    ub_row = ub_ref[...].astype(f32).reshape(1, ub_ref.shape[0])
    side = rank_ref[2]
    wu_s[at_rows(rank, part)] = u0[...]
    wu_s[at_rows(rank ^ 1, part)] = g1[rows:]

    @pl.when(side == 0)
    def _():
        wu_s[at_rows(rank ^ 2, part)] = g2[rows:]
        wu_s[at_rows(rank ^ 3, part)] = pair_ref[...]

    @pl.when(side == 1)
    def _():
        wu_s[at_rows(rank ^ 2, part)] = pair_ref[...]
        wu_s[at_rows(rank ^ 3, part)] = g3[rows:]

    for k, (n, c) in enumerate(((n0, c0[...]), (n1, g1[0:rows]), (n2, g2[0:rows]), (n3, g3[0:rows]))):
        pre = jnp.dot(n[...], wu_s[...], preferred_element_type=f32) + ub_row
        act, slope = gelu_pair(pre)
        act_ref[k * rows:(k + 1) * rows] = act.astype(bf16)
        pg = (contract(c, dw_ref[...], 1, 1) * slope).astype(bf16)
        pg_ref[k * rows:(k + 1) * rows] = pg
        back = contract(pg, wu_s[...], 1, 1)
        if k % 2:
            send_ref[(k // 2) * rows:(k // 2 + 1) * rows] = back.astype(bf16)
        else:
            (far_ref if k else keep_ref)[...] = back


def chunk_at(rank, me, count, p):
    top, next_bit = count // 2, count // 4
    turned = p
    if next_bit:
        turned = (p % next_bit) + jnp.where((p & top) != 0, next_bit, 0) + jnp.where((p & next_bit) != 0, top, 0)
    return me ^ jnp.where((rank & 1) == 0, p, turned)


def chunk_feed(rank, me, count, gd_s, gu_s, keep_ref, gsend_ref):
    down_rows, up_rows = gd_s.shape[0] // count, gu_s.shape[0] // count // 4
    part = gu_s.shape[0] // 4

    def store(target, start):
        def one(p, carry):
            nat = chunk_at(rank, me, count, p + start)
            target[p, 0:down_rows] = gd_s[at_rows(nat, down_rows)].astype(target.dtype)
            for k in range(4):
                at = pl.ds(pl.multiple_of((rank ^ k) * part + nat * up_rows, 8), up_rows)
                lo = down_rows + k * up_rows
                target[p, lo:lo + up_rows] = gu_s[at].astype(target.dtype)
            return carry

        lax.fori_loop(0, count // 2, one, 0)

    store(keep_ref, 0)
    store(gsend_ref, count // 2)


def feed_grad_body(count, rank_ref, n0, n1, n2, n3, c0, g1, g2, g3, act_ref, pg_ref,
                   upb_ref, gkeep_ref, gsend_ref, gd_s, gu_s):
    rank, me = rank_ref[0], rank_ref[1]
    rows, width = n0.shape
    part = width // 4
    up_b = jnp.zeros((1, pg_ref.shape[1]), f32)
    blocks = ((n0, c0[...]), (n1, g1[0:rows]), (n2, g2[0:rows]), (n3, g3[0:rows]))
    for k, (n, c) in enumerate(blocks):
        act = act_ref[k * rows:(k + 1) * rows]
        pg = pg_ref[k * rows:(k + 1) * rows]
        gd = contract(act, c, 0, 0)
        gu = contract(n[...], pg, 0, 0)
        gd_s[...] = gd if k == 0 else gd_s[...] + gd
        gu_s[...] = gu if k == 0 else gu_s[...] + gu
        up_b = up_b + jnp.sum(pg.astype(f32), 0, keepdims=True)
    upb_ref[0:1] = up_b
    if in_kernel(count, width):
        chunk_feed(rank, me, count, gd_s, gu_s, gkeep_ref, gsend_ref)
    else:
        gkeep_ref[...] = gd_s[...]
        gsend_ref[...] = gu_s[...]


def feed_out_body(dw_ref, act_ref, send_ref, keep_ref, far_ref):
    rows = keep_ref.shape[0]
    for k in range(4):
        out = jnp.dot(act_ref[k * rows:(k + 1) * rows], dw_ref[...], preferred_element_type=f32)
        if k % 2:
            send_ref[(k // 2) * rows:(k // 2 + 1) * rows] = out.astype(bf16)
        else:
            (far_ref if k else keep_ref)[...] = out


def in_kernel(count, width):
    return (width // 4 // count) % 24 == 0


def mid_back_body(mid_ref, par_ref, cot_ref, ids_ref, keep_ref, recv_ref, yrecv_ref,
                  grad_ref, branch_ref, small_ref):
    rows = mid_ref.shape[0]
    back = keep_ref[...] + recv_ref[0:rows].astype(f32) + yrecv_ref[...].astype(f32)
    unit, inverse = unit_of(mid_ref[...])
    cot = cot_ref[...].astype(f32)
    grad = cot + norm_back(back, unit, inverse, par_ref[8:9])
    grad_ref[...] = grad
    branch = grad.astype(bf16)
    branch_ref[...] = branch
    one = (lax.broadcasted_iota(jnp.int32, (8, rows), 0).astype(f32) == ids_ref[0:1]).astype(bf16)
    small_ref[0:8] = contract(one, branch, 1, 0)
    small_ref[8:9] = jnp.sum(back * unit, 0, keepdims=True)
    small_ref[9:10] = jnp.sum(back, 0, keepdims=True)
    small_ref[10:11] = jnp.sum(branch.astype(f32), 0, keepdims=True)
    small_ref[11:12] = jnp.sum(cot, 0, keepdims=True)


def heads_back(heads, segc_ref, segr_ref, qkv_ref, lse_ref, delta_ref, dctx_ref, dqkv_ref, dq_s):
    part = dctx_ref.shape[1]
    total_rows = qkv_ref.shape[0]
    rows = total_rows // 4
    for h in heads:
        q = qkv_ref[:, h * HD:(h + 1) * HD] * jnp.asarray(score_scale, bf16)
        key = qkv_ref[:, part + h * HD:part + (h + 1) * HD]
        val = qkv_ref[:, 2 * part + h * HD:2 * part + (h + 1) * HD]
        dctx = dctx_ref[:, h * HD:(h + 1) * HD]
        for j in range(total_rows // rows):
            lo = j * rows
            hi = lo + rows
            nq = total_rows - lo
            sc = contract(key[lo:hi], q[lo:], 1, 1)
            kpos = lax.broadcasted_iota(jnp.int32, (rows, nq), 0)
            qpos = lax.broadcasted_iota(jnp.int32, (rows, nq), 1)
            seen = (segc_ref[lo:hi] == segr_ref[:, lo:]) & (kpos <= qpos)
            prob = jnp.where(seen, jnp.exp(sc - lse_ref[h:h + 1, lo:]), 0.0)
            dv = jnp.dot(prob.astype(bf16), dctx[lo:], preferred_element_type=f32)
            dprob = contract(val[lo:hi], dctx[lo:], 1, 1)
            ds = (prob * (dprob - delta_ref[h:h + 1, lo:])).astype(bf16)
            dk = jnp.dot(ds, q[lo:], preferred_element_type=f32)
            dq = contract(ds, key[lo:hi], 0, 0)
            if j == 0:
                dq_s[...] = dq
            else:
                dq_s[lo:] += dq
            dqkv_ref[lo:hi, part + h * HD:part + (h + 1) * HD] = dk.astype(bf16)
            dqkv_ref[lo:hi, 2 * part + h * HD:2 * part + (h + 1) * HD] = dv.astype(bf16)
        dqkv_ref[:, h * HD:(h + 1) * HD] = (dq_s[...] * score_scale).astype(bf16)


def attn_back_one_body(heads, rank_ref, segc_ref, segr_ref, g0, g1, g2, g3, qkv_ref, ctx_ref, lse_ref, wout_ref,
                       dctx_ref, delta_ref, go_ref, dqkv_ref, del_s, dq_s):
    rank = rank_ref[0]
    rows, width = g0.shape
    part = width // 4
    go = jnp.zeros((part, width), f32)
    for k, g in enumerate((g0, g1, g2, g3)):
        at = at_rows(rank ^ k, rows)
        dctx_ref[at] = contract(g[...], wout_ref[...], 1, 1).astype(bf16)
        go = go + contract(ctx_ref[at], g[...], 0, 0)
    go_ref[...] = go
    prod = dctx_ref[...].astype(f32) * ctx_ref[...].astype(f32)
    for h in range(part // HD):
        del_s[:, h:h + 1] = jnp.sum(prod[:, h * HD:(h + 1) * HD], -1, keepdims=True)
    delta_ref[...] = del_s[...].T[0:8]
    heads_back(heads, segc_ref, segr_ref, qkv_ref, lse_ref, delta_ref, dctx_ref, dqkv_ref, dq_s)


def attn_back_two_body(count, heads, rank_ref, segc_ref, segr_ref, qkv_ref, lse_ref, delta_ref, dctx_ref, dqkv_in,
                       go_s, nrm_ref, unit_ref, inv_ref, ids_ref, par_ref, smid_ref, upb_ref, wq_ref,
                       send_ref, keep_ref, far_ref, gkeep_ref, gsend_ref, sm_ref, dqkv_s,
                       dq_s, gq_s, sm_s):
    dqkv_s[...] = dqkv_in[...]
    rank, me = rank_ref[0], rank_ref[1]
    rows, width = keep_ref.shape
    part = width // 4
    heads_back(heads, segc_ref, segr_ref, qkv_ref, lse_ref, delta_ref, dctx_ref, dqkv_s, dq_s)
    gain = par_ref[5:6]
    by_pass = smid_ref[0:8]
    gain_sum = jnp.zeros((1, width), f32)
    bias_sum = jnp.zeros((1, width), f32)
    for k in range(4):
        at = at_rows(rank ^ k, rows)
        back = contract(dqkv_s[at], wq_ref[...], 1, 1)
        if k % 2:
            send_ref[(k // 2) * rows:(k // 2 + 1) * rows] = back.astype(bf16)
        else:
            (far_ref if k else keep_ref)[...] = back
        unit = unit_ref[at].astype(f32)
        gain_sum = gain_sum + jnp.sum(back * unit, 0, keepdims=True)
        bias_sum = bias_sum + jnp.sum(back, 0, keepdims=True)
        one = (lax.broadcasted_iota(jnp.int32, (8, rows), 0).astype(f32) == ids_ref[k:k + 1]).astype(bf16)
        by_pass = by_pass + contract(one, norm_back(back, unit, inv_ref[at], gain).astype(bf16), 1, 0)
    gq_s[...] = contract(nrm_ref[...], dqkv_s[...], 0, 0)
    full = jnp.concatenate([by_pass[0:5], gain_sum, bias_sum, smid_ref[8:12],
                            jnp.zeros((5, width), f32)], 0)
    up_b = upb_ref[0:1]
    mine = lax.broadcasted_iota(jnp.int32, (16, part), 0)
    for j in range(4):
        sm = full[:, j * part:(j + 1) * part]
        for i in range(4):
            sm = jnp.where((mine == 11 + i) & (rank == j), up_b[:, i * part:(i + 1) * part], sm)
        sm_s[j] = sm
    if in_kernel(count, width):
        chunk_qkv(rank, me, count, gq_s, go_s, sm_s, gkeep_ref, gsend_ref)
        sm_ref[...] = jnp.zeros(sm_ref.shape, f32)
    else:
        gkeep_ref[...] = gq_s[...]
        gsend_ref[...] = go_s[...]
        for k in range(4):
            sm_ref[k] = sm_s[rank ^ k]


def chunk_qkv(rank, me, count, gq_s, go_s, sm_s, keep_ref, gsend_ref):
    part = go_s.shape[0]
    rows = part // count
    small = 16 // count
    wide = gq_s.shape[1]
    step = rows + small

    def store(target, p, nat, place):
        for k in range(4):
            at = pl.ds(pl.multiple_of((rank ^ k) * part + nat * rows, 8), rows)
            target[place, k * step:k * step + rows] = gq_s[at].astype(target.dtype)
        out = go_s[at_rows(nat, rows)]
        third = rows // 3
        target[place, 4 * step:4 * step + rows] = out[:, 0:wide].astype(target.dtype)
        tail = out[:, wide:]
        packed = jnp.concatenate([tail[i * third:(i + 1) * third] for i in range(3)], 1)
        target[place, 4 * step + rows:4 * step + rows + third] = packed.astype(target.dtype)

    for p in range(count):
        target, place = (keep_ref, p) if p < count // 2 else (gsend_ref, p - count // 2)
        nat = chunk_at(rank, me, count, p)
        store(target, p, nat, place)
        for k in range(4):
            sm = sm_s[rank ^ k]
            row = jnp.zeros((small, part), f32)
            for c in range(count):
                row = jnp.where(nat == c, sm[c * small:(c + 1) * small], row)
            target[place, k * step + rows:k * step + rows + small, 0:part] = row.astype(target.dtype)
            target[place, k * step + rows:k * step + rows + small, part:] = jnp.zeros(
                (small, wide - part), target.dtype)


def last_body(sin_ref, par_ref, grad_ref, keep_ref, recv_ref, yrecv_ref, tok_ref):
    rows = sin_ref.shape[0]
    back = keep_ref[...] + recv_ref[0:rows].astype(f32) + yrecv_ref[...].astype(f32)
    unit, inverse = unit_of(sin_ref[...])
    tok_ref[...] = (grad_ref[...] + norm_back(back, unit, inverse, par_ref[5:6])).astype(bf16)


def place_feed_body(rank_ref, g_ref, *refs):
    down_ref, up_ref = refs[-2:]
    rank = rank_ref[0]
    down_rows = down_ref.shape[0]
    up_rows, hidden = up_ref.shape[0], up_ref.shape[1] // 4
    down_ref[...] = g_ref[0, 0:down_rows].astype(f32)
    for k in range(4):
        lo = down_rows + k * up_rows
        up_ref[:, pl.ds(pl.multiple_of((rank ^ k) * hidden, hidden), hidden)] = g_ref[0, lo:lo + up_rows].astype(f32)


def place_qkv_body(count, start, rank_ref, g_ref, *refs):
    rank, me = rank_ref[0], rank_ref[1]
    if start:
        sm_in, _, _, qkv_ref, out_ref = refs[:5]
        small_refs, stage_s, sm_s = refs[5:-2], refs[-2], refs[-1]
    else:
        qkv_ref, out_ref, sm_s, stage_s = refs
    step = pl.program_id(0)
    rows, third = out_ref.shape[0], out_ref.shape[0] // 3
    width = out_ref.shape[1]
    part = width // 4
    wide = g_ref.shape[2]
    small = 16 // count
    if start:
        @pl.when(step == 0)
        def _():
            sm_s[...] = sm_in[...]
    stage_s[...] = g_ref[0, 0:4 * rows].astype(f32)
    for j in range(4):
        block = stage_s[at_rows(rank ^ j, rows)]
        for i in range(3):
            qkv_ref[:, i * width + j * part:i * width + (j + 1) * part] = block[:, i * part:(i + 1) * part]
    sm_s[chunk_at(rank, me, count, step + start)] = g_ref[0, 4 * rows:4 * rows + small, 0:part].astype(f32)
    lo = 4 * rows + small
    out_ref[:, 0:wide] = g_ref[0, lo:lo + rows].astype(f32)
    packed = g_ref[0, lo + rows:lo + rows + third].astype(f32)
    out_ref[:, wide:] = jnp.concatenate([packed[:, i * part:(i + 1) * part] for i in range(3)], 0)
    if start:
        @pl.when(step == pl.num_programs(0) - 1)
        def _():
            rows_of = [sm_s[i // small, i % small:i % small + 1] for i in range(16)]
            table_ref = small_refs[0]
            for i in range(table_ref.shape[0]):
                table_ref[i:i + 1] = rows_of[i]
            for ref, i in zip(small_refs[1:7], (5, 6, 9, 7, 8, 10)):
                ref[...] = rows_of[i].reshape(part)
            for i in range(4):
                small_refs[7][i * part:(i + 1) * part] = rows_of[11 + i].reshape(part)


def qkv_blocks_body(rank_ref, w_ref, own_ref, near_ref, far_ref, stage_s):
    rank = rank_ref[0]
    part = w_ref.shape[0]
    for t in range(4):
        stage_s[t] = jnp.concatenate(
            [w_ref[:, (4 * i + t) * part:(4 * i + t + 1) * part] for i in range(3)], 1)
    own_ref[...] = stage_s[rank]
    near_ref[...] = stage_s[rank ^ 1]
    far_ref[0:part] = stage_s[rank ^ 2]
    far_ref[part:] = stage_s[rank ^ 3]


def up_blocks_body(rank_ref, w_ref, cot_ref, own_ref, near_ref, far_ref):
    rank, side = rank_ref[0], rank_ref[2]
    rows = cot_ref.shape[0]
    hidden = own_ref.shape[1]

    def block(k):
        return w_ref[:, pl.ds(pl.multiple_of((rank ^ k) * hidden, hidden), hidden)]

    own_ref[...] = block(0)
    near_ref[0:rows] = cot_ref[...]
    near_ref[rows:] = block(1)
    far_ref[0:rows] = cot_ref[...]
    far_ref[rows:] = block(2 + side)


def by_core(value):
    return lax.ppermute(value, "shard", CORE)


def by_row(value):
    return lax.ppermute(value, "shard", ROWY)


def gather_rows(block):
    far = by_row(block)
    return block, by_core(block), far, by_core(far)


def scatter_sum(send, keep, far, rows):
    recv = by_core(send)
    onward = (far + recv[rows:].astype(f32)).astype(bf16)
    return keep, recv, by_row(onward), onward


def after(value, *others):
    return lax.optimization_barrier((value,) + others)[0]


def phases_of(count):
    return (count - 1).bit_length()


def order_of(count, core):
    order = list(range(phases_of(count)))
    if core and len(order) > 1:
        order[0], order[1] = order[1], order[0]
    return order


def plane_pairs(count, phase):
    pairs = []
    for r in range(count):
        for s in range(4):
            pairs.append((4 * r + s, 4 * (r ^ (1 << order_of(count, s % 2)[phase])) + s))
    return pairs


def chunk_index(count, replica):
    total = jnp.zeros((), jnp.int32)
    for position in order_of(count, 0):
        total = total * 2 + ((replica >> position) & 1)
    return total


def plane_swap(value, count, phase):
    return lax.ppermute(value, ("replica", "shard"), plane_pairs(count, phase))


def split_step(keep, got):
    half = keep.shape[0] // 2
    total = (keep.astype(f32) + got.astype(f32)).astype(bf16)
    return total[:half], total[half:]


def shards(replicas, tokens, pass_ids, seg_ids, cotangent, pass_table, norm1_gain, norm1_bias, qkv_weight, out_weight,
           out_bias, norm2_gain, norm2_bias, up_weight, up_bias, down_weight, down_bias):
    rows, width = tokens.shape
    part = width // 4
    seq = seg_ids.shape[0]
    hidden = up_bias.shape[0]
    phases = phases_of(replicas)
    packed = in_kernel(replicas, width)
    rank = lax.axis_index("shard").astype(jnp.int32)
    replica = lax.axis_index("replica").astype(jnp.int32)
    me = chunk_index(replicas, replica)
    place = jnp.stack([rank, me, replica & 1])
    smem = pl.BlockSpec(memory_space=pltpu.SMEM)
    vmem = pl.BlockSpec(memory_space=pltpu.VMEM)

    def call(body, micros, outs, scratch, *args, ranked=True, aliases=None, wide=False):
        specs = [smem] * ranked + [vmem] * (len(args) - ranked)
        return pl.pallas_call(
            body,
            out_shape=[jax.ShapeDtypeStruct(s, d) for s, d in outs],
            in_specs=specs,
            out_specs=[vmem] * len(outs),
            scratch_shapes=[pltpu.VMEM(s, d) for s, d in scratch],
            input_output_aliases=aliases or {},
            compiler_params=pltpu.CompilerParams(vmem_limit_bytes=None if wide else 24 * 2**20),
            cost_estimate=pl.CostEstimate(flops=int(micros * 1.1e9), bytes_accessed=0, transcendentals=0),
        )(*args)

    def placed(body, values, start, shapes, blocks_of, extra, scratch, aliases):
        def at_chunk(p, s):
            return (chunk_at(s[0], s[1], replicas, p + start), 0)

        def whole(shape):
            return pl.BlockSpec(shape, lambda p, s: (0,) * len(shape))

        return pl.pallas_call(
            body,
            out_shape=[jax.ShapeDtypeStruct(s, f32) for s in shapes],
            grid_spec=pltpu.PrefetchScalarGridSpec(
                num_scalar_prefetch=1, grid=(replicas // 2,),
                in_specs=[pl.BlockSpec((1,) + values.shape[1:], lambda p, s: (p, 0, 0))]
                + [whole(e.shape) if e.ndim == 3 else pl.BlockSpec(memory_space=pl.ANY) for e in extra],
                out_specs=[pl.BlockSpec(b, at_chunk) if b else whole(s) for s, b in zip(shapes, blocks_of)],
                scratch_shapes=[pltpu.VMEM(s, f32) for s in scratch]),
            input_output_aliases=aliases,
            compiler_params=pltpu.CompilerParams(vmem_limit_bytes=24 * 2**20),
            cost_estimate=pl.CostEstimate(flops=int(2.2e9), bytes_accessed=0, transcendentals=0),
        )(place, values, *extra)

    block, = call(pack_body, 1, [((rows + 16, width), bf16)], [], tokens, pass_ids, pass_table.T, norm1_gain, norm1_bias,
                  out_bias, norm2_gain, norm2_bias, down_bias, ranked=False, wide=True)
    x1, x2 = by_core(block), by_row(block)
    own_q, near_q, far_q = call(
        qkv_blocks_body, 0, [((part, 3 * part), bf16), ((part, 3 * part), bf16), ((2 * part, 3 * part), bf16)],
        [((4, part, 3 * part), bf16)], place, after(qkv_weight, block))
    far_q = by_row(far_q)
    own_u, near_u, far_u = call(
        up_blocks_body, 0,
        [((part, hidden), bf16), ((rows + part, width), bf16), ((rows + part, width), bf16)],
        [], place, up_weight, after(cotangent, own_q))
    x2 = after(x2, own_u)
    blocks = block, x1, x2, by_core(x2)
    sin, par, nrm, nrm_late, unit, inv, ids = call(
        norm_body, 0,
        [((rows, width), f32), ((16, width), f32), ((seq, width), bf16), ((seq, width), bf16), ((seq, width), bf16),
         ((seq, 1), f32), ((8, rows), f32)], [], place, *blocks)
    far_q = after(far_q, nrm)
    wq = own_q, by_core(near_q), far_q, by_core(far_q[part:])
    far_u = by_row(far_u)
    group = by_core(near_u), far_u, by_core(far_u)
    pair_u = lax.ppermute(far_u[rows:], ("replica", "shard"), [
        (4 * r + s, 4 * (r ^ 1) + (s ^ (r & 1))) for r in range(replicas) for s in range(4)])

    segc, segr = seg_ids[:, None], seg_ids[None, :]
    heads = part // HD
    half_f, half_b, row_f, row_b = ((2 * rows, width), f32), ((2 * rows, width), bf16), ((rows, width), f32), ((rows, width), bf16)
    send, keep, far, qkv, ctx, lse, wq_full = call(
        front_body, 4,
        [half_b, row_f, row_f, ((seq, 3 * part), bf16), ((seq, part), bf16), ((8, seq), f32), ((width, 3 * part), bf16)],
        [((seq, 128), f32), ((3 * heads, seq, HD), bf16), ((heads, seq, HD), bf16), ((heads, seq, 1), f32)],
        place, segc, segr, nrm, *wq, out_weight)
    parts = scatter_sum(after(send, far_u), keep, far, rows)
    mid, nrm2 = call(mid_body, 1, [row_f, row_b], [], sin, par, *parts[:2], after(parts[2], pair_u), ranked=False)
    n2 = gather_rows(nrm2)
    send, keep, far, act, pg = call(
        feed_body, 5, [half_b, row_f, row_f, ((seq, hidden), bf16), ((seq, hidden), bf16)],
        [((width, hidden), bf16)],
        place, *n2, cotangent, *group, own_u, pair_u, up_bias, down_weight)
    *back, onward = scatter_sum(send, keep, far, rows)
    feed_rows = hidden // replicas + 4 * (part // replicas)
    if packed:
        grads = [((replicas // 2, feed_rows, width), bf16)] * 2
    else:
        grads = [((hidden, width), f32), ((width, hidden), f32)]
    up_b, gkeep, gsend = call(
        functools.partial(feed_grad_body, replicas), 8, [((8, hidden), f32)] + grads,
        [((hidden, width), f32), ((width, hidden), f32)],
        place, *n2, cotangent, *group, after(act, onward), pg)
    if not packed:
        nat = chunk_at(rank, me, replicas, jnp.arange(replicas))
        downs = gkeep.reshape(replicas, -1, width)[nat]
        ups = gsend.reshape(4, replicas, -1, hidden)[rank ^ jnp.arange(4)][:, nat].transpose(1, 0, 2, 3)
        both = jnp.concatenate([downs, ups.reshape(replicas, -1, width)], 1)
        both = both.astype(bf16)
        gkeep, gsend = both[:replicas // 2], both[replicas // 2:]
    got = plane_swap(gsend, replicas, 0)
    mid_grad, branch, small_mid = call(
        mid_back_body, 6, [row_f, row_b, ((16, width), f32)], [], mid, par, after(cotangent, up_b), ids, *back, ranked=False)
    branches = gather_rows(branch)
    got = after(got, branches[1])
    for phase in range(1, max(phases - 1, 1)):
        gkeep, gsend = split_step(gkeep, got)
        got = plane_swap(gsend, replicas, phase)

    small = max(16, replicas)
    step = part // replicas + small // replicas
    qkv_rows = 4 * step + part // replicas + part // replicas // 3
    if packed:
        grads = [((replicas // 2, qkv_rows, 3 * part), bf16)] * 2
    else:
        grads = [((width, 3 * part), f32), ((part, width), f32)]
    first, rest = range(heads - 1), range(heads - 1, heads)
    dctx, delta, grad_out, dqkv = call(
        functools.partial(attn_back_one_body, first), 6,
        [((seq, part), bf16), ((8, seq), f32), ((part, width), f32), ((seq, 3 * part), bf16)],
        [((seq, 128), f32), ((seq, HD), f32)],
        place, segc, segr, *branches, qkv, ctx, lse, out_weight)
    if phases > 1:
        gkeep, gsend = split_step(gkeep, after(got, delta))
        got = plane_swap(gsend, replicas, phases - 1)
    send, keep, far, qkeep, qsend, smalls = call(
        functools.partial(attn_back_two_body, replicas, rest), 6,
        [half_b, row_f, row_f] + grads + [((4, 16, part), f32)],
        [((seq, 3 * part), bf16), ((seq, HD), f32), ((width, 3 * part), f32), ((4, 16, part), f32)],
        place, segc, segr, qkv, lse, after(delta, gsend), dctx, dqkv, grad_out, nrm_late, unit, inv, ids, par, small_mid, up_b,
        wq_full)
    if not packed:
        qs = qkeep.reshape(4, replicas, -1, 3 * part)[rank ^ jnp.arange(4)][:, nat].transpose(1, 0, 2, 3)
        sm = jnp.pad(smalls, ((0, 0), (0, small - 16), (0, 2 * part)))
        sm = sm.reshape(4, replicas, -1, 3 * part)[:, nat].transpose(1, 0, 2, 3)
        os = qsend.reshape(replicas, -1, width)[nat]
        both = jnp.concatenate([
            jnp.concatenate([qs, sm], 2).reshape(replicas, -1, 3 * part), os[:, :, :3 * part],
            os[:, :, 3 * part:].reshape(replicas, -1, 3 * part)], 1)
        both = both.astype(bf16)
        qkeep, qsend = both[:replicas // 2], both[replicas // 2:]
    qgot = plane_swap(qsend, replicas, 0)
    lo, ur = hidden // replicas, part // replicas

    last_phase = phases - 1
    now = {"turn": qkeep, "feed": got, "qkv": qgot}

    def swap_piece(at):
        return by_core(at(1)), by_row(at(2)), lax.ppermute(at(3), "shard", BOTH)

    def feed_swap():
        piece = (gkeep.astype(f32) + after(now["feed"], now["turn"]).astype(f32))[0].astype(bf16)
        now["swapped"] = swap_piece(lambda k: piece[lo + k * ur:lo + (k + 1) * ur])
        now["piece"], now["turn"] = piece, now["swapped"][0]

    def feed_first():
        now["feed_all"] = jnp.concatenate(
            [now["piece"][:lo + ur]] + [after(s, now["turn"]) for s in now["swapped"]], 0)[None]
        now["feed"] = plane_swap(now["feed_all"], replicas, last_phase)
        now["turn"] = now["feed_all"]

    def feed_join(phase):
        now["feed_all"] = jnp.concatenate([now["feed_all"], after(now["feed"], now["turn"])], 0)
        now["feed"] = plane_swap(now["feed_all"], replicas, phase)
        now["turn"] = now["feed_all"]

    def qkv_split(phase):
        now["qkeep"], qsend = split_step(now.get("qkeep", qkeep), after(now["qkv"], now["turn"]))
        now["qkv"] = plane_swap(qsend, replicas, phase)
        now["turn"] = qsend

    def qkv_swap():
        low = (now.get("qkeep", qkeep).astype(f32) + after(now["qkv"], now["turn"]).astype(f32))[0].astype(bf16)
        now["quads"] = swap_piece(lambda k: low[k * step:(k + 1) * step])
        now["low"], now["turn"] = low, now["quads"][0]

    def qkv_first():
        low = now["low"]
        quads = [low[:step]] + [after(s, now["turn"]) for s in now["quads"]]
        own_small = sum(q[ur:].astype(f32) for q in quads).astype(bf16)
        now["qkv_all"] = jnp.concatenate([q[:ur] for q in quads] + [own_small, low[4 * step:]], 0)[None]
        now["qkv"] = plane_swap(now["qkv_all"], replicas, last_phase)
        now["turn"] = now["qkv_all"]

    def qkv_join(phase):
        now["qkv_all"] = jnp.concatenate([now["qkv_all"], after(now["qkv"], now["turn"])], 0)
        now["qkv"] = plane_swap(now["qkv_all"], replicas, phase)
        now["turn"] = now["qkv_all"]

    recv = by_core(send)

    def tokens_onward():
        onward = (far + after(recv, now["turn"])[rows:].astype(f32)).astype(bf16)
        now["tokens"], now["turn"] = by_row(onward), onward

    def tokens_end():
        now["tokens_grad"], = call(last_body, 1, [row_b], [], sin, par, after(mid_grad, now["turn"]), keep, recv,
                                   now["tokens"], ranked=False)
        now["turn"] = now["tokens_grad"]

    def out_start():
        now["out"] = call(feed_out_body, 0, [half_b, row_f, row_f], [], down_weight, after(act, now["turn"]),
                          ranked=False)
        now["turn"] = now["out"][0]
        now["recv_o"] = by_core(now["out"][0])

    def out_onward():
        onward = (now["out"][2] + after(now["recv_o"], now["turn"])[rows:].astype(f32)).astype(bf16)
        now["far_o"], now["turn"] = by_row(onward), onward

    def out_end():
        now["output"] = (mid + now["out"][1] + now["recv_o"][:rows].astype(f32)
                         + after(now["far_o"], now["turn"]).astype(f32) + par[10:11]).astype(bf16)
        now["turn"] = now["output"]

    def feed_place():
        if packed:
            now["filled"] = placed(place_feed_body, after(now["feed_all"], now["turn"]), 0, *feed_shapes, [], [], {})
            now["turn"] = now["filled"][0]

    def qkv_place():
        if packed:
            now["qfilled"] = placed(
                functools.partial(place_qkv_body, replicas, 0), after(now["qkv_all"], now["turn"]), 0,
                qkv_shapes[0] + [sm_shape], qkv_shapes[1] + [None], [], [stage], {})
            now["turn"] = now["qfilled"][0]

    feed_shapes = [(hidden, width), (part, 4 * hidden)], [(lo, width), (ur, 4 * hidden)]
    qkv_shapes = [(part, 12 * part), (part, width)], [(ur, 12 * part), (ur, width)]
    stage, sm_shape = (4 * ur, 3 * part), (replicas, 16 // replicas, part)
    feed_joins = [functools.partial(feed_join, p) for p in reversed(range(last_phase))]
    qkv_joins = [functools.partial(qkv_join, p) for p in reversed(range(last_phase))]
    splits = [functools.partial(qkv_split, p) for p in range(1, phases)]
    for run in ([feed_swap, tokens_onward, out_start, feed_first] + splits[:1] + [tokens_end] + splits[1:]
                + feed_joins[:-1] + [qkv_swap, out_onward, qkv_first] + feed_joins[-1:] + [feed_place]
                + qkv_joins + [out_end, qkv_place]):
        run()
    tokens_grad, output, feed_all, got, qkv_all, qgot = (
        now[n] for n in ("tokens_grad", "output", "feed_all", "feed", "qkv_all", "qkv"))

    if packed:
        final_down, final_up = placed(
            place_feed_body, after(got, now["turn"]), replicas // 2, *feed_shapes, list(now["filled"]), [], {2: 0, 3: 1})
        filled = now["qfilled"]
        shapes, split = qkv_shapes
        vectors = [pass_table.T.shape] + [(part,)] * 6 + [(hidden,)]
        final_qkv, final_out, table, g1, b1, ob, g2, b2, db, ub = placed(
            functools.partial(place_qkv_body, replicas, replicas // 2), after(qgot, final_down), replicas // 2, shapes + vectors,
            split + [None] * 8, [filled[2], filled[0], filled[1]], [stage, sm_shape], {3: 0, 4: 1})
    else:
        back_at = jnp.argsort(nat)
        feed_all = jnp.concatenate([feed_all, got], 0)[back_at].astype(f32)
        qkv_all = jnp.concatenate([qkv_all, qgot], 0)[back_at].astype(f32)
        final_down = feed_all[:, :lo].reshape(hidden, width)
        final_up = feed_all[:, lo:].reshape(replicas, 4, ur, hidden)[:, rank ^ jnp.arange(4)]
        final_up = final_up.transpose(0, 2, 1, 3).reshape(part, 4 * hidden)
        final_qkv = qkv_all[:, :4 * ur].reshape(replicas, 4, ur, 3, part)[:, rank ^ jnp.arange(4)]
        final_qkv = final_qkv.transpose(0, 2, 3, 1, 4).reshape(part, 12 * part)
        hi = 4 * ur + small // replicas
        mine = qkv_all[:, 4 * ur:hi, :part].reshape(small, part)
        final_out = jnp.concatenate(
            [qkv_all[:, hi:hi + ur].reshape(part, 3 * part), qkv_all[:, hi + ur:].reshape(part, part)], 1)
        table, g1, b1, ob, g2, b2, db = mine[0:5], mine[5], mine[6], mine[9], mine[7], mine[8], mine[10]
        ub = mine[11:15].reshape(hidden)
    return (output, tokens_grad, table.T, g1, b1, final_qkv, final_out, ob, g2, b2, final_up, ub, final_down, db)


def solution(mesh):
    row = P(("replica", "shard"), None)
    flat = P(("replica", "shard"))
    w2, w1 = P("shard", None), P("shard")
    return jax.shard_map(
        functools.partial(shards, mesh.shape["replica"]),
        mesh=mesh,
        in_specs=(row, flat, P("replica"), row, w2, w1, w1, w2, w2, w1, w1, w1, w2, w1, w2, w1),
        out_specs=(row, row, w2, w1, w1, w2, w2, w1, w1, w1, w2, w1, w2, w1),
        check_vma=False,
    )
```

profile of v0, /device:TPU:0, one launch (start us, length us, event | category | flops | bytes accessed | tf_op | source)
XLA Modules:
  0.0 198.8 jit_solution(16191391754551525395)
XLA Ops:
  0.7 2.0 %shard_map.263.x0 = bf16[272,768]{1,0:T(8,128)(2,1)} custom-call(bf16[256,768]{1,0:T(8,128)(2,1)} %x_ref.1, s32[256]{0:T(256)} %ids_ref.1, bf16[5,192]{1,0:T(8,128)(2,1)} %bitcast.40, bf16[192]{0:T(256)(128)(2,1)} %g1_ref.1, bf16[192]{0:T(256)(128)(2,1)} %b1_ref.1, bf16[192]{0:T(256)(128)(2,1)} %ob_ref.1, bf16[192]{0:T(256)(128)(2,1)} %g2_ref.1, ...), custom_call_target="tpu_custom_call" | custom-call | flops 1100000000 | tf_op jit(solution)/shard_map/pallas_call | solution.py:553
  2.7 3.0 %collective-permute-start.1 = (bf16[272,768]{1,0:T(8,128)(2,1)}, bf16[272,768]{1,0:T(8,128)(2,1)S(1)}, u32[]{:S(2)}, u32[]{:S(2)}) collective-permute-start(bf16[272,768]{1,0:T(8,128)(2,1)} %shard_map.263.x0), channel_id=1, source_target_pairs={{0,2},{1,3},{2,0},{3,1},{4,6},{5,7},{6,4},{7,5},{8,10},{9,11},{10,... | collective-permute-start | bytes 1253384 | tf_op jit(solution)/shard_map/ppermute | solution.py:482
  11.3 5.0 %collective-permute-done.1.x2 = bf16[272,768]{1,0:T(8,128)(2,1)S(1)} collective-permute-done((bf16[272,768]{1,0:T(8,128)(2,1)}, bf16[272,768]{1,0:T(8,128)(2,1)S(1)}, u32[]{:S(2)}, u32[]{:S(2)}) %collective-permute-start.1) | collective-permute-done | bytes 417824 | tf_op jit(solution)/shard_map/ppermute | solution.py:482
  16.3 2.1 %collective-permute-start.6 = (bf16[448,768]{1,0:T(8,128)(2,1)}, bf16[448,768]{1,0:T(8,128)(2,1)S(1)}, u32[]{:S(2)}, u32[]{:S(2)}) collective-permute-start(bf16[448,768]{1,0:T(8,128)(2,1)} %get-tuple-element.123), channel_id=1, source_target_pairs={{0,2},{1,3},{2,0},{3,1},{4,6},{5,7},{6,4},{7,5},{8,10},{9,11},{10,... | collective-permute-start | bytes 2064392 | tf_op jit(solution)/shard_map/ppermute | solution.py:482
  18.6 2.1 %shard_map.266 = (f32[256,768]{1,0:T(8,128)S(1)}, f32[16,768]{1,0:T(8,128)S(1)}, bf16[1024,768]{1,0:T(8,128)(2,1)S(1)}, bf16[1024,768]{1,0:T(8,128)(2,1)S(1)}, b...) custom-call(s32[3]{0:T(128)S(1)} %pad_add_fusion.rank_ref, ...), custom_call_target="tpu_custom_call" | custom-call | tf_op jit(solution)/shard_map/pallas_call | solution.py:553
  24.9 1.9 collective-permute-done.4.w2
  30.7 10.3 %shard_map.267 = (bf16[512,768]{1,0:T(8,128)(2,1)S(1)}, f32[256,768]{1,0:T(8,128)S(1)}, f32[256,768]{1,0:T(8,128)S(1)}, bf16[1024,576]{1,0:T(8,128)(2,1)S(1)}, b...) custom-call(s32[3]{0:T(128)S(1)} %pad_add_fusion.rank_ref, ...), custom_call_target="tpu_custom_call" | custom-call | flops 4400000000 | tf_op jit(solution)/shard_map/pallas_call | solution.py:553
  41.3 2.1 %collective-permute-done.7.recv_ref = bf16[512,768]{1,0:T(8,128)(2,1)S(1)} collective-permute-done((bf16[512,768]{1,0:T(8,128)(2,1)S(1)}, bf16[512,768]{1,0:T(8,128)(2,1)S(1)}, u32[]{:S(2)}, u32[]{:S(2)}) %collective-permute-start.7) | collective-permute-done | bytes 786464 | tf_op jit(solution)/shard_map/ppermute | solution.py:478
  43.5 2.1 %collective-permute-start.8 = (bf16[256,768]{1,0:T(8,128)(2,1)S(1)}, bf16[256,768]{1,0:T(8,128)(2,1)S(1)}, u32[]{:S(2)}, u32[]{:S(2)}) collective-permute-start(bf16[256,768]{1,0:T(8,128)(2,1)S(1)} %add_convert_fusion.7), channel_id=1, source_target_pairs={{0,2},{1,3},{2,0},{3,1},{4,6},{5,7},{6,4},{7,5},{8,10},{9,11},{10,... | collective-permute-start | bytes 1179656 | tf_op jit(solution)/shard_map/ppermute | solution.py:482
  47.2 7.8 %collective-permute-done.9.pair_ref = bf16[192,768]{1,0:T(8,128)(2,1)S(1)} collective-permute-done((bf16[192,768]{1,0:T(8,128)(2,1)S(1)}, bf16[192,768]{1,0:T(8,128)(2,1)S(1)}, u32[]{:S(2)}, u32[]{:S(2)}) %collective-permute-start.9) | collective-permute-done | bytes 294944 | tf_op jit(solution)/shard_map/ppermute | solution.py:606
  57.8 8.9 %collective-permute-done.11.n2 = bf16[256,768]{1,0:T(8,128)(2,1)S(1)} collective-permute-done((bf16[256,768]{1,0:T(8,128)(2,1)S(1)}, bf16[256,768]{1,0:T(8,128)(2,1)S(1)}, u32[]{:S(2)}, u32[]{:S(2)}) %collective-permute-start.11) | collective-permute-done | bytes 393248 | tf_op jit(solution)/shard_map/ppermute | solution.py:482
  68.4 5.3 %shard_map.269 = (bf16[512,768]{1,0:T(8,128)(2,1)S(1)}, f32[256,768]{1,0:T(8,128)S(1)}, f32[256,768]{1,0:T(8,128)S(1)}, bf16[1024,768]{1,0:T(8,128)(2,1)S(1)}, bf16[1024,768]{1,0:T(8,128)(2,1)S(1)}) custom-call(s32[3]{0:T(128)S(1)} %pad_add_fusion.rank_ref, bf16[256,768]{1,0:T(8,128)(2,1)S(1)} %get-tuple-element.128.n0, ...), custom_call_target="tpu_custom_call" | custom-call | flops 5500000256 | tf_op jit(solution)/shard_map/pallas_call | solution.py:553
  74.0 2.2 %collective-permute-done.15.recv_ref = bf16[512,768]{1,0:T(8,128)(2,1)S(1)} collective-permute-done((bf16[512,768]{1,0:T(8,128)(2,1)S(1)}, bf16[512,768]{1,0:T(8,128)(2,1)S(1)}, u32[]{:S(2)}, u32[]{:S(2)}) %collective-permute-start.15) | collective-permute-done | bytes 786464 | tf_op jit(solution)/shard_map/ppermute | solution.py:478
  77.2 3.8 %shard_map.270 = (f32[8,768]{1,0:T(8,128)S(1)}, bf16[4,192,768]{2,1,0:T(8,128)(2,1)S(1)}, bf16[4,192,768]{2,1,0:T(8,128)(2,1)S(1)}) custom-call(s32[3]{0:T(128)S(1)} %pad_add_fusion.rank_ref, bf16[256,768]{1,0:T(8,128)(2,1)S(1)} %get-tuple-element.128.n0, bf16[256,768]{1,0:T(8,128)(2,1)S(1)} %collective-permute-done.10.n1, ...), custom_call_target="tpu_custom_call" | custom-call | flops 8800000000 | tf_op jit(solution)/shard_map/pallas_call | solution.py:553
  82.5 4.9 %collective-permute-done.16.yrecv_ref = bf16[256,768]{1,0:T(8,128)(2,1)S(1)} collective-permute-done((bf16[256,768]{1,0:T(8,128)(2,1)S(1)}, bf16[256,768]{1,0:T(8,128)(2,1)S(1)}, u32[]{:S(2)}, u32[]{:S(2)}) %collective-permute-start.16) | collective-permute-done | bytes 393248 | tf_op jit(solution)/shard_map/ppermute | solution.py:482
  89.3 9.4 %collective-permute-done.18.g2 = bf16[256,768]{1,0:T(8,128)(2,1)S(1)} collective-permute-done((bf16[256,768]{1,0:T(8,128)(2,1)S(1)}, bf16[256,768]{1,0:T(8,128)(2,1)S(1)}, u32[]{:S(2)}, u32[]{:S(2)}) %collective-permute-start.18) | collective-permute-done | bytes 393248 | tf_op jit(solution)/shard_map/ppermute | solution.py:482
  100.7 6.4 %shard_map.272 = (bf16[1024,192]{1,0:T(8,128)(2,1)S(1)}, f32[8,1024]{1,0:T(8,128)S(1)}, f32[192,768]{1,0:T(8,128)S(1)}, bf16[1024,576]{1,0:T(8,128)(2,1)S(1)}) custom-call(s32[3]{0:T(128)S(1)} %pad_add_fusion.rank_ref, s32[1024,1]{1,0:T(8,128)S(1)} %copy.37.segc_ref, s32[1,1024]{1,0:T(1,128)S(1)} %bitcast.35, bf16[256,768]{1,0:T(8,128)(2,1)S(1)} %get-tuple-element.141.g0, ...), custom_call_target="tpu_custom_call" | custom-call | flops 6600000000 | tf_op jit(solution)/shard_map/pallas_call | solution.py:553
  109.2 2.6 %collective-permute-start.23 = (bf16[1,192,768]{2,1,0:T(8,128)(2,1)S(1)}, bf16[1,192,768]{2,1,0:T(8,128)(2,1)S(1)}, u32[]{:S(2)}, u32[]{:S(2)}) collective-permute-start(bf16[1,192,768]{2,1,0:T(8,128)(2,1)S(1)} %slice.173), channel_id=1, source_target_pairs={{0,16},{1,17},{2,18},{3,19},{4,20},{5,21},{6,22},{7,23},{8,24},{9,... | collective-permute-start | bytes 884744 | tf_op jit(solution)/shard_map/ppermute | solution.py:527
  111.8 8.4 %shard_map.273 = (bf16[512,768]{1,0:T(8,128)(2,1)S(1)}, f32[256,768]{1,0:T(8,128)S(1)}, f32[256,768]{1,0:T(8,128)S(1)}, bf16[4,136,576]{2,1,0:T(8,128)(2,1)S(1)}...) custom-call(s32[3]{0:T(128)S(1)} %pad_add_fusion.rank_ref, s32[1024,1]{1,0:T(8,128)S(1)} %copy.37.segc_ref, ...), custom_call_target="tpu_custom_call" | custom-call | flops 6600000000 | tf_op jit(solution)/shard_map/pallas_call | solution.py:553
  121.1 4.0 %collective-permute-done.23 = bf16[1,192,768]{2,1,0:T(8,128)(2,1)S(1)} collective-permute-done((bf16[1,192,768]{2,1,0:T(8,128)(2,1)S(1)}, bf16[1,192,768]{2,1,0:T(8,128)(2,1)S(1)}, u32[]{:S(2)}, u32[]{:S(2)}) %collective-permute-start.23) | collective-permute-done | bytes 294944 | tf_op jit(solution)/shard_map/ppermute | solution.py:527
  133.0 2.1 %collective-permute-start.32 = (bf16[1,192,768]{2,1,0:T(8,128)(2,1)S(1)}, bf16[1,192,768]{2,1,0:T(8,128)(2,1)S(1)}, u32[]{:S(2)}, u32[]{:S(2)}) collective-permute-start(bf16[1,192,768]{2,1,0:T(8,128)(2,1)S(1)} %maximum_bitcast_fusion), channel_id=1, source_target_pairs={{0,16},{1,17},{2,18},{3,19},{4,20},{5,21},{6,22},{7,23},{8,24},{9,... | collective-permute-start | bytes 884744 | tf_op jit(solution)/shard_map/ppermute | solution.py:527
  135.2 3.6 %collective-permute-done.30.yrecv_ref = bf16[256,768]{1,0:T(8,128)(2,1)S(1)} collective-permute-done((bf16[256,768]{1,0:T(8,128)(2,1)S(1)}, bf16[256,768]{1,0:T(8,128)(2,1)S(1)}, u32[]{:S(2)}, u32[]{:S(2)}) %collective-permute-start.30) | collective-permute-done | bytes 393248 | tf_op jit(solution)/shard_map/ppermute | solution.py:482
  143.1 10.7 %collective-permute-done.32 = bf16[1,192,768]{2,1,0:T(8,128)(2,1)S(1)} collective-permute-done((bf16[1,192,768]{2,1,0:T(8,128)(2,1)S(1)}, bf16[1,192,768]{2,1,0:T(8,128)(2,1)S(1)}, u32[]{:S(2)}, u32[]{:S(2)}) %collective-permute-start.32) | collective-permute-done | bytes 294944 | tf_op jit(solution)/shard_map/ppermute | solution.py:527
  154.7 2.4 %collective-permute-done.31 = bf16[1,136,576]{2,1,0:T(8,128)(2,1)S(1)} collective-permute-done((bf16[1,136,576]{2,1,0:T(8,128)(2,1)S(1)}, bf16[1,136,576]{2,1,0:T(8,128)(2,1)S(1)}, u32[]{:S(2)}, u32[]{:S(2)}) %collective-permute-start.31) | collective-permute-done | bytes 156704 | tf_op jit(solution)/shard_map/ppermute | solution.py:527
  163.0 1.9 collective-permute-done.38
  167.1 2.5 %shard_map.276 = (f32[768,768]{1,0:T(8,128)}, f32[192,3072]{1,0:T(8,128)}) custom-call(s32[3]{0:T(128)S(1)} %pad_add_fusion.rank_ref, bf16[4,192,768]{2,1,0:T(8,128)(2,1)S(1)} %pad_maximum_fusion.g_ref), custom_call_target="tpu_custom_call" | custom-call | flops 2200000000 | tf_op jit(solution)/shard_map/pallas_call | solution.py:571
  169.6 3.6 %collective-permute-done.37 = bf16[1,130,576]{2,1,0:T(8,128)(2,1)S(1)} collective-permute-done((bf16[1,130,576]{2,1,0:T(8,128)(2,1)S(1)}, bf16[1,130,576]{2,1,0:T(8,128)(2,1)S(1)}, u32[]{:S(2)}, u32[]{:S(2)}) %collective-permute-start.37) | collective-permute-done | bytes 149792 | tf_op jit(solution)/shard_map/ppermute | solution.py:527
  174.6 9.8 %collective-permute-done.39 = bf16[2,130,576]{2,1,0:T(8,128)(2,1)S(1)} collective-permute-done((bf16[2,130,576]{2,1,0:T(8,128)(2,1)S(1)}, bf16[2,130,576]{2,1,0:T(8,128)(2,1)S(1)}, u32[]{:S(2)}, u32[]{:S(2)}) %collective-permute-start.39) | collective-permute-done | bytes 299552 | tf_op jit(solution)/shard_map/ppermute | solution.py:527
  187.3 2.4 %shard_map.277 = (f32[192,2304]{1,0:T(8,128)}, f32[192,768]{1,0:T(8,128)}, f32[8,2,192]{2,1,0:T(2,128)S(1)}) custom-call(s32[3]{0:T(128)S(1)} %pad_add_fusion.rank_ref, bf16[4,130,576]{2,1,0:T(8,128)(2,1)S(1)} %pad_maximum_fusion.1.g_ref), custom_call_target="tpu_custom_call" | custom-call | flops 2200000000 | tf_op jit(solution)/shard_map/pallas_call | solution.py:571
  189.7 2.5 %shard_map.278 = (f32[768,768]{1,0:T(8,128)}, f32[192,3072]{1,0:T(8,128)}) custom-call(s32[3]{0:T(128)S(1)} %pad_add_fusion.rank_ref, bf16[4,192,768]{2,1,0:T(8,128)(2,1)S(1)} %collective-permute-done.41.g_ref, f32[768,768]{1,0:T(8,128)} %get-tuple-element.183.refs_0_, ...), custom_call_target="tpu_custom_call", output_to_operand_aliasing={{0}: (2, {}), {1}: (3, {})} | custom-call | flops 2200000000 | tf_op jit(solution)/shard_map/pallas_call | solution.py:571
  192.2 3.7 %collective-permute-done.40 = bf16[4,130,576]{2,0,1:T(4,128)(2,1)S(1)} collective-permute-done((bf16[4,130,576]{2,0,1:T(4,128)(2,1)S(1)}, bf16[4,130,576]{2,0,1:T(4,128)(2,1)S(1)}, u32[]{:S(2)}, u32[]{:S(2)}) %collective-permute-start.40) | collective-permute-done | bytes 599072 | tf_op jit(solution)/shard_map/ppermute | solution.py:527
  196.0 2.6 %shard_map.279 = (f32[192,2304]{1,0:T(8,128)}, f32[192,768]{1,0:T(8,128)}, f32[5,192]{1,0:T(8,128)}, f32[192]{0:T(256)}, f32[192]{0:T(256)}, /*index=5*/f32[192]...) custom-call(s32[3]{0:T(128)S(1)} %pad_add_fusion.rank_ref, ...), custom_call_target="tpu_custom_call", output_to_operand_aliasing={{0}: (3, {}), {1}: (4, {})} | custom-call | flops 2200000000 | tf_op jit(solution)/shard_map/pallas_call | solution.py:571
  (156 shorter events, 55.5 us)
Async XLA Ops:
  2.7 13.6 %collective-permute-start.1 = (bf16[272,768]{1,0:T(8,128)(2,1)}, bf16[272,768]{1,0:T(8,128)(2,1)S(1)}, u32[]{:S(2)}, u32[]{:S(2)}) collective-permute-start(bf16[272,768]{1,0:T(8,128)(2,1)} %shard_map.263.x0), channel_id=1, source_target_pairs={{0,2},{1,3},{2,0},{3,1},{4,6},{5,7},{6,4},{7,5},{8,10},{9,11},{10,... | collective-permute-start | bytes 1253384 | tf_op jit(solution)/shard_map/ppermute | solution.py:482
  7.3 19.6 %collective-permute-start.4 = (bf16[384,576]{1,0:T(8,128)(2,1)S(1)}, bf16[384,576]{1,0:T(8,128)(2,1)S(1)}, u32[]{:S(2)}, u32[]{:S(2)}) collective-permute-start(bf16[384,576]{1,0:T(8,128)(2,1)S(1)} %get-tuple-element.119), channel_id=1, source_target_pairs={{0,2},{1,3},{2,0},{3,1},{4,6},{5,7},{6,4},{7,5},{8,10},{9,11},{10,... | collective-permute-start | bytes 1327112 | tf_op jit(solution)/shard_map/ppermute | solution.py:482
  7.3 11.4 %collective-permute-start = (bf16[272,768]{1,0:T(8,128)(2,1)}, bf16[272,768]{1,0:T(8,128)(2,1)S(1)}, u32[]{:S(2)}, u32[]{:S(2)}) collective-permute-start(bf16[272,768]{1,0:T(8,128)(2,1)} %shard_map.263.x0), channel_id=1, source_target_pairs={{0,1},{1,0},{2,3},{3,2},{4,5},{5,4},{6,7},{7,6},{8,9},{9,8},{10,11... | collective-permute-start | bytes 1253384 | tf_op jit(solution)/shard_map/ppermute | solution.py:478
  16.3 24.7 %collective-permute-start.6 = (bf16[448,768]{1,0:T(8,128)(2,1)}, bf16[448,768]{1,0:T(8,128)(2,1)S(1)}, u32[]{:S(2)}, u32[]{:S(2)}) collective-permute-start(bf16[448,768]{1,0:T(8,128)(2,1)} %get-tuple-element.123), channel_id=1, source_target_pairs={{0,2},{1,3},{2,0},{3,1},{4,6},{5,7},{6,4},{7,5},{8,10},{9,11},{10,... | collective-permute-start | bytes 2064392 | tf_op jit(solution)/shard_map/ppermute | solution.py:482
  18.4 9.4 %collective-permute-start.3 = (bf16[192,576]{1,0:T(8,128)(2,1)}, bf16[192,576]{1,0:T(8,128)(2,1)}, u32[]{:S(2)}, u32[]{:S(2)}) collective-permute-start(bf16[192,576]{1,0:T(8,128)(2,1)} %get-tuple-element.118), channel_id=1, source_target_pairs={{0,1},{1,0},{2,3},{3,2},{4,5},{5,4},{6,7},{7,6},{8,9},{9,8},{10,11... | collective-permute-start | bytes 663560 | tf_op jit(solution)/shard_map/ppermute | solution.py:478
  43.5 11.6 %collective-permute-start.8 = (bf16[256,768]{1,0:T(8,128)(2,1)S(1)}, bf16[256,768]{1,0:T(8,128)(2,1)S(1)}, u32[]{:S(2)}, u32[]{:S(2)}) collective-permute-start(bf16[256,768]{1,0:T(8,128)(2,1)S(1)} %add_convert_fusion.7), channel_id=1, source_target_pairs={{0,2},{1,3},{2,0},{3,1},{4,6},{5,7},{6,4},{7,5},{8,10},{9,11},{10,... | collective-permute-start | bytes 1179656 | tf_op jit(solution)/shard_map/ppermute | solution.py:482
  45.7 9.3 %collective-permute-start.9 = (bf16[192,768]{1,0:T(8,128)(2,1)S(1)}, bf16[192,768]{1,0:T(8,128)(2,1)S(1)}, u32[]{:S(2)}, u32[]{:S(2)}) collective-permute-start(bf16[192,768]{1,0:T(8,128)(2,1)S(1)} %slice.169), channel_id=1, source_target_pairs={{0,4},{1,5},{2,6},{3,7},{4,1},{5,0},{6,3},{7,2},{8,12},{9,13},{10,... | collective-permute-start | bytes 884744 | tf_op jit(solution)/shard_map/ppermute | solution.py:606
  55.5 11.2 %collective-permute-start.11 = (bf16[256,768]{1,0:T(8,128)(2,1)S(1)}, bf16[256,768]{1,0:T(8,128)(2,1)S(1)}, u32[]{:S(2)}, u32[]{:S(2)}) collective-permute-start(bf16[256,768]{1,0:T(8,128)(2,1)S(1)} %get-tuple-element.128.n0), channel_id=1, source_target_pairs={{0,2},{1,3},{2,0},{3,1},{4,6},{5,7},{6,4},{7,5},{8,10},{9,11},{10,... | collective-permute-start | bytes 1179656 | tf_op jit(solution)/shard_map/ppermute | solution.py:482
  57.3 9.4 %collective-permute-start.13 = (bf16[448,768]{1,0:T(8,128)(2,1)S(1)}, bf16[448,768]{1,0:T(8,128)(2,1)S(1)}, u32[]{:S(2)}, u32[]{:S(2)}) collective-permute-start(bf16[448,768]{1,0:T(8,128)(2,1)S(1)} %copy-done.16), channel_id=1, source_target_pairs={{0,1},{1,0},{2,3},{3,2},{4,5},{5,4},{6,7},{7,6},{8,9},{9,8},{10,11... | collective-permute-start | bytes 2064392 | tf_op jit(solution)/shard_map/ppermute | solution.py:478
  57.3 9.4 %collective-permute-start.14 = (bf16[448,768]{1,0:T(8,128)(2,1)S(1)}, bf16[448,768]{1,0:T(8,128)(2,1)S(1)}, u32[]{:S(2)}, u32[]{:S(2)}) collective-permute-start(bf16[448,768]{1,0:T(8,128)(2,1)S(1)} %collective-permute-done.6.g2), channel_id=1, source_target_pairs={{0,1},{1,0},{2,3},{3,2},{4,5},{5,4},{6,7},{7,6},{8,9},{9,8},{10,11... | collective-permute-start | bytes 2064392 | tf_op jit(solution)/shard_map/ppermute | solution.py:478
  57.8 8.9 %collective-permute-start.10 = (bf16[256,768]{1,0:T(8,128)(2,1)S(1)}, bf16[256,768]{1,0:T(8,128)(2,1)S(1)}, u32[]{:S(2)}, u32[]{:S(2)}) collective-permute-start(bf16[256,768]{1,0:T(8,128)(2,1)S(1)} %get-tuple-element.128.n0), channel_id=1, source_target_pairs={{0,1},{1,0},{2,3},{3,2},{4,5},{5,4},{6,7},{7,6},{8,9},{9,8},{10,11... | collective-permute-start | bytes 1179656 | tf_op jit(solution)/shard_map/ppermute | solution.py:478
  76.2 11.2 %collective-permute-start.16 = (bf16[256,768]{1,0:T(8,128)(2,1)S(1)}, bf16[256,768]{1,0:T(8,128)(2,1)S(1)}, u32[]{:S(2)}, u32[]{:S(2)}) collective-permute-start(bf16[256,768]{1,0:T(8,128)(2,1)S(1)} %add_convert_fusion.6), channel_id=1, source_target_pairs={{0,2},{1,3},{2,0},{3,1},{4,6},{5,7},{6,4},{7,5},{8,10},{9,11},{10,... | collective-permute-start | bytes 1179656 | tf_op jit(solution)/shard_map/ppermute | solution.py:482
  81.0 17.7 %collective-permute-start.20 = (bf16[4,192,768]{2,1,0:T(8,128)(2,1)S(1)}, bf16[4,192,768]{2,1,0:T(8,128)(2,1)S(1)}, u32[]{:S(2)}, u32[]{:S(2)}) collective-permute-start(bf16[4,192,768]{2,1,0:T(8,128)(2,1)S(1)} %get-tuple-element.145), channel_id=1, source_target_pairs={{0,4},{1,9},{2,6},{3,11},{4,0},{5,13},{6,2},{7,15},{8,12},{9,1},{1... | collective-permute-start | bytes 3538952 | tf_op jit(solution)/shard_map/ppermute | solution.py:527
  88.3 10.3 %collective-permute-start.18 = (bf16[256,768]{1,0:T(8,128)(2,1)S(1)}, bf16[256,768]{1,0:T(8,128)(2,1)S(1)}, u32[]{:S(2)}, u32[]{:S(2)}) collective-permute-start(bf16[256,768]{1,0:T(8,128)(2,1)S(1)} %get-tuple-element.141.g0), channel_id=1, source_target_pairs={{0,2},{1,3},{2,0},{3,1},{4,6},{5,7},{6,4},{7,5},{8,10},{9,11},{10,... | collective-permute-start | bytes 1179656 | tf_op jit(solution)/shard_map/ppermute | solution.py:482
  89.3 9.4 %collective-permute-start.17 = (bf16[256,768]{1,0:T(8,128)(2,1)S(1)}, bf16[256,768]{1,0:T(8,128)(2,1)S(1)}, u32[]{:S(2)}, u32[]{:S(2)}) collective-permute-start(bf16[256,768]{1,0:T(8,128)(2,1)S(1)} %get-tuple-element.141.g0), channel_id=1, source_target_pairs={{0,1},{1,0},{2,3},{3,2},{4,5},{5,4},{6,7},{7,6},{8,9},{9,8},{10,11... | collective-permute-start | bytes 1179656 | tf_op jit(solution)/shard_map/ppermute | solution.py:478
  99.0 9.9 %collective-permute-start.21 = (bf16[2,192,768]{2,1,0:T(8,128)(2,1)S(1)}, bf16[2,192,768]{2,1,0:T(8,128)(2,1)S(1)}, u32[]{:S(2)}, u32[]{:S(2)}) collective-permute-start(bf16[2,192,768]{2,1,0:T(8,128)(2,1)S(1)} %slice.172), channel_id=1, source_target_pairs={{0,8},{1,5},{2,10},{3,7},{4,12},{5,1},{6,14},{7,3},{8,0},{9,13},{1... | collective-permute-start | bytes 1769480 | tf_op jit(solution)/shard_map/ppermute | solution.py:527
  109.2 16.0 %collective-permute-start.23 = (bf16[1,192,768]{2,1,0:T(8,128)(2,1)S(1)}, bf16[1,192,768]{2,1,0:T(8,128)(2,1)S(1)}, u32[]{:S(2)}, u32[]{:S(2)}) collective-permute-start(bf16[1,192,768]{2,1,0:T(8,128)(2,1)S(1)} %slice.173), channel_id=1, source_target_pairs={{0,16},{1,17},{2,18},{3,19},{4,20},{5,21},{6,22},{7,23},{8,24},{9,... | collective-permute-start | bytes 884744 | tf_op jit(solution)/shard_map/ppermute | solution.py:527
  120.2 7.3 %collective-permute-start.22 = (bf16[512,768]{1,0:T(8,128)(2,1)S(1)}, bf16[512,768]{1,0:T(8,128)(2,1)S(1)}, u32[]{:S(2)}, u32[]{:S(2)}) collective-permute-start(bf16[512,768]{1,0:T(8,128)(2,1)S(1)} %get-tuple-element.158), channel_id=1, source_target_pairs={{0,1},{1,0},{2,3},{3,2},{4,5},{5,4},{6,7},{7,6},{8,9},{9,8},{10,11... | collective-permute-start | bytes 2359304 | tf_op jit(solution)/shard_map/ppermute | solution.py:478
  120.2 11.0 %collective-permute-start.26 = (bf16[4,136,576]{2,1,0:T(8,128)(2,1)S(1)}, bf16[4,136,576]{2,1,0:T(8,128)(2,1)S(1)}, u32[]{:S(2)}, u32[]{:S(2)}) collective-permute-start(bf16[4,136,576]{2,1,0:T(8,128)(2,1)S(1)} %get-tuple-element.166), channel_id=1, source_target_pairs={{0,4},{1,9},{2,6},{3,11},{4,0},{5,13},{6,2},{7,15},{8,12},{9,1},{1... | collective-permute-start | bytes 1880072 | tf_op jit(solution)/shard_map/ppermute | solution.py:527
  125.3 4.7 %collective-permute-start.28 = (bf16[24,768]{1,0:T(8,128)(2,1)S(1)}, bf16[24,768]{1,0:T(8,128)(2,1)S(1)}, u32[]{:S(2)}, u32[]{:S(2)}) collective-permute-start(bf16[24,768]{1,0:T(8,128)(2,1)S(1)} %get-tuple-element.207), channel_id=1, source_target_pairs={{0,3},{1,2},{2,1},{3,0},{4,7},{5,6},{6,5},{7,4},{8,11},{9,10},{10,... | collective-permute-start | bytes 110600 | tf_op jit(solution)/shard_map/ppermute | solution.py:689
  126.4 4.4 %collective-permute-start.27 = (bf16[24,768]{1,0:T(8,128)(2,1)S(1)}, bf16[24,768]{1,0:T(8,128)(2,1)S(1)}, u32[]{:S(2)}, u32[]{:S(2)}) collective-permute-start(bf16[24,768]{1,0:T(8,128)(2,1)S(1)} %get-tuple-element.206), channel_id=1, source_target_pairs={{0,2},{1,3},{2,0},{3,1},{4,6},{5,7},{6,4},{7,5},{8,10},{9,11},{10,... | collective-permute-start | bytes 110600 | tf_op jit(solution)/shard_map/ppermute | solution.py:482
  127.6 11.2 %collective-permute-start.30 = (bf16[256,768]{1,0:T(8,128)(2,1)S(1)}, bf16[256,768]{1,0:T(8,128)(2,1)S(1)}, u32[]{:S(2)}, u32[]{:S(2)}) collective-permute-start(bf16[256,768]{1,0:T(8,128)(2,1)S(1)} %add_convert_fusion.5), channel_id=1, source_target_pairs={{0,2},{1,3},{2,0},{3,1},{4,6},{5,7},{6,4},{7,5},{8,10},{9,11},{10,... | collective-permute-start | bytes 1179656 | tf_op jit(solution)/shard_map/ppermute | solution.py:482
  131.4 10.0 %collective-permute-start.29 = (bf16[2,136,576]{2,1,0:T(8,128)(2,1)S(1)}, bf16[2,136,576]{2,1,0:T(8,128)(2,1)S(1)}, u32[]{:S(2)}, u32[]{:S(2)}) collective-permute-start(bf16[2,136,576]{2,1,0:T(8,128)(2,1)S(1)} %slice.181), channel_id=1, source_target_pairs={{0,8},{1,5},{2,10},{3,7},{4,12},{5,1},{6,14},{7,3},{8,0},{9,13},{1... | collective-permute-start | bytes 940040 | tf_op jit(solution)/shard_map/ppermute | solution.py:527
  133.0 20.8 %collective-permute-start.32 = (bf16[1,192,768]{2,1,0:T(8,128)(2,1)S(1)}, bf16[1,192,768]{2,1,0:T(8,128)(2,1)S(1)}, u32[]{:S(2)}, u32[]{:S(2)}) collective-permute-start(bf16[1,192,768]{2,1,0:T(8,128)(2,1)S(1)} %maximum_bitcast_fusion), channel_id=1, source_target_pairs={{0,16},{1,17},{2,18},{3,19},{4,20},{5,21},{6,22},{7,23},{8,24},{9,... | collective-permute-start | bytes 884744 | tf_op jit(solution)/shard_map/ppermute | solution.py:527
  141.5 15.6 %collective-permute-start.31 = (bf16[1,136,576]{2,1,0:T(8,128)(2,1)S(1)}, bf16[1,136,576]{2,1,0:T(8,128)(2,1)S(1)}, u32[]{:S(2)}, u32[]{:S(2)}) collective-permute-start(bf16[1,136,576]{2,1,0:T(8,128)(2,1)S(1)} %slice.183), channel_id=1, source_target_pairs={{0,16},{1,17},{2,18},{3,19},{4,20},{5,21},{6,22},{7,23},{8,24},{9,... | collective-permute-start | bytes 470024 | tf_op jit(solution)/shard_map/ppermute | solution.py:527
  143.1 16.1 %collective-permute-start.25 = (bf16[512,768]{1,0:T(8,128)(2,1)S(1)}, bf16[512,768]{1,0:T(8,128)(2,1)S(1)}, u32[]{:S(2)}, u32[]{:S(2)}) collective-permute-start(bf16[512,768]{1,0:T(8,128)(2,1)S(1)} %get-tuple-element.164), channel_id=1, source_target_pairs={{0,1},{1,0},{2,3},{3,2},{4,5},{5,4},{6,7},{7,6},{8,9},{9,8},{10,11... | collective-permute-start | bytes 2359304 | tf_op jit(solution)/shard_map/ppermute | solution.py:478
  154.7 10.2 %collective-permute-start.38 = (bf16[2,192,768]{2,1,0:T(8,128)(2,1)}, bf16[2,192,768]{2,1,0:T(8,128)(2,1)}, u32[]{:S(2)}, u32[]{:S(2)}) collective-permute-start(bf16[2,192,768]{2,1,0:T(8,128)(2,1)} %pad_maximum_fusion.2), channel_id=1, source_target_pairs={{0,8},{1,5},{2,10},{3,7},{4,12},{5,1},{6,14},{7,3},{8,0},{9,13},{1... | collective-permute-start | bytes 1769480 | tf_op jit(solution)/shard_map/ppermute | solution.py:527
  162.9 10.3 %collective-permute-start.37 = (bf16[1,130,576]{2,1,0:T(8,128)(2,1)S(1)}, bf16[1,130,576]{2,1,0:T(8,128)(2,1)S(1)}, u32[]{:S(2)}, u32[]{:S(2)}) collective-permute-start(bf16[1,130,576]{2,1,0:T(8,128)(2,1)S(1)} %bitcast.37), channel_id=1, source_target_pairs={{0,16},{1,17},{2,18},{3,19},{4,20},{5,21},{6,22},{7,23},{8,24},{9,... | collective-permute-start | bytes 449288 | tf_op jit(solution)/shard_map/ppermute | solution.py:527
  166.1 23.7 %collective-permute-start.41 = (bf16[4,192,768]{2,1,0:T(8,128)(2,1)S(1)}, bf16[4,192,768]{2,1,0:T(8,128)(2,1)S(1)}, u32[]{:S(2)}, u32[]{:S(2)}) collective-permute-start(bf16[4,192,768]{2,1,0:T(8,128)(2,1)S(1)} %pad_maximum_fusion.g_ref), channel_id=1, source_target_pairs={{0,4},{1,9},{2,6},{3,11},{4,0},{5,13},{6,2},{7,15},{8,12},{9,1},{1... | collective-permute-start | bytes 3538952 | tf_op jit(solution)/shard_map/ppermute | solution.py:527
  173.2 11.2 %collective-permute-start.39 = (bf16[2,130,576]{2,1,0:T(8,128)(2,1)S(1)}, bf16[2,130,576]{2,1,0:T(8,128)(2,1)S(1)}, u32[]{:S(2)}, u32[]{:S(2)}) collective-permute-start(bf16[2,130,576]{2,1,0:T(8,128)(2,1)S(1)} %pad_maximum_fusion.3), channel_id=1, source_target_pairs={{0,8},{1,5},{2,10},{3,7},{4,12},{5,1},{6,14},{7,3},{8,0},{9,13},{1... | collective-permute-start | bytes 898568 | tf_op jit(solution)/shard_map/ppermute | solution.py:527
  173.3 11.9 %collective-permute-start.34 = (bf16[256,768]{1,0:T(8,128)(2,1)S(1)}, bf16[256,768]{1,0:T(8,128)(2,1)S(1)}, u32[]{:S(2)}, u32[]{:S(2)}) collective-permute-start(bf16[256,768]{1,0:T(8,128)(2,1)S(1)} %copy-done.24), channel_id=1, source_target_pairs={{0,2},{1,3},{2,0},{3,1},{4,6},{5,7},{6,4},{7,5},{8,10},{9,11},{10,... | collective-permute-start | bytes 1179656 | tf_op jit(solution)/shard_map/ppermute | solution.py:482
  185.2 10.7 %collective-permute-start.40 = (bf16[4,130,576]{2,0,1:T(4,128)(2,1)S(1)}, bf16[4,130,576]{2,0,1:T(4,128)(2,1)S(1)}, u32[]{:S(2)}, u32[]{:S(2)}) collective-permute-start(bf16[4,130,576]{2,0,1:T(4,128)(2,1)S(1)} %copy.40), channel_id=1, source_target_pairs={{0,4},{1,9},{2,6},{3,11},{4,0},{5,13},{6,2},{7,15},{8,12},{9,1},{1... | collective-permute-start | bytes 1797128 | tf_op jit(solution)/shard_map/ppermute | solution.py:527
  (35 other events, 184.1 us)
where the time goes:
time: 199 us
  waiting for transfers between devices  92.3 us (46%)
  Pallas kernels  55.4 us (28%)
  starting transfers between devices  34.6 us (17%)
  local copies, waits for them, and re-layouts  10.1 us (5%)
  other arithmetic  5.14 us (3%)
    pallas_call x13, Pallas kernels, call(): pl.pallas_call(body, out_shape=[jax.ShapeDtypeStruct(s, d) for s, d in ou...  45.3 us
    ppermute x12, waiting for transfers between devices, plane_swap(): return lax.ppermute(value, ('replica', 'shard'), plane_pairs(count, phase))  39.6 us
    ppermute x11, waiting for transfers between devices, by_row(): return lax.ppermute(value, 'shard', ROWY)  36.2 us
    ppermute x11, starting transfers between devices, by_row(): return lax.ppermute(value, 'shard', ROWY)  15.9 us
    ppermute x12, starting transfers between devices, plane_swap(): return lax.ppermute(value, ('replica', 'shard'), plane_pairs(count, phase))  14.4 us
    pallas_call x4, Pallas kernels, placed(): pl.pallas_call(body, out_shape=[jax.ShapeDtypeStruct(s, f32) for s in sha...  10 us
    unnamed x50, local copies, waits for them, and re-layouts  8.25 us
    ppermute x1, waiting for transfers between devices, shards(): lax.ppermute(far_u[rows:], ('replica', 'shard'), [(4 * r + s, 4 * (r ^ 1)...  7.78 us
  transfers between devices with their start and end apart: 42, of which 26 were waited for; matrix products, arithmetic and copies ran while one was open for 3% of the time, Pallas kernels for 23%

commit v1 on v0

--- a/solution.py
+++ b/solution.py
@@ -54,11 +54,14 @@
     out_ref[rows + 11:rows + 12, 0:rows] = ids_ref[...].astype(f32).reshape(1, rows).astype(bf16)
 
 
-def norm_body(rank_ref, x0, x1, x2, x3,
-              sin_ref, par_ref, nrm_ref, late_ref, unit_ref, inv_ref, ids_ref):
+def norm_body(rank_ref, seg_ref, x0, x1, x2, x3,
+              segc_ref, segr_ref, sin_ref, par_ref, nrm_ref, late_ref, unit_ref, inv_ref, ids_ref):
     rank = rank_ref[0]
     rows, width = sin_ref.shape
     part = width // 4
+    seg = seg_ref[...].astype(f32).reshape(1, seg_ref.shape[0])
+    segr_ref[...] = jnp.broadcast_to(seg, segr_ref.shape)
+    segc_ref[...] = jnp.broadcast_to(seg, (128, seg.shape[1])).T[:, 0:1]
     ext = [b[rows:rows + 16, 0:part].astype(f32) for b in (x0, x1, x2, x3)]
     cols = []
     for j in range(4):
@@ -107,7 +110,7 @@
             sc = contract(q[lo:nk], key[:nk], 1, 1)
             qpos = lo + lax.broadcasted_iota(jnp.int32, (rows, nk), 0)
             kpos = lax.broadcasted_iota(jnp.int32, (rows, nk), 1)
-            seen = (segc_ref[lo:nk] == segr_ref[:, :nk]) & (kpos <= qpos)
+            seen = (segc_ref[lo:nk] == segr_ref[0:1, :nk]) & (kpos <= qpos)
             sc = jnp.where(seen, sc, masked_score)
             top = jnp.max(sc, -1, keepdims=True)
             e = jnp.exp(sc - top)
@@ -129,9 +132,9 @@
         ref[...] = jnp.dot(ctx_ref[at_rows(rank ^ k, rows)], wout_ref[...], preferred_element_type=f32)
 
 
-def mid_body(sin_ref, par_ref, keep_ref, recv_ref, yrecv_ref, mid_ref, nrm_ref):
-    rows = sin_ref.shape[0]
-    mid = (sin_ref[...] + keep_ref[...] + recv_ref[0:rows].astype(f32)
+def mid_body(start, sin_ref, par_ref, keep_ref, recv_ref, yrecv_ref, mid_ref, nrm_ref):
+    at = slice(start, start + yrecv_ref.shape[0])
+    mid = (sin_ref[at] + keep_ref[at] + recv_ref[at].astype(f32)
            + yrecv_ref[...].astype(f32) + par_ref[7:8])
     mid_ref[...] = mid
     unit, _ = unit_of(mid)
@@ -146,10 +149,14 @@
     return v * half, half + 0.5 * v * (1.0 - t * t) * (c0 * (1.0 + 3.0 * c1 * sq))
 
 
-def feed_body(rank_ref, n0, n1, n2, n3, c0, g1, g2, g3, u0, pair_ref, ub_ref, dw_ref,
+def whole_block(halves):
+    return jnp.concatenate([half[...] for half in halves], 0)
+
+
+def feed_body(rank_ref, n0, m0, n1, m1, n2, m2, n3, m3, c0, g1, g2, g3, u0, pair_ref, ub_ref, dw_ref,
               send_ref, keep_ref, far_ref, act_ref, pg_ref, wu_s):
     rank = rank_ref[0]
-    rows, width = n0.shape
+    rows, width = c0.shape
     part = width // 4
     ub_row = ub_ref[...].astype(f32).reshape(1, ub_ref.shape[0])
     side = rank_ref[2]
@@ -166,8 +173,9 @@
         wu_s[at_rows(rank ^ 2, part)] = pair_ref[...]
         wu_s[at_rows(rank ^ 3, part)] = g3[rows:]
 
-    for k, (n, c) in enumerate(((n0, c0[...]), (n1, g1[0:rows]), (n2, g2[0:rows]), (n3, g3[0:rows]))):
-        pre = jnp.dot(n[...], wu_s[...], preferred_element_type=f32) + ub_row
+    for k, (n, c) in enumerate((
+            ((n0, m0), c0[...]), ((n1, m1), g1[0:rows]), ((n2, m2), g2[0:rows]), ((n3, m3), g3[0:rows]))):
+        pre = jnp.dot(whole_block(n), wu_s[...], preferred_element_type=f32) + ub_row
         act, slope = gelu_pair(pre)
         act_ref[k * rows:(k + 1) * rows] = act.astype(bf16)
         pg = (contract(c, dw_ref[...], 1, 1) * slope).astype(bf16)
@@ -207,18 +215,19 @@
     store(gsend_ref, count // 2)
 
 
-def feed_grad_body(count, rank_ref, n0, n1, n2, n3, c0, g1, g2, g3, act_ref, pg_ref,
+def feed_grad_body(count, rank_ref, n0, m0, n1, m1, n2, m2, n3, m3, c0, g1, g2, g3, act_ref, pg_ref,
                    upb_ref, gkeep_ref, gsend_ref, gd_s, gu_s):
     rank, me = rank_ref[0], rank_ref[1]
-    rows, width = n0.shape
+    rows, width = c0.shape
     part = width // 4
     up_b = jnp.zeros((1, pg_ref.shape[1]), f32)
-    blocks = ((n0, c0[...]), (n1, g1[0:rows]), (n2, g2[0:rows]), (n3, g3[0:rows]))
+    blocks = (
+        ((n0, m0), c0[...]), ((n1, m1), g1[0:rows]), ((n2, m2), g2[0:rows]), ((n3, m3), g3[0:rows]))
     for k, (n, c) in enumerate(blocks):
         act = act_ref[k * rows:(k + 1) * rows]
         pg = pg_ref[k * rows:(k + 1) * rows]
         gd = contract(act, c, 0, 0)
-        gu = contract(n[...], pg, 0, 0)
+        gu = contract(whole_block(n), pg, 0, 0)
         gd_s[...] = gd if k == 0 else gd_s[...] + gd
         gu_s[...] = gu if k == 0 else gu_s[...] + gu
         up_b = up_b + jnp.sum(pg.astype(f32), 0, keepdims=True)
@@ -230,8 +239,9 @@
         gsend_ref[...] = gu_s[...]
 
 
-def feed_out_body(dw_ref, act_ref, send_ref, keep_ref, far_ref):
+def feed_out_body(rank_ref, dw_ref, act_ref, send_ref, keep_ref, far_ref):
     rows = keep_ref.shape[0]
+    del rank_ref
     for k in range(4):
         out = jnp.dot(act_ref[k * rows:(k + 1) * rows], dw_ref[...], preferred_element_type=f32)
         if k % 2:
@@ -244,17 +254,18 @@
     return (width // 4 // count) % 24 == 0
 
 
-def mid_back_body(mid_ref, par_ref, cot_ref, ids_ref, keep_ref, recv_ref, yrecv_ref,
+def mid_back_body(start, mid_ref, par_ref, cot_ref, ids_ref, keep_ref, recv_ref, yrecv_ref,
                   grad_ref, branch_ref, small_ref):
     rows = mid_ref.shape[0]
-    back = keep_ref[...] + recv_ref[0:rows].astype(f32) + yrecv_ref[...].astype(f32)
+    at = slice(start, start + rows)
+    back = keep_ref[at] + recv_ref[at].astype(f32) + yrecv_ref[...].astype(f32)
     unit, inverse = unit_of(mid_ref[...])
-    cot = cot_ref[...].astype(f32)
+    cot = cot_ref[at].astype(f32)
     grad = cot + norm_back(back, unit, inverse, par_ref[8:9])
     grad_ref[...] = grad
     branch = grad.astype(bf16)
     branch_ref[...] = branch
-    one = (lax.broadcasted_iota(jnp.int32, (8, rows), 0).astype(f32) == ids_ref[0:1]).astype(bf16)
+    one = (lax.broadcasted_iota(jnp.int32, (8, rows), 0).astype(f32) == ids_ref[0:1, at]).astype(bf16)
     small_ref[0:8] = contract(one, branch, 1, 0)
     small_ref[8:9] = jnp.sum(back * unit, 0, keepdims=True)
     small_ref[9:10] = jnp.sum(back, 0, keepdims=True)
@@ -278,7 +289,7 @@
             sc = contract(key[lo:hi], q[lo:], 1, 1)
             kpos = lax.broadcasted_iota(jnp.int32, (rows, nq), 0)
             qpos = lax.broadcasted_iota(jnp.int32, (rows, nq), 1)
-            seen = (segc_ref[lo:hi] == segr_ref[:, lo:]) & (kpos <= qpos)
+            seen = (segc_ref[lo:hi] == segr_ref[0:1, lo:]) & (kpos <= qpos)
             prob = jnp.where(seen, jnp.exp(sc - lse_ref[h:h + 1, lo:]), 0.0)
             dv = jnp.dot(prob.astype(bf16), dctx[lo:], preferred_element_type=f32)
             dprob = contract(val[lo:hi], dctx[lo:], 1, 1)
@@ -294,16 +305,17 @@
         dqkv_ref[:, h * HD:(h + 1) * HD] = (dq_s[...] * score_scale).astype(bf16)
 
 
-def attn_back_one_body(heads, rank_ref, segc_ref, segr_ref, g0, g1, g2, g3, qkv_ref, ctx_ref, lse_ref, wout_ref,
+def attn_back_one_body(heads, rank_ref, segc_ref, segr_ref, g0, f0, g1, f1, g2, f2, g3, f3, qkv_ref, ctx_ref, lse_ref, wout_ref,
                        dctx_ref, delta_ref, go_ref, dqkv_ref, del_s, dq_s):
     rank = rank_ref[0]
-    rows, width = g0.shape
+    rows, width = 2 * g0.shape[0], g0.shape[1]
     part = width // 4
     go = jnp.zeros((part, width), f32)
-    for k, g in enumerate((g0, g1, g2, g3)):
+    for k, halves in enumerate(((g0, f0), (g1, f1), (g2, f2), (g3, f3))):
         at = at_rows(rank ^ k, rows)
-        dctx_ref[at] = contract(g[...], wout_ref[...], 1, 1).astype(bf16)
-        go = go + contract(ctx_ref[at], g[...], 0, 0)
+        g = whole_block(halves)
+        dctx_ref[at] = contract(g, wout_ref[...], 1, 1).astype(bf16)
+        go = go + contract(ctx_ref[at], g, 0, 0)
     go_ref[...] = go
     prod = dctx_ref[...].astype(f32) * ctx_ref[...].astype(f32)
     for h in range(part // HD):
@@ -312,17 +324,14 @@
     heads_back(heads, segc_ref, segr_ref, qkv_ref, lse_ref, delta_ref, dctx_ref, dqkv_ref, dq_s)
 
 
-def attn_back_two_body(count, heads, rank_ref, segc_ref, segr_ref, qkv_ref, lse_ref, delta_ref, dctx_ref, dqkv_in,
-                       go_s, nrm_ref, unit_ref, inv_ref, ids_ref, par_ref, smid_ref, upb_ref, wq_ref,
-                       send_ref, keep_ref, far_ref, gkeep_ref, gsend_ref, sm_ref, dqkv_s,
-                       dq_s, gq_s, sm_s):
-    dqkv_s[...] = dqkv_in[...]
+def attn_back_two_body(count, rank_ref, dqkv_s, go_s, nrm_ref, unit_ref, inv_ref, ids_ref, par_ref, smid_ref, smid2_ref, upb_ref, wq_ref,
+                       send_ref, keep_ref, far_ref, gkeep_ref, gsend_ref, sm_ref, gq_s, sm_s):
     rank, me = rank_ref[0], rank_ref[1]
     rows, width = keep_ref.shape
     part = width // 4
-    heads_back(heads, segc_ref, segr_ref, qkv_ref, lse_ref, delta_ref, dctx_ref, dqkv_s, dq_s)
     gain = par_ref[5:6]
-    by_pass = smid_ref[0:8]
+    smid = smid_ref[...] + smid2_ref[...]
+    by_pass = smid[0:8]
     gain_sum = jnp.zeros((1, width), f32)
     bias_sum = jnp.zeros((1, width), f32)
     for k in range(4):
@@ -338,7 +347,7 @@
         one = (lax.broadcasted_iota(jnp.int32, (8, rows), 0).astype(f32) == ids_ref[k:k + 1]).astype(bf16)
         by_pass = by_pass + contract(one, norm_back(back, unit, inv_ref[at], gain).astype(bf16), 1, 0)
     gq_s[...] = contract(nrm_ref[...], dqkv_s[...], 0, 0)
-    full = jnp.concatenate([by_pass[0:5], gain_sum, bias_sum, smid_ref[8:12],
+    full = jnp.concatenate([by_pass[0:5], gain_sum, bias_sum, smid[8:12],
                             jnp.zeros((5, width), f32)], 0)
     up_b = upb_ref[0:1]
     mine = lax.broadcasted_iota(jnp.int32, (16, part), 0)
@@ -389,11 +398,11 @@
                 (small, wide - part), target.dtype)
 
 
-def last_body(sin_ref, par_ref, grad_ref, keep_ref, recv_ref, yrecv_ref, tok_ref):
+def last_body(sin_ref, par_ref, grad_a, grad_b, keep_ref, recv_ref, yrecv_ref, tok_ref):
     rows = sin_ref.shape[0]
     back = keep_ref[...] + recv_ref[0:rows].astype(f32) + yrecv_ref[...].astype(f32)
     unit, inverse = unit_of(sin_ref[...])
-    tok_ref[...] = (grad_ref[...] + norm_back(back, unit, inverse, par_ref[5:6])).astype(bf16)
+    tok_ref[...] = (whole_block((grad_a, grad_b)) + norm_back(back, unit, inverse, par_ref[5:6])).astype(bf16)
 
 
 def place_feed_body(rank_ref, g_ref, *refs):
@@ -447,6 +456,19 @@
                 small_refs[7][i * part:(i + 1) * part] = rows_of[11 + i].reshape(part)
 
 
+def join_qkv_body(low_ref, b1, b2, b3, out_ref):
+    step = b1.shape[0]
+    small = (low_ref.shape[0] - out_ref.shape[0]) // 3
+    rows = step - small
+    total = low_ref[rows:step].astype(f32)
+    out_ref[0:rows] = low_ref[0:rows]
+    for k, b in enumerate((b1, b2, b3)):
+        out_ref[(k + 1) * rows:(k + 2) * rows] = b[0:rows]
+        total = total + b[rows:step].astype(f32)
+    out_ref[4 * rows:4 * rows + small] = total.astype(bf16)
+    out_ref[4 * rows + small:] = low_ref[4 * step:]
+
+
 def qkv_blocks_body(rank_ref, w_ref, own_ref, near_ref, far_ref, stage_s):
     rank = rank_ref[0]
     part = w_ref.shape[0]
@@ -489,8 +511,14 @@
 
 def scatter_sum(send, keep, far, rows):
     recv = by_core(send)
-    onward = (far + recv[rows:].astype(f32)).astype(bf16)
-    return keep, recv, by_row(onward), onward
+    half = rows // 2
+    onward = [(far[i:i + half] + recv[rows + i:rows + i + half].astype(f32)).astype(bf16) for i in (0, half)]
+    return keep, recv, [by_row(o) for o in onward], onward
+
+
+def gather_halves(first, second, near):
+    far = by_row(first), by_row(second)
+    return first, second, near, by_core(second), *far, by_core(far[0]), by_core(far[1])
 
 
 def after(value, *others):
@@ -557,11 +585,11 @@
             out_specs=[vmem] * len(outs),
             scratch_shapes=[pltpu.VMEM(s, d) for s, d in scratch],
             input_output_aliases=aliases or {},
-            compiler_params=pltpu.CompilerParams(vmem_limit_bytes=None if wide else 24 * 2**20),
+            compiler_params=pltpu.CompilerParams(vmem_limit_bytes=None if wide else 8 * 2**20),
             cost_estimate=pl.CostEstimate(flops=int(micros * 1.1e9), bytes_accessed=0, transcendentals=0),
         )(*args)
 
-    def placed(body, values, start, shapes, blocks_of, extra, scratch, aliases):
+    def placed(body, values, start, shapes, blocks_of, extra, scratch, aliases, *first):
         def at_chunk(p, s):
             return (chunk_at(s[0], s[1], replicas, p + start), 0)
 
@@ -578,9 +606,9 @@
                 out_specs=[pl.BlockSpec(b, at_chunk) if b else whole(s) for s, b in zip(shapes, blocks_of)],
                 scratch_shapes=[pltpu.VMEM(s, f32) for s in scratch]),
             input_output_aliases=aliases,
-            compiler_params=pltpu.CompilerParams(vmem_limit_bytes=24 * 2**20),
+            compiler_params=pltpu.CompilerParams(vmem_limit_bytes=8 * 2**20),
             cost_estimate=pl.CostEstimate(flops=int(2.2e9), bytes_accessed=0, transcendentals=0),
-        )(place, values, *extra)
+        )(after(place, *first) if first else place, values, *extra)
 
     block, = call(pack_body, 1, [((rows + 16, width), bf16)], [], tokens, pass_ids, pass_table.T, norm1_gain, norm1_bias,
                   out_bias, norm2_gain, norm2_bias, down_bias, ranked=False, wide=True)
@@ -595,18 +623,17 @@
         [], place, up_weight, after(cotangent, own_q))
     x2 = after(x2, own_u)
     blocks = block, x1, x2, by_core(x2)
-    sin, par, nrm, nrm_late, unit, inv, ids = call(
+    segc, segr, sin, par, nrm, nrm_late, unit, inv, ids = call(
         norm_body, 0,
-        [((rows, width), f32), ((16, width), f32), ((seq, width), bf16), ((seq, width), bf16), ((seq, width), bf16),
-         ((seq, 1), f32), ((8, rows), f32)], [], place, *blocks)
-    far_q = after(far_q, nrm)
+        [((seq, 1), f32), ((8, seq), f32), ((rows, width), f32), ((16, width), f32), ((seq, width), bf16),
+         ((seq, width), bf16), ((seq, width), bf16), ((seq, 1), f32), ((8, rows), f32)], [], place, seg_ids, *blocks)
+    far_q = after(far_q, ids)
     wq = own_q, by_core(near_q), far_q, by_core(far_q[part:])
     far_u = by_row(far_u)
     group = by_core(near_u), far_u, by_core(far_u)
     pair_u = lax.ppermute(far_u[rows:], ("replica", "shard"), [
         (4 * r + s, 4 * (r ^ 1) + (s ^ (r & 1))) for r in range(replicas) for s in range(4)])
 
-    segc, segr = seg_ids[:, None], seg_ids[None, :]
     heads = part // HD
     half_f, half_b, row_f, row_b = ((2 * rows, width), f32), ((2 * rows, width), bf16), ((rows, width), f32), ((rows, width), bf16)
     send, keep, far, qkv, ctx, lse, wq_full = call(
@@ -614,23 +641,33 @@
         [half_b, row_f, row_f, ((seq, 3 * part), bf16), ((seq, part), bf16), ((8, seq), f32), ((width, 3 * part), bf16)],
         [((seq, 128), f32), ((3 * heads, seq, HD), bf16), ((heads, seq, HD), bf16), ((heads, seq, 1), f32)],
         place, segc, segr, nrm, *wq, out_weight)
-    parts = scatter_sum(after(send, far_u), keep, far, rows)
-    mid, nrm2 = call(mid_body, 1, [row_f, row_b], [], sin, par, *parts[:2], after(parts[2], pair_u), ranked=False)
-    n2 = gather_rows(nrm2)
+    half = rows // 2
+    hrow_f, hrow_b = ((half, width), f32), ((half, width), bf16)
+    keep, recv, (first, second), _ = scatter_sum(after(send, far_u), keep, far, rows)
+    def middle(start, part_far):
+        return call(functools.partial(mid_body, start), 1, [hrow_f, hrow_b], [], sin, par, keep, recv, part_far,
+                    ranked=False)
+
+    mid_a, nrm_a = middle(0, first)
+    near_a = by_core(nrm_a)
+    mid_b, nrm_b = middle(half, after(second, pair_u, near_a))
+    mids = mid_a, mid_b
+    n2 = gather_halves(nrm_a, nrm_b, near_a)
     send, keep, far, act, pg = call(
         feed_body, 5, [half_b, row_f, row_f, ((seq, hidden), bf16), ((seq, hidden), bf16)],
         [((width, hidden), bf16)],
         place, *n2, cotangent, *group, own_u, pair_u, up_bias, down_weight)
-    *back, onward = scatter_sum(send, keep, far, rows)
+    keep, recv, fars, onward = scatter_sum(send, keep, far, rows)
     feed_rows = hidden // replicas + 4 * (part // replicas)
     if packed:
         grads = [((replicas // 2, feed_rows, width), bf16)] * 2
     else:
         grads = [((hidden, width), f32), ((width, hidden), f32)]
+    place_g = after(place, *onward)
     up_b, gkeep, gsend = call(
         functools.partial(feed_grad_body, replicas), 8, [((8, hidden), f32)] + grads,
         [((hidden, width), f32), ((width, hidden), f32)],
-        place, *n2, cotangent, *group, after(act, onward), pg)
+        place_g, *n2, cotangent, *group, act, pg)
     if not packed:
         nat = chunk_at(rank, me, replicas, jnp.arange(replicas))
         downs = gkeep.reshape(replicas, -1, width)[nat]
@@ -639,10 +676,14 @@
         both = both.astype(bf16)
         gkeep, gsend = both[:replicas // 2], both[replicas // 2:]
     got = plane_swap(gsend, replicas, 0)
-    mid_grad, branch, small_mid = call(
-        mid_back_body, 6, [row_f, row_b, ((16, width), f32)], [], mid, par, after(cotangent, up_b), ids, *back, ranked=False)
-    branches = gather_rows(branch)
-    got = after(got, branches[1])
+    mid_grads, halves, smalls_mid = [], [], []
+    for start, value, part_far in ((0, mids[0], fars[0]), (half, mids[1], fars[1])):
+        outs = call(functools.partial(mid_back_body, start), 8, [hrow_f, hrow_b, ((16, width), f32)], [],
+                    value, par, cotangent, after(ids, up_b), keep, recv, part_far, ranked=False)
+        for group_of, out in zip((mid_grads, halves, smalls_mid), outs):
+            group_of.append(out)
+    branches = gather_halves(*halves, by_core(halves[0]))
+    got = after(got, branches[2])
     for phase in range(1, max(phases - 1, 1)):
         gkeep, gsend = split_step(gkeep, got)
         got = plane_swap(gsend, replicas, phase)
@@ -654,9 +695,8 @@
         grads = [((replicas // 2, qkv_rows, 3 * part), bf16)] * 2
     else:
         grads = [((width, 3 * part), f32), ((part, width), f32)]
-    first, rest = range(heads - 1), range(heads - 1, heads)
     dctx, delta, grad_out, dqkv = call(
-        functools.partial(attn_back_one_body, first), 6,
+        functools.partial(attn_back_one_body, range(heads)), 9,
         [((seq, part), bf16), ((8, seq), f32), ((part, width), f32), ((seq, 3 * part), bf16)],
         [((seq, 128), f32), ((seq, HD), f32)],
         place, segc, segr, *branches, qkv, ctx, lse, out_weight)
@@ -664,10 +704,10 @@
         gkeep, gsend = split_step(gkeep, after(got, delta))
         got = plane_swap(gsend, replicas, phases - 1)
     send, keep, far, qkeep, qsend, smalls = call(
-        functools.partial(attn_back_two_body, replicas, rest), 6,
+        functools.partial(attn_back_two_body, replicas), 5,
         [half_b, row_f, row_f] + grads + [((4, 16, part), f32)],
-        [((seq, 3 * part), bf16), ((seq, HD), f32), ((width, 3 * part), f32), ((4, 16, part), f32)],
-        place, segc, segr, qkv, lse, after(delta, gsend), dctx, dqkv, grad_out, nrm_late, unit, inv, ids, par, small_mid, up_b,
+        [((width, 3 * part), f32), ((4, 16, part), f32)],
+        after(place, gsend), dqkv, grad_out, nrm_late, unit, inv, ids, par, *smalls_mid, up_b,
         wq_full)
     if not packed:
         qs = qkeep.reshape(4, replicas, -1, 3 * part)[rank ^ jnp.arange(4)][:, nat].transpose(1, 0, 2, 3)
@@ -716,9 +756,15 @@
 
     def qkv_first():
         low = now["low"]
-        quads = [low[:step]] + [after(s, now["turn"]) for s in now["quads"]]
-        own_small = sum(q[ur:].astype(f32) for q in quads).astype(bf16)
-        now["qkv_all"] = jnp.concatenate([q[:ur] for q in quads] + [own_small, low[4 * step:]], 0)[None]
+        quads = [after(s, now["turn"]) for s in now["quads"]]
+        if packed:
+            joined, = call(join_qkv_body, 0, [((qkv_rows - 3 * (small // replicas), 3 * part), bf16)], [], low, *quads,
+                           ranked=False)
+        else:
+            quads = [low[:step]] + quads
+            own_small = sum(q[ur:].astype(f32) for q in quads).astype(bf16)
+            joined = jnp.concatenate([q[:ur] for q in quads] + [own_small, low[4 * step:]], 0)
+        now["qkv_all"] = joined[None]
         now["qkv"] = plane_swap(now["qkv_all"], replicas, last_phase)
         now["turn"] = now["qkv_all"]
 
@@ -734,13 +780,12 @@
         now["tokens"], now["turn"] = by_row(onward), onward
 
     def tokens_end():
-        now["tokens_grad"], = call(last_body, 1, [row_b], [], sin, par, after(mid_grad, now["turn"]), keep, recv,
+        now["tokens_grad"], = call(last_body, 0, [row_b], [], sin, after(par, now["turn"]), *mid_grads, keep, recv,
                                    now["tokens"], ranked=False)
         now["turn"] = now["tokens_grad"]
 
     def out_start():
-        now["out"] = call(feed_out_body, 0, [half_b, row_f, row_f], [], down_weight, after(act, now["turn"]),
-                          ranked=False)
+        now["out"] = call(feed_out_body, 0, [half_b, row_f, row_f], [], after(place, now["turn"]), down_weight, act)
         now["turn"] = now["out"][0]
         now["recv_o"] = by_core(now["out"][0])
 
@@ -749,20 +794,20 @@
         now["far_o"], now["turn"] = by_row(onward), onward
 
     def out_end():
-        now["output"] = (mid + now["out"][1] + now["recv_o"][:rows].astype(f32)
+        now["output"] = (jnp.concatenate(mids, 0) + now["out"][1] + now["recv_o"][:rows].astype(f32)
                          + after(now["far_o"], now["turn"]).astype(f32) + par[10:11]).astype(bf16)
         now["turn"] = now["output"]
 
     def feed_place():
         if packed:
-            now["filled"] = placed(place_feed_body, after(now["feed_all"], now["turn"]), 0, *feed_shapes, [], [], {})
+            now["filled"] = placed(place_feed_body, now["feed_all"], 0, *feed_shapes, [], [], {}, now["turn"])
             now["turn"] = now["filled"][0]
 
     def qkv_place():
         if packed:
             now["qfilled"] = placed(
-                functools.partial(place_qkv_body, replicas, 0), after(now["qkv_all"], now["turn"]), 0,
-                qkv_shapes[0] + [sm_shape], qkv_shapes[1] + [None], [], [stage], {})
+                functools.partial(place_qkv_body, replicas, 0), now["qkv_all"], 0,
+                qkv_shapes[0] + [sm_shape], qkv_shapes[1] + [None], [], [stage], {}, now["turn"])
             now["turn"] = now["qfilled"][0]
 
     feed_shapes = [(hidden, width), (part, 4 * hidden)], [(lo, width), (ur, 4 * hidden)]

time: 199 us -> 194 us (0.975)
  waiting for transfers between devices: 92.3 us -> 102 us
  local copies, waits for them, and re-layouts: 10.1 us -> 0.6 us
  other arithmetic: 5.14 us -> 2.56 us
    ppermute x11 -> x15, waiting for transfers between devices: 36.2 us -> 46.9 us  [by_row(): return lax.ppermute(value, 'shard', ROWY)]
    unnamed x50 -> x16, local copies, waits for them, and re-layouts: 8.25 us -> 0.04 us
    ppermute x1, waiting for transfers between devices: 7.78 us -> 2.38 us  [shards(): lax.ppermute(far_u[rows:], ('replica', 'shard'), [(4 * r + s, 4 * (r ^ 1)...]
    ppermute x12, waiting for transfers between devices: 39.6 us -> 43.9 us  [plane_swap(): return lax.ppermute(value, ('replica', 'shard'), plane_pairs(count, phase))]
    ppermute x12, starting transfers between devices: 14.4 us -> 10.8 us  [plane_swap(): return lax.ppermute(value, ('replica', 'shard'), plane_pairs(count, phase))]
    pallas_call x13 -> x16, Pallas kernels: 45.3 us -> 44.2 us  [call(): pl.pallas_call(body, out_shape=[jax.ShapeDtypeStruct(s, d) for s, d in ou...]
    ppermute x11 -> x15, starting transfers between devices: 15.9 us -> 16.1 us  [by_row(): return lax.ppermute(value, 'shard', ROWY)]
    ppermute x16 -> x20, waiting for transfers between devices: 7.49 us -> 7.37 us  [by_core(): return lax.ppermute(value, 'shard', CORE)]
  transfers between devices with their start and end apart: 42 -> 50, of which waited for: 26 -> 29; matrix products, arithmetic and copies ran while one was open for 3% -> 1% of each run, Pallas kernels for 23% -> 23%
where the time goes in v1:
time: 194 us
  waiting for transfers between devices  102 us (53%)
  Pallas kernels  54.2 us (28%)
  starting transfers between devices  33.3 us (17%)
  other arithmetic  2.56 us (1%)
    ppermute x15, waiting for transfers between devices, by_row(): return lax.ppermute(value, 'shard', ROWY)  46.9 us
    pallas_call x16, Pallas kernels, call(): pl.pallas_call(body, out_shape=[jax.ShapeDtypeStruct(s, d) for s, d in ou...  44.2 us
    ppermute x12, waiting for transfers between devices, plane_swap(): return lax.ppermute(value, ('replica', 'shard'), plane_pairs(count, phase))  43.9 us
    ppermute x15, starting transfers between devices, by_row(): return lax.ppermute(value, 'shard', ROWY)  16.1 us
    ppermute x12, starting transfers between devices, plane_swap(): return lax.ppermute(value, ('replica', 'shard'), plane_pairs(count, phase))  10.8 us
    pallas_call x4, Pallas kernels, placed(): pl.pallas_call(body, out_shape=[jax.ShapeDtypeStruct(s, f32) for s in sha...  10 us
    ppermute x20, waiting for transfers between devices, by_core(): return lax.ppermute(value, 'shard', CORE)  7.37 us
  transfers between devices with their start and end apart: 50, of which 29 were waited for; matrix products, arithmetic and copies ran while one was open for 1% of the time, Pallas kernels for 23%

profile of v1, /device:TPU:0, one launch (start us, length us, event | category | flops | bytes accessed | tf_op | source)
XLA Modules:
  0.0 193.8 jit_solution(4515044479315224070)
XLA Ops:
  2.7 3.0 %collective-permute-start.1 = (bf16[272,768]{1,0:T(8,128)(2,1)}, bf16[272,768]{1,0:T(8,128)(2,1)S(1)}, u32[]{:S(2)}, u32[]{:S(2)}) collective-permute-start(bf16[272,768]{1,0:T(8,128)(2,1)} %shard_map.263.x0), channel_id=1, source_target_pairs={{0,2},{1,3},{2,0},{3,1},{4,6},{5,7},{6,4},{7,5},{8,10},{9,11},{10,... | collective-permute-start | bytes 1253384 | tf_op jit(solution)/shard_map/ppermute | solution.py:504
  7.4 8.9 %collective-permute-done.1.x2 = bf16[272,768]{1,0:T(8,128)(2,1)S(1)} collective-permute-done((bf16[272,768]{1,0:T(8,128)(2,1)}, bf16[272,768]{1,0:T(8,128)(2,1)S(1)}, u32[]{:S(2)}, u32[]{:S(2)}) %collective-permute-start.1) | collective-permute-done | bytes 417824 | tf_op jit(solution)/shard_map/ppermute | solution.py:504
  20.7 6.1 %collective-permute-done.4.w2 = bf16[384,576]{1,0:T(8,128)(2,1)S(1)} collective-permute-done((bf16[384,576]{1,0:T(8,128)(2,1)S(1)}, bf16[384,576]{1,0:T(8,128)(2,1)S(1)}, u32[]{:S(2)}, u32[]{:S(2)}) %collective-permute-start.4) | collective-permute-done | bytes 442400 | tf_op jit(solution)/shard_map/ppermute | solution.py:504
  28.5 9.9 %shard_map.267 = (bf16[512,768]{1,0:T(8,128)(2,1)S(1)}, f32[256,768]{1,0:T(8,128)S(1)}, f32[256,768]{1,0:T(8,128)S(1)}, bf16[1024,576]{1,0:T(8,128)(2,1)S(1)}, b...) custom-call(s32[3]{0:T(128)S(1)} %pad_add_fusion.rank_ref, ...), custom_call_target="tpu_custom_call" | custom-call | flops 4400000000 | tf_op jit(solution)/shard_map/pallas_call | solution.py:581
  38.4 2.4 %collective-permute-done.6.g2 = bf16[448,768]{1,0:T(8,128)(2,1)S(1)} collective-permute-done((bf16[448,768]{1,0:T(8,128)(2,1)S(1)}, bf16[448,768]{1,0:T(8,128)(2,1)S(1)}, u32[]{:S(2)}, u32[]{:S(2)}) %collective-permute-start.6) | collective-permute-done | bytes 688160 | tf_op jit(solution)/shard_map/ppermute | solution.py:504
  40.8 2.3 %collective-permute-done.7.recv_ref = bf16[512,768]{1,0:T(8,128)(2,1)S(1)} collective-permute-done((bf16[512,768]{1,0:T(8,128)(2,1)S(1)}, bf16[512,768]{1,0:T(8,128)(2,1)S(1)}, u32[]{:S(2)}, u32[]{:S(2)}) %collective-permute-start.7) | collective-permute-done | bytes 786464 | tf_op jit(solution)/shard_map/ppermute | solution.py:500
  47.0 3.9 %collective-permute-done.8.yrecv_ref = bf16[128,768]{1,0:T(8,128)(2,1)S(1)} collective-permute-done((bf16[128,768]{1,0:T(8,128)(2,1)S(1)}, bf16[128,768]{1,0:T(8,128)(2,1)S(1)}, u32[]{:S(2)}, u32[]{:S(2)}) %collective-permute-start.8) | collective-permute-done | bytes 196640 | tf_op jit(solution)/shard_map/ppermute | solution.py:504
  51.9 2.4 %collective-permute-done.10.pair_ref = bf16[192,768]{1,0:T(8,128)(2,1)S(1)} collective-permute-done((bf16[192,768]{1,0:T(8,128)(2,1)S(1)}, bf16[192,768]{1,0:T(8,128)(2,1)S(1)}, u32[]{:S(2)}, u32[]{:S(2)}) %collective-permute-start.10) | collective-permute-done | bytes 294944 | tf_op jit(solution)/shard_map/ppermute | solution.py:634
  56.7 5.4 %collective-permute-done.13.n2 = bf16[128,768]{1,0:T(8,128)(2,1)S(1)} collective-permute-done((bf16[128,768]{1,0:T(8,128)(2,1)S(1)}, bf16[128,768]{1,0:T(8,128)(2,1)S(1)}, u32[]{:S(2)}, u32[]{:S(2)}) %collective-permute-start.13) | collective-permute-done | bytes 196640 | tf_op jit(solution)/shard_map/ppermute | solution.py:504
  62.1 3.4 %collective-permute-done.14.m2 = bf16[128,768]{1,0:T(8,128)(2,1)S(1)} collective-permute-done((bf16[128,768]{1,0:T(8,128)(2,1)S(1)}, bf16[128,768]{1,0:T(8,128)(2,1)S(1)}, u32[]{:S(2)}, u32[]{:S(2)}) %collective-permute-start.14) | collective-permute-done | bytes 196640 | tf_op jit(solution)/shard_map/ppermute | solution.py:504
  66.9 5.4 %shard_map.270 = (bf16[512,768]{1,0:T(8,128)(2,1)S(1)}, f32[256,768]{1,0:T(8,128)S(1)}, f32[256,768]{1,0:T(8,128)S(1)}, bf16[1024,768]{1,0:T(8,128)(2,1)S(1)}, bf16[1024,768]{1,0:T(8,128)(2,1)S(1)}) custom-call(s32[3]{0:T(128)S(1)} %pad_add_fusion.rank_ref, bf16[128,768]{1,0:T(8,128)(2,1)S(1)} %get-tuple-element.134.n0, ...), custom_call_target="tpu_custom_call" | custom-call | flops 5500000256 | tf_op jit(solution)/shard_map/pallas_call | solution.py:581
  72.5 2.1 %collective-permute-done.19.recv_ref = bf16[512,768]{1,0:T(8,128)(2,1)S(1)} collective-permute-done((bf16[512,768]{1,0:T(8,128)(2,1)S(1)}, bf16[512,768]{1,0:T(8,128)(2,1)S(1)}, u32[]{:S(2)}, u32[]{:S(2)}) %collective-permute-start.19) | collective-permute-done | bytes 786464 | tf_op jit(solution)/shard_map/ppermute | solution.py:500
  76.9 3.8 %shard_map.271 = (f32[8,768]{1,0:T(8,128)S(1)}, bf16[4,192,768]{2,1,0:T(8,128)(2,1)S(1)}, bf16[4,192,768]{2,1,0:T(8,128)(2,1)S(1)}) custom-call(s32[3]{0:T(128)S(1)} %pad_add_fusion.rank_ref, bf16[128,768]{1,0:T(8,128)(2,1)S(1)} %get-tuple-element.134.n0, bf16[128,768]{1,0:T(8,128)(2,1)S(1)} %get-tuple-element.137.m0, ...), custom_call_target="tpu_custom_call" | custom-call | flops 8800000000 | tf_op jit(solution)/shard_map/pallas_call | solution.py:581
  83.5 3.3 %collective-permute-done.21.yrecv_ref = bf16[128,768]{1,0:T(8,128)(2,1)S(1)} collective-permute-done((bf16[128,768]{1,0:T(8,128)(2,1)S(1)}, bf16[128,768]{1,0:T(8,128)(2,1)S(1)}, u32[]{:S(2)}, u32[]{:S(2)}) %collective-permute-start.21) | collective-permute-done | bytes 196640 | tf_op jit(solution)/shard_map/ppermute | solution.py:504
  88.2 2.8 %collective-permute-done.27.f2 = bf16[128,768]{1,0:T(8,128)(2,1)S(1)} collective-permute-done((bf16[128,768]{1,0:T(8,128)(2,1)S(1)}, bf16[128,768]{1,0:T(8,128)(2,1)S(1)}, u32[]{:S(2)}, u32[]{:S(2)}) %collective-permute-start.27) | collective-permute-done | bytes 196640 | tf_op jit(solution)/shard_map/ppermute | solution.py:504
  91.0 3.4 %collective-permute-done.26.g2 = bf16[128,768]{1,0:T(8,128)(2,1)S(1)} collective-permute-done((bf16[128,768]{1,0:T(8,128)(2,1)S(1)}, bf16[128,768]{1,0:T(8,128)(2,1)S(1)}, u32[]{:S(2)}, u32[]{:S(2)}) %collective-permute-start.26) | collective-permute-done | bytes 196640 | tf_op jit(solution)/shard_map/ppermute | solution.py:504
  94.4 2.5 %collective-permute-done.20 = bf16[4,192,768]{2,1,0:T(8,128)(2,1)S(1)} collective-permute-done((bf16[4,192,768]{2,1,0:T(8,128)(2,1)S(1)}, bf16[4,192,768]{2,1,0:T(8,128)(2,1)S(1)}, u32[]{:S(2)}, u32[]{:S(2)}) %collective-permute-start.20) | collective-permute-done | bytes 1179680 | tf_op jit(solution)/shard_map/ppermute | solution.py:555
  99.0 8.5 %shard_map.274 = (bf16[1024,192]{1,0:T(8,128)(2,1)}, f32[8,1024]{1,0:T(8,128)}, f32[192,768]{1,0:T(8,128)S(1)}, bf16[1024,576]{1,0:T(8,128)(2,1)S(1)}) custom-call(s32[3]{0:T(128)S(1)} %pad_add_fusion.rank_ref, f32[1024,1]{1,0:T(8,128)S(1)} %get-tuple-element.121.segc_ref, f32[8,1024]{1,0:T(8,128)S(1)} %get-tuple-element.122.segr_ref, ...), custom_call_target="tpu_custom_call" | custom-call | flops 9900000256 | tf_op jit(solution)/shard_map/pallas_call | solution.py:581
  107.6 2.7 %collective-permute-start.31 = (bf16[1,192,768]{2,1,0:T(8,128)(2,1)S(1)}, bf16[1,192,768]{2,1,0:T(8,128)(2,1)S(1)}, u32[]{:S(2)}, u32[]{:S(2)}) collective-permute-start(bf16[1,192,768]{2,1,0:T(8,128)(2,1)S(1)} %slice.151), channel_id=1, source_target_pairs={{0,16},{1,17},{2,18},{3,19},{4,20},{5,21},{6,22},{7,23},{8,24},{9,... | collective-permute-start | bytes 884744 | tf_op jit(solution)/shard_map/ppermute | solution.py:555
  110.3 6.0 %shard_map.275 = (bf16[512,768]{1,0:T(8,128)(2,1)S(1)}, f32[256,768]{1,0:T(8,128)S(1)}, f32[256,768]{1,0:T(8,128)S(1)}, bf16[4,136,576]{2,1,0:T(8,128)(2,1)S(1)}...) custom-call(s32[3]{0:T(128)S(1)} %pad_add_fusion.rank_ref, bf16[1024,576]{1,0:T(8,128)(2,1)S(1)} %get-tuple-element.156.dqkv_s, ...), custom_call_target="tpu_custom_call" | custom-call | flops 5500000256 | tf_op jit(solution)/shard_map/pallas_call | solution.py:581
  116.3 5.3 %collective-permute-done.31 = bf16[1,192,768]{2,1,0:T(8,128)(2,1)S(1)} collective-permute-done((bf16[1,192,768]{2,1,0:T(8,128)(2,1)S(1)}, bf16[1,192,768]{2,1,0:T(8,128)(2,1)S(1)}, u32[]{:S(2)}, u32[]{:S(2)}) %collective-permute-start.31) | collective-permute-done | bytes 294944 | tf_op jit(solution)/shard_map/ppermute | solution.py:555
  131.6 3.6 %collective-permute-done.38.yrecv_ref = bf16[256,768]{1,0:T(8,128)(2,1)S(1)} collective-permute-done((bf16[256,768]{1,0:T(8,128)(2,1)S(1)}, bf16[256,768]{1,0:T(8,128)(2,1)S(1)}, u32[]{:S(2)}, u32[]{:S(2)}) %collective-permute-start.38) | collective-permute-done | bytes 393248 | tf_op jit(solution)/shard_map/ppermute | solution.py:504
  137.1 2.1 %collective-permute-start.39 = (bf16[1,136,576]{2,1,0:T(8,128)(2,1)S(1)}, bf16[1,136,576]{2,1,0:T(8,128)(2,1)S(1)}, u32[]{:S(2)}, u32[]{:S(2)}) collective-permute-start(bf16[1,136,576]{2,1,0:T(8,128)(2,1)S(1)} %slice.161), channel_id=1, source_target_pairs={{0,16},{1,17},{2,18},{3,19},{4,20},{5,21},{6,22},{7,23},{8,24},{9,... | collective-permute-start | bytes 470024 | tf_op jit(solution)/shard_map/ppermute | solution.py:555
  139.2 10.4 %collective-permute-done.40 = bf16[1,192,768]{2,1,0:T(8,128)(2,1)S(1)} collective-permute-done((bf16[1,192,768]{2,1,0:T(8,128)(2,1)S(1)}, bf16[1,192,768]{2,1,0:T(8,128)(2,1)S(1)}, u32[]{:S(2)}, u32[]{:S(2)}) %collective-permute-start.40) | collective-permute-done | bytes 294944 | tf_op jit(solution)/shard_map/ppermute | solution.py:555
  149.8 3.6 %collective-permute-done.39 = bf16[1,136,576]{2,1,0:T(8,128)(2,1)S(1)} collective-permute-done((bf16[1,136,576]{2,1,0:T(8,128)(2,1)S(1)}, bf16[1,136,576]{2,1,0:T(8,128)(2,1)S(1)}, u32[]{:S(2)}, u32[]{:S(2)}) %collective-permute-start.39) | collective-permute-done | bytes 156704 | tf_op jit(solution)/shard_map/ppermute | solution.py:555
  160.2 2.5 %shard_map.279 = (f32[768,768]{1,0:T(8,128)}, f32[192,3072]{1,0:T(8,128)}) custom-call(s32[3]{0:T(128)S(1)} %pad_add_fusion.rank_ref, bf16[4,192,768]{2,1,0:T(8,128)(2,1)S(1)} %pad_maximum_fusion.g_ref), custom_call_target="tpu_custom_call" | custom-call | flops 2200000000 | tf_op jit(solution)/shard_map/pallas_call | solution.py:599
  162.7 5.6 %collective-permute-done.45 = bf16[1,130,576]{2,1,0:T(8,128)(2,1)S(1)} collective-permute-done((bf16[1,130,576]{2,1,0:T(8,128)(2,1)S(1)}, bf16[1,130,576]{2,1,0:T(8,128)(2,1)S(1)}, u32[]{:S(2)}, u32[]{:S(2)}) %collective-permute-start.45) | collective-permute-done | bytes 149792 | tf_op jit(solution)/shard_map/ppermute | solution.py:555
  169.8 9.7 %collective-permute-done.47 = bf16[2,130,576]{2,1,0:T(8,128)(2,1)S(1)} collective-permute-done((bf16[2,130,576]{2,1,0:T(8,128)(2,1)S(1)}, bf16[2,130,576]{2,1,0:T(8,128)(2,1)S(1)}, u32[]{:S(2)}, u32[]{:S(2)}) %collective-permute-start.47) | collective-permute-done | bytes 299552 | tf_op jit(solution)/shard_map/ppermute | solution.py:555
  182.0 2.4 %shard_map.280 = (f32[192,2304]{1,0:T(8,128)}, f32[192,768]{1,0:T(8,128)}, f32[8,2,192]{2,1,0:T(2,128)S(1)}) custom-call(s32[3]{0:T(128)S(1)} %pad_add_fusion.rank_ref, bf16[4,130,576]{2,1,0:T(8,128)(2,1)S(1)} %pad_maximum_fusion.1.g_ref), custom_call_target="tpu_custom_call" | custom-call | flops 2200000000 | tf_op jit(solution)/shard_map/pallas_call | solution.py:599
  184.4 2.5 %shard_map.281 = (f32[768,768]{1,0:T(8,128)}, f32[192,3072]{1,0:T(8,128)}) custom-call(s32[3]{0:T(128)S(1)} %pad_add_fusion.rank_ref, bf16[4,192,768]{2,1,0:T(8,128)(2,1)S(1)} %collective-permute-done.49.g_ref, f32[768,768]{1,0:T(8,128)} %get-tuple-element.191.refs_0_, ...), custom_call_target="tpu_custom_call", output_to_operand_aliasing={{0}: (2, {}), {1}: (3, {})} | custom-call | flops 2200000000 | tf_op jit(solution)/shard_map/pallas_call | solution.py:599
  186.9 4.0 %collective-permute-done.48 = bf16[4,130,576]{2,0,1:T(4,128)(2,1)S(1)} collective-permute-done((bf16[4,130,576]{2,0,1:T(4,128)(2,1)S(1)}, bf16[4,130,576]{2,0,1:T(4,128)(2,1)S(1)}, u32[]{:S(2)}, u32[]{:S(2)}) %collective-permute-start.48) | collective-permute-done | bytes 599072 | tf_op jit(solution)/shard_map/ppermute | solution.py:555
  191.0 2.6 %shard_map.282 = (f32[192,2304]{1,0:T(8,128)}, f32[192,768]{1,0:T(8,128)}, f32[5,192]{1,0:T(8,128)}, f32[192]{0:T(256)}, f32[192]{0:T(256)}, /*index=5*/f32[192]...) custom-call(s32[3]{0:T(128)S(1)} %pad_add_fusion.rank_ref, ...), custom_call_target="tpu_custom_call", output_to_operand_aliasing={{0}: (3, {}), {1}: (4, {})} | custom-call | flops 2200000000 | tf_op jit(solution)/shard_map/pallas_call | solution.py:599
  (133 shorter events, 49.9 us)
Async XLA Ops:
  2.7 13.6 %collective-permute-start.1 = (bf16[272,768]{1,0:T(8,128)(2,1)}, bf16[272,768]{1,0:T(8,128)(2,1)S(1)}, u32[]{:S(2)}, u32[]{:S(2)}) collective-permute-start(bf16[272,768]{1,0:T(8,128)(2,1)} %shard_map.263.x0), channel_id=1, source_target_pairs={{0,2},{1,3},{2,0},{3,1},{4,6},{5,7},{6,4},{7,5},{8,10},{9,11},{10,... | collective-permute-start | bytes 1253384 | tf_op jit(solution)/shard_map/ppermute | solution.py:504
  6.6 20.3 %collective-permute-start.4 = (bf16[384,576]{1,0:T(8,128)(2,1)S(1)}, bf16[384,576]{1,0:T(8,128)(2,1)S(1)}, u32[]{:S(2)}, u32[]{:S(2)}) collective-permute-start(bf16[384,576]{1,0:T(8,128)(2,1)S(1)} %get-tuple-element.125), channel_id=1, source_target_pairs={{0,2},{1,3},{2,0},{3,1},{4,6},{5,7},{6,4},{7,5},{8,10},{9,11},{10,... | collective-permute-start | bytes 1327112 | tf_op jit(solution)/shard_map/ppermute | solution.py:504
  6.7 12.0 %collective-permute-start = (bf16[272,768]{1,0:T(8,128)(2,1)}, bf16[272,768]{1,0:T(8,128)(2,1)S(1)}, u32[]{:S(2)}, u32[]{:S(2)}) collective-permute-start(bf16[272,768]{1,0:T(8,128)(2,1)} %shard_map.263.x0), channel_id=1, source_target_pairs={{0,1},{1,0},{2,3},{3,2},{4,5},{5,4},{6,7},{7,6},{8,9},{9,8},{10,11... | collective-permute-start | bytes 1253384 | tf_op jit(solution)/shard_map/ppermute | solution.py:500
  16.3 24.4 %collective-permute-start.6 = (bf16[448,768]{1,0:T(8,128)(2,1)S(1)}, bf16[448,768]{1,0:T(8,128)(2,1)S(1)}, u32[]{:S(2)}, u32[]{:S(2)}) collective-permute-start(bf16[448,768]{1,0:T(8,128)(2,1)S(1)} %get-tuple-element.130), channel_id=1, source_target_pairs={{0,2},{1,3},{2,0},{3,1},{4,6},{5,7},{6,4},{7,5},{8,10},{9,11},{10,... | collective-permute-start | bytes 2064392 | tf_op jit(solution)/shard_map/ppermute | solution.py:504
  18.4 8.6 %collective-permute-start.3 = (bf16[192,576]{1,0:T(8,128)(2,1)S(1)}, bf16[192,576]{1,0:T(8,128)(2,1)S(1)}, u32[]{:S(2)}, u32[]{:S(2)}) collective-permute-start(bf16[192,576]{1,0:T(8,128)(2,1)S(1)} %get-tuple-element.124), channel_id=1, source_target_pairs={{0,1},{1,0},{2,3},{3,2},{4,5},{5,4},{6,7},{7,6},{8,9},{9,8},{10,11... | collective-permute-start | bytes 663560 | tf_op jit(solution)/shard_map/ppermute | solution.py:500
  43.2 7.8 %collective-permute-start.8 = (bf16[128,768]{1,0:T(8,128)(2,1)S(1)}, bf16[128,768]{1,0:T(8,128)(2,1)S(1)}, u32[]{:S(2)}, u32[]{:S(2)}) collective-permute-start(bf16[128,768]{1,0:T(8,128)(2,1)S(1)} %get-tuple-element.217), channel_id=1, source_target_pairs={{0,2},{1,3},{2,0},{3,1},{4,6},{5,7},{6,4},{7,5},{8,10},{9,11},{10,... | collective-permute-start | bytes 589832 | tf_op jit(solution)/shard_map/ppermute | solution.py:504
  45.0 9.3 %collective-permute-start.10 = (bf16[192,768]{1,0:T(8,128)(2,1)S(1)}, bf16[192,768]{1,0:T(8,128)(2,1)S(1)}, u32[]{:S(2)}, u32[]{:S(2)}) collective-permute-start(bf16[192,768]{1,0:T(8,128)(2,1)S(1)} %slice.146), channel_id=1, source_target_pairs={{0,4},{1,5},{2,6},{3,7},{4,1},{5,0},{6,3},{7,2},{8,12},{9,13},{10,... | collective-permute-start | bytes 884744 | tf_op jit(solution)/shard_map/ppermute | solution.py:634
  46.5 7.9 %collective-permute-start.9 = (bf16[128,768]{1,0:T(8,128)(2,1)S(1)}, bf16[128,768]{1,0:T(8,128)(2,1)S(1)}, u32[]{:S(2)}, u32[]{:S(2)}) collective-permute-start(bf16[128,768]{1,0:T(8,128)(2,1)S(1)} %get-tuple-element.216), channel_id=1, source_target_pairs={{0,2},{1,3},{2,0},{3,1},{4,6},{5,7},{6,4},{7,5},{8,10},{9,11},{10,... | collective-permute-start | bytes 589832 | tf_op jit(solution)/shard_map/ppermute | solution.py:504
  51.3 14.1 %collective-permute-start.17 = (bf16[448,768]{1,0:T(8,128)(2,1)S(1)}, bf16[448,768]{1,0:T(8,128)(2,1)S(1)}, u32[]{:S(2)}, u32[]{:S(2)}) collective-permute-start(bf16[448,768]{1,0:T(8,128)(2,1)S(1)} %get-tuple-element.138), channel_id=1, source_target_pairs={{0,1},{1,0},{2,3},{3,2},{4,5},{5,4},{6,7},{7,6},{8,9},{9,8},{10,11... | collective-permute-start | bytes 2064392 | tf_op jit(solution)/shard_map/ppermute | solution.py:500
  51.8 13.7 %collective-permute-start.18 = (bf16[448,768]{1,0:T(8,128)(2,1)S(1)}, bf16[448,768]{1,0:T(8,128)(2,1)S(1)}, u32[]{:S(2)}, u32[]{:S(2)}) collective-permute-start(bf16[448,768]{1,0:T(8,128)(2,1)S(1)} %collective-permute-done.6.g2), channel_id=1, source_target_pairs={{0,1},{1,0},{2,3},{3,2},{4,5},{5,4},{6,7},{7,6},{8,9},{9,8},{10,11... | collective-permute-start | bytes 2064392 | tf_op jit(solution)/shard_map/ppermute | solution.py:500
  54.7 10.8 %collective-permute-start.14 = (bf16[128,768]{1,0:T(8,128)(2,1)S(1)}, bf16[128,768]{1,0:T(8,128)(2,1)S(1)}, u32[]{:S(2)}, u32[]{:S(2)}) collective-permute-start(bf16[128,768]{1,0:T(8,128)(2,1)S(1)} %get-tuple-element.137.m0), channel_id=1, source_target_pairs={{0,2},{1,3},{2,0},{3,1},{4,6},{5,7},{6,4},{7,5},{8,10},{9,11},{10,... | collective-permute-start | bytes 589832 | tf_op jit(solution)/shard_map/ppermute | solution.py:504
  56.7 8.8 %collective-permute-start.12 = (bf16[128,768]{1,0:T(8,128)(2,1)S(1)}, bf16[128,768]{1,0:T(8,128)(2,1)S(1)}, u32[]{:S(2)}, u32[]{:S(2)}) collective-permute-start(bf16[128,768]{1,0:T(8,128)(2,1)S(1)} %get-tuple-element.137.m0), channel_id=1, source_target_pairs={{0,1},{1,0},{2,3},{3,2},{4,5},{5,4},{6,7},{7,6},{8,9},{9,8},{10,11... | collective-permute-start | bytes 589832 | tf_op jit(solution)/shard_map/ppermute | solution.py:500
  74.8 7.8 %collective-permute-start.24 = (bf16[128,768]{1,0:T(8,128)(2,1)S(1)}, bf16[128,768]{1,0:T(8,128)(2,1)S(1)}, u32[]{:S(2)}, u32[]{:S(2)}) collective-permute-start(bf16[128,768]{1,0:T(8,128)(2,1)S(1)} %get-tuple-element.214), channel_id=1, source_target_pairs={{0,2},{1,3},{2,0},{3,1},{4,6},{5,7},{6,4},{7,5},{8,10},{9,11},{10,... | collective-permute-start | bytes 589832 | tf_op jit(solution)/shard_map/ppermute | solution.py:504
  75.1 11.7 %collective-permute-start.21 = (bf16[128,768]{1,0:T(8,128)(2,1)S(1)}, bf16[128,768]{1,0:T(8,128)(2,1)S(1)}, u32[]{:S(2)}, u32[]{:S(2)}) collective-permute-start(bf16[128,768]{1,0:T(8,128)(2,1)S(1)} %get-tuple-element.215), channel_id=1, source_target_pairs={{0,2},{1,3},{2,0},{3,1},{4,6},{5,7},{6,4},{7,5},{8,10},{9,11},{10,... | collective-permute-start | bytes 589832 | tf_op jit(solution)/shard_map/ppermute | solution.py:504
  80.7 16.3 %collective-permute-start.20 = (bf16[4,192,768]{2,1,0:T(8,128)(2,1)S(1)}, bf16[4,192,768]{2,1,0:T(8,128)(2,1)S(1)}, u32[]{:S(2)}, u32[]{:S(2)}) collective-permute-start(bf16[4,192,768]{2,1,0:T(8,128)(2,1)S(1)} %get-tuple-element.145), channel_id=1, source_target_pairs={{0,4},{1,9},{2,6},{3,11},{4,0},{5,13},{6,2},{7,15},{8,12},{9,1},{1... | collective-permute-start | bytes 3538952 | tf_op jit(solution)/shard_map/ppermute | solution.py:555
  83.2 7.8 %collective-permute-start.27 = (bf16[128,768]{1,0:T(8,128)(2,1)S(1)}, bf16[128,768]{1,0:T(8,128)(2,1)S(1)}, u32[]{:S(2)}, u32[]{:S(2)}) collective-permute-start(bf16[128,768]{1,0:T(8,128)(2,1)S(1)} %get-tuple-element.152.f0), channel_id=1, source_target_pairs={{0,2},{1,3},{2,0},{3,1},{4,6},{5,7},{6,4},{7,5},{8,10},{9,11},{10,... | collective-permute-start | bytes 589832 | tf_op jit(solution)/shard_map/ppermute | solution.py:504
  87.7 11.3 %collective-permute-start.25 = (bf16[128,768]{1,0:T(8,128)(2,1)S(1)}, bf16[128,768]{1,0:T(8,128)(2,1)S(1)}, u32[]{:S(2)}, u32[]{:S(2)}) collective-permute-start(bf16[128,768]{1,0:T(8,128)(2,1)S(1)} %get-tuple-element.152.f0), channel_id=1, source_target_pairs={{0,1},{1,0},{2,3},{3,2},{4,5},{5,4},{6,7},{7,6},{8,9},{9,8},{10,11... | collective-permute-start | bytes 589832 | tf_op jit(solution)/shard_map/ppermute | solution.py:500
  91.0 8.0 %collective-permute-start.29 = (bf16[128,768]{1,0:T(8,128)(2,1)S(1)}, bf16[128,768]{1,0:T(8,128)(2,1)S(1)}, u32[]{:S(2)}, u32[]{:S(2)}) collective-permute-start(bf16[128,768]{1,0:T(8,128)(2,1)S(1)} %collective-permute-done.27.f2), channel_id=1, source_target_pairs={{0,1},{1,0},{2,3},{3,2},{4,5},{5,4},{6,7},{7,6},{8,9},{9,8},{10,11... | collective-permute-start | bytes 589832 | tf_op jit(solution)/shard_map/ppermute | solution.py:500
  97.3 10.1 %collective-permute-start.23 = (bf16[2,192,768]{2,1,0:T(8,128)(2,1)S(1)}, bf16[2,192,768]{2,1,0:T(8,128)(2,1)S(1)}, u32[]{:S(2)}, u32[]{:S(2)}) collective-permute-start(bf16[2,192,768]{2,1,0:T(8,128)(2,1)S(1)} %slice.150), channel_id=1, source_target_pairs={{0,8},{1,5},{2,10},{3,7},{4,12},{5,1},{6,14},{7,3},{8,0},{9,13},{1... | collective-permute-start | bytes 1769480 | tf_op jit(solution)/shard_map/ppermute | solution.py:555
  107.6 14.0 %collective-permute-start.31 = (bf16[1,192,768]{2,1,0:T(8,128)(2,1)S(1)}, bf16[1,192,768]{2,1,0:T(8,128)(2,1)S(1)}, u32[]{:S(2)}, u32[]{:S(2)}) collective-permute-start(bf16[1,192,768]{2,1,0:T(8,128)(2,1)S(1)} %slice.151), channel_id=1, source_target_pairs={{0,16},{1,17},{2,18},{3,19},{4,20},{5,21},{6,22},{7,23},{8,24},{9,... | collective-permute-start | bytes 884744 | tf_op jit(solution)/shard_map/ppermute | solution.py:555
  116.3 11.0 %collective-permute-start.34 = (bf16[4,136,576]{2,1,0:T(8,128)(2,1)S(1)}, bf16[4,136,576]{2,1,0:T(8,128)(2,1)S(1)}, u32[]{:S(2)}, u32[]{:S(2)}) collective-permute-start(bf16[4,136,576]{2,1,0:T(8,128)(2,1)S(1)} %get-tuple-element.173), channel_id=1, source_target_pairs={{0,4},{1,9},{2,6},{3,11},{4,0},{5,13},{6,2},{7,15},{8,12},{9,1},{1... | collective-permute-start | bytes 1880072 | tf_op jit(solution)/shard_map/ppermute | solution.py:555
  123.8 11.4 %collective-permute-start.38 = (bf16[256,768]{1,0:T(8,128)(2,1)S(1)}, bf16[256,768]{1,0:T(8,128)(2,1)S(1)}, u32[]{:S(2)}, u32[]{:S(2)}) collective-permute-start(bf16[256,768]{1,0:T(8,128)(2,1)S(1)} %add_convert_fusion.4), channel_id=1, source_target_pairs={{0,2},{1,3},{2,0},{3,1},{4,6},{5,7},{6,4},{7,5},{8,10},{9,11},{10,... | collective-permute-start | bytes 1179656 | tf_op jit(solution)/shard_map/ppermute | solution.py:504
  127.6 9.4 %collective-permute-start.37 = (bf16[2,136,576]{2,1,0:T(8,128)(2,1)S(1)}, bf16[2,136,576]{2,1,0:T(8,128)(2,1)S(1)}, u32[]{:S(2)}, u32[]{:S(2)}) collective-permute-start(bf16[2,136,576]{2,1,0:T(8,128)(2,1)S(1)} %slice.159), channel_id=1, source_target_pairs={{0,8},{1,5},{2,10},{3,7},{4,12},{5,1},{6,14},{7,3},{8,0},{9,13},{1... | collective-permute-start | bytes 940040 | tf_op jit(solution)/shard_map/ppermute | solution.py:555
  129.0 20.6 %collective-permute-start.40 = (bf16[1,192,768]{2,1,0:T(8,128)(2,1)S(1)}, bf16[1,192,768]{2,1,0:T(8,128)(2,1)S(1)}, u32[]{:S(2)}, u32[]{:S(2)}) collective-permute-start(bf16[1,192,768]{2,1,0:T(8,128)(2,1)S(1)} %maximum_bitcast_fusion), channel_id=1, source_target_pairs={{0,16},{1,17},{2,18},{3,19},{4,20},{5,21},{6,22},{7,23},{8,24},{9,... | collective-permute-start | bytes 884744 | tf_op jit(solution)/shard_map/ppermute | solution.py:555
  130.7 24.9 %collective-permute-start.33 = (bf16[512,768]{1,0:T(8,128)(2,1)S(1)}, bf16[512,768]{1,0:T(8,128)(2,1)S(1)}, u32[]{:S(2)}, u32[]{:S(2)}) collective-permute-start(bf16[512,768]{1,0:T(8,128)(2,1)S(1)} %get-tuple-element.171), channel_id=1, source_target_pairs={{0,1},{1,0},{2,3},{3,2},{4,5},{5,4},{6,7},{7,6},{8,9},{9,8},{10,11... | collective-permute-start | bytes 2359304 | tf_op jit(solution)/shard_map/ppermute | solution.py:500
  137.1 16.3 %collective-permute-start.39 = (bf16[1,136,576]{2,1,0:T(8,128)(2,1)S(1)}, bf16[1,136,576]{2,1,0:T(8,128)(2,1)S(1)}, u32[]{:S(2)}, u32[]{:S(2)}) collective-permute-start(bf16[1,136,576]{2,1,0:T(8,128)(2,1)S(1)} %slice.161), channel_id=1, source_target_pairs={{0,16},{1,17},{2,18},{3,19},{4,20},{5,21},{6,22},{7,23},{8,24},{9,... | collective-permute-start | bytes 470024 | tf_op jit(solution)/shard_map/ppermute | solution.py:555
  149.7 10.3 %collective-permute-start.46 = (bf16[2,192,768]{2,1,0:T(8,128)(2,1)S(1)}, bf16[2,192,768]{2,1,0:T(8,128)(2,1)S(1)}, u32[]{:S(2)}, u32[]{:S(2)}) collective-permute-start(bf16[2,192,768]{2,1,0:T(8,128)(2,1)S(1)} %pad_maximum_fusion.2), channel_id=1, source_target_pairs={{0,8},{1,5},{2,10},{3,7},{4,12},{5,1},{6,14},{7,3},{8,0},{9,13},{1... | collective-permute-start | bytes 1769480 | tf_op jit(solution)/shard_map/ppermute | solution.py:555
  158.4 9.8 %collective-permute-start.45 = (bf16[1,130,576]{2,1,0:T(8,128)(2,1)S(1)}, bf16[1,130,576]{2,1,0:T(8,128)(2,1)S(1)}, u32[]{:S(2)}, u32[]{:S(2)}) collective-permute-start(bf16[1,130,576]{2,1,0:T(8,128)(2,1)S(1)} %bitcast.23), channel_id=1, source_target_pairs={{0,16},{1,17},{2,18},{3,19},{4,20},{5,21},{6,22},{7,23},{8,24},{9,... | collective-permute-start | bytes 449288 | tf_op jit(solution)/shard_map/ppermute | solution.py:555
  160.1 24.3 %collective-permute-start.49 = (bf16[4,192,768]{2,1,0:T(8,128)(2,1)S(1)}, bf16[4,192,768]{2,1,0:T(8,128)(2,1)S(1)}, u32[]{:S(2)}, u32[]{:S(2)}) collective-permute-start(bf16[4,192,768]{2,1,0:T(8,128)(2,1)S(1)} %pad_maximum_fusion.g_ref), channel_id=1, source_target_pairs={{0,4},{1,9},{2,6},{3,11},{4,0},{5,13},{6,2},{7,15},{8,12},{9,1},{1... | collective-permute-start | bytes 3538952 | tf_op jit(solution)/shard_map/ppermute | solution.py:555
  168.3 11.2 %collective-permute-start.47 = (bf16[2,130,576]{2,1,0:T(8,128)(2,1)S(1)}, bf16[2,130,576]{2,1,0:T(8,128)(2,1)S(1)}, u32[]{:S(2)}, u32[]{:S(2)}) collective-permute-start(bf16[2,130,576]{2,1,0:T(8,128)(2,1)S(1)} %pad_maximum_fusion.3), channel_id=1, source_target_pairs={{0,8},{1,5},{2,10},{3,7},{4,12},{5,1},{6,14},{7,3},{8,0},{9,13},{1... | collective-permute-start | bytes 898568 | tf_op jit(solution)/shard_map/ppermute | solution.py:555
  168.4 11.9 %collective-permute-start.42 = (bf16[256,768]{1,0:T(8,128)(2,1)S(1)}, bf16[256,768]{1,0:T(8,128)(2,1)S(1)}, u32[]{:S(2)}, u32[]{:S(2)}) collective-permute-start(bf16[256,768]{1,0:T(8,128)(2,1)S(1)} %add_convert_fusion.3), channel_id=1, source_target_pairs={{0,2},{1,3},{2,0},{3,1},{4,6},{5,7},{6,4},{7,5},{8,10},{9,11},{10,... | collective-permute-start | bytes 1179656 | tf_op jit(solution)/shard_map/ppermute | solution.py:504
  180.2 10.7 %collective-permute-start.48 = (bf16[4,130,576]{2,0,1:T(4,128)(2,1)S(1)}, bf16[4,130,576]{2,0,1:T(4,128)(2,1)S(1)}, u32[]{:S(2)}, u32[]{:S(2)}) collective-permute-start(bf16[4,130,576]{2,0,1:T(4,128)(2,1)S(1)} %copy.34), channel_id=1, source_target_pairs={{0,4},{1,9},{2,6},{3,11},{4,0},{5,13},{6,2},{7,15},{8,12},{9,1},{1... | collective-permute-start | bytes 1797128 | tf_op jit(solution)/shard_map/ppermute | solution.py:555
  (26 other events, 163.7 us)

commit v2 on v1

--- a/solution.py
+++ b/solution.py
@@ -90,7 +90,7 @@
 
 
 def front_body(rank_ref, segc_ref, segr_ref, nrm_ref, w0, w1, w2, w3, wout_ref,
-               send_ref, keep_ref, far_ref, qkv_ref, ctx_ref, lse_ref, wq_ref, lse_s, head_s, ctx_s, top_s):
+               near_ref, both_ref, keep_ref, far_ref, qkv_ref, ctx_ref, lse_ref, wq_ref, lse_s, head_s, ctx_s, top_s, bias_s):
     rank = rank_ref[0]
     rows, width = keep_ref.shape
     part = width // 4
@@ -103,20 +103,23 @@
         head = qkv_ref[:, i * HD:(i + 1) * HD]
         head_s[i] = head * jnp.asarray(score_scale, bf16) if i < heads else head
 
+    for i in range(total_rows // rows):
+        lo, nk = i * rows, (i + 1) * rows
+        qpos = lo + lax.broadcasted_iota(jnp.int32, (rows, nk), 0)
+        kpos = lax.broadcasted_iota(jnp.int32, (rows, nk), 1)
+        seen = (segc_ref[lo:nk] == segr_ref[0:1, :nk]) & (kpos <= qpos)
+        bias_s[lo:nk, :nk] = jnp.where(seen, 0.0, masked_score)
+
     def one_head(h, carry):
         q, key, val = head_s[h], head_s[heads + h], head_s[2 * heads + h]
         for i in range(total_rows // rows):
             lo, nk = i * rows, (i + 1) * rows
-            sc = contract(q[lo:nk], key[:nk], 1, 1)
-            qpos = lo + lax.broadcasted_iota(jnp.int32, (rows, nk), 0)
-            kpos = lax.broadcasted_iota(jnp.int32, (rows, nk), 1)
-            seen = (segc_ref[lo:nk] == segr_ref[0:1, :nk]) & (kpos <= qpos)
-            sc = jnp.where(seen, sc, masked_score)
+            sc = contract(q[lo:nk], key[:nk], 1, 1) + bias_s[lo:nk, :nk]
             top = jnp.max(sc, -1, keepdims=True)
             e = jnp.exp(sc - top)
             total = jnp.sum(e, -1, keepdims=True)
-            prob = (e * (1.0 / total)).astype(bf16)
-            ctx_s[h, lo:nk] = jnp.dot(prob, val[:nk], preferred_element_type=f32).astype(bf16)
+            value_sum = jnp.dot(e.astype(bf16), val[:nk], preferred_element_type=f32)
+            ctx_s[h, lo:nk] = (value_sum * (1.0 / total)).astype(bf16)
             top_s[h, lo:nk] = top + jnp.log(total)
         return carry
 
@@ -125,8 +128,8 @@
         ctx_ref[:, h * HD:(h + 1) * HD] = ctx_s[h]
         lse_s[:, h:h + 1] = top_s[h]
     lse_ref[...] = lse_s[...].T[0:8]
-    for i, k in enumerate((1, 3)):
-        send_ref[i * rows:(i + 1) * rows] = jnp.dot(
+    for ref, k in ((both_ref, 3), (near_ref, 1)):
+        ref[...] = jnp.dot(
             ctx_ref[at_rows(rank ^ k, rows)], wout_ref[...], preferred_element_type=f32).astype(bf16)
     for ref, k in ((keep_ref, 0), (far_ref, 2)):
         ref[...] = jnp.dot(ctx_ref[at_rows(rank ^ k, rows)], wout_ref[...], preferred_element_type=f32)
@@ -154,7 +157,7 @@
 
 
 def feed_body(rank_ref, n0, m0, n1, m1, n2, m2, n3, m3, c0, g1, g2, g3, u0, pair_ref, ub_ref, dw_ref,
-              send_ref, keep_ref, far_ref, act_ref, pg_ref, wu_s):
+              near_ref, both_ref, keep_ref, far_ref, act_ref, pg_ref, wu_s):
     rank = rank_ref[0]
     rows, width = c0.shape
     part = width // 4
@@ -182,7 +185,7 @@
         pg_ref[k * rows:(k + 1) * rows] = pg
         back = contract(pg, wu_s[...], 1, 1)
         if k % 2:
-            send_ref[(k // 2) * rows:(k // 2 + 1) * rows] = back.astype(bf16)
+            (near_ref if k == 1 else both_ref)[...] = back.astype(bf16)
         else:
             (far_ref if k else keep_ref)[...] = back
 
@@ -273,10 +276,16 @@
     small_ref[11:12] = jnp.sum(cot, 0, keepdims=True)
 
 
-def heads_back(heads, segc_ref, segr_ref, qkv_ref, lse_ref, delta_ref, dctx_ref, dqkv_ref, dq_s):
+def heads_back(heads, segc_ref, segr_ref, qkv_ref, lse_ref, delta_ref, dctx_ref, dqkv_ref, dq_s, bias_s):
     part = dctx_ref.shape[1]
     total_rows = qkv_ref.shape[0]
     rows = total_rows // 4
+    for j in range(total_rows // rows):
+        lo, hi, nq = j * rows, (j + 1) * rows, total_rows - j * rows
+        kpos = lax.broadcasted_iota(jnp.int32, (rows, nq), 0)
+        qpos = lax.broadcasted_iota(jnp.int32, (rows, nq), 1)
+        seen = (segc_ref[lo:hi] == segr_ref[0:1, lo:]) & (kpos <= qpos)
+        bias_s[lo:hi, lo:] = jnp.where(seen, 0.0, masked_score)
     for h in heads:
         q = qkv_ref[:, h * HD:(h + 1) * HD] * jnp.asarray(score_scale, bf16)
         key = qkv_ref[:, part + h * HD:part + (h + 1) * HD]
@@ -285,12 +294,8 @@
         for j in range(total_rows // rows):
             lo = j * rows
             hi = lo + rows
-            nq = total_rows - lo
-            sc = contract(key[lo:hi], q[lo:], 1, 1)
-            kpos = lax.broadcasted_iota(jnp.int32, (rows, nq), 0)
-            qpos = lax.broadcasted_iota(jnp.int32, (rows, nq), 1)
-            seen = (segc_ref[lo:hi] == segr_ref[0:1, lo:]) & (kpos <= qpos)
-            prob = jnp.where(seen, jnp.exp(sc - lse_ref[h:h + 1, lo:]), 0.0)
+            sc = contract(key[lo:hi], q[lo:], 1, 1) + bias_s[lo:hi, lo:]
+            prob = jnp.exp(sc - lse_ref[h:h + 1, lo:])
             dv = jnp.dot(prob.astype(bf16), dctx[lo:], preferred_element_type=f32)
             dprob = contract(val[lo:hi], dctx[lo:], 1, 1)
             ds = (prob * (dprob - delta_ref[h:h + 1, lo:])).astype(bf16)
@@ -306,7 +311,7 @@
 
 
 def attn_back_one_body(heads, rank_ref, segc_ref, segr_ref, g0, f0, g1, f1, g2, f2, g3, f3, qkv_ref, ctx_ref, lse_ref, wout_ref,
-                       dctx_ref, delta_ref, go_ref, dqkv_ref, del_s, dq_s):
+                       dctx_ref, delta_ref, go_ref, dqkv_ref, del_s, dq_s, bias_s):
     rank = rank_ref[0]
     rows, width = 2 * g0.shape[0], g0.shape[1]
     part = width // 4
@@ -321,12 +326,48 @@
     for h in range(part // HD):
         del_s[:, h:h + 1] = jnp.sum(prod[:, h * HD:(h + 1) * HD], -1, keepdims=True)
     delta_ref[...] = del_s[...].T[0:8]
-    heads_back(heads, segc_ref, segr_ref, qkv_ref, lse_ref, delta_ref, dctx_ref, dqkv_ref, dq_s)
-
-
-def attn_back_two_body(count, rank_ref, dqkv_s, go_s, nrm_ref, unit_ref, inv_ref, ids_ref, par_ref, smid_ref, smid2_ref, upb_ref, wq_ref,
-                       send_ref, keep_ref, far_ref, gkeep_ref, gsend_ref, sm_ref, gq_s, sm_s):
+    heads_back(heads, segc_ref, segr_ref, qkv_ref, lse_ref, delta_ref, dctx_ref, dqkv_ref, dq_s, bias_s)
+
+
+def attn_back_two_body(count, rank_ref, dqkv_s, go_s, nrm_ref, wq_ref,
+                       send_ref, keep_ref, far_ref, gkeep_ref, gsend_ref, gq_s):
     rank, me = rank_ref[0], rank_ref[1]
+    rows, width = keep_ref.shape
+    for k in range(4):
+        back = contract(dqkv_s[at_rows(rank ^ k, rows)], wq_ref[...], 1, 1)
+        if k % 2:
+            send_ref[(k // 2) * rows:(k // 2 + 1) * rows] = back.astype(bf16)
+        else:
+            (far_ref if k else keep_ref)[...] = back
+    gq_s[...] = contract(nrm_ref[...], dqkv_s[...], 0, 0)
+    if in_kernel(count, width):
+        chunk_qkv(rank, me, count, gq_s, go_s, gkeep_ref, gsend_ref)
+    else:
+        gkeep_ref[...] = gq_s[...]
+        gsend_ref[...] = go_s[...]
+
+
+def chunk_qkv(rank, me, count, gq_s, go_s, keep_ref, gsend_ref):
+    part = go_s.shape[0]
+    rows, third = part // count, part // count // 3
+    wide = gq_s.shape[1]
+    for p in range(count):
+        target, place = (keep_ref, p) if p < count // 2 else (gsend_ref, p - count // 2)
+        nat = chunk_at(rank, me, count, p)
+        for k in range(4):
+            at = pl.ds(pl.multiple_of((rank ^ k) * part + nat * rows, 8), rows)
+            target[place, k * rows:(k + 1) * rows] = gq_s[at].astype(target.dtype)
+        out = go_s[at_rows(nat, rows)]
+        target[place, 4 * rows:5 * rows] = out[:, 0:wide].astype(target.dtype)
+        tail = out[:, wide:]
+        packed = jnp.concatenate([tail[i * third:(i + 1) * third] for i in range(3)], 1)
+        target[place, 5 * rows:5 * rows + third] = packed.astype(target.dtype)
+        target[place, 5 * rows + third:] = jnp.zeros((target.shape[1] - 5 * rows - third, wide), target.dtype)
+
+
+def small_body(rank_ref, send_ref, keep_ref, far_ref, unit_ref, inv_ref, ids_ref, par_ref, smid_ref, smid2_ref, upb_ref,
+               sm_ref, sm_s):
+    rank = rank_ref[0]
     rows, width = keep_ref.shape
     part = width // 4
     gain = par_ref[5:6]
@@ -336,17 +377,12 @@
     bias_sum = jnp.zeros((1, width), f32)
     for k in range(4):
         at = at_rows(rank ^ k, rows)
-        back = contract(dqkv_s[at], wq_ref[...], 1, 1)
-        if k % 2:
-            send_ref[(k // 2) * rows:(k // 2 + 1) * rows] = back.astype(bf16)
-        else:
-            (far_ref if k else keep_ref)[...] = back
+        back = send_ref[(k // 2) * rows:(k // 2 + 1) * rows].astype(f32) if k % 2 else (far_ref if k else keep_ref)[...]
         unit = unit_ref[at].astype(f32)
         gain_sum = gain_sum + jnp.sum(back * unit, 0, keepdims=True)
         bias_sum = bias_sum + jnp.sum(back, 0, keepdims=True)
         one = (lax.broadcasted_iota(jnp.int32, (8, rows), 0).astype(f32) == ids_ref[k:k + 1]).astype(bf16)
         by_pass = by_pass + contract(one, norm_back(back, unit, inv_ref[at], gain).astype(bf16), 1, 0)
-    gq_s[...] = contract(nrm_ref[...], dqkv_s[...], 0, 0)
     full = jnp.concatenate([by_pass[0:5], gain_sum, bias_sum, smid[8:12],
                             jnp.zeros((5, width), f32)], 0)
     up_b = upb_ref[0:1]
@@ -356,46 +392,51 @@
         for i in range(4):
             sm = jnp.where((mine == 11 + i) & (rank == j), up_b[:, i * part:(i + 1) * part], sm)
         sm_s[j] = sm
-    if in_kernel(count, width):
-        chunk_qkv(rank, me, count, gq_s, go_s, sm_s, gkeep_ref, gsend_ref)
-        sm_ref[...] = jnp.zeros(sm_ref.shape, f32)
-    else:
-        gkeep_ref[...] = gq_s[...]
-        gsend_ref[...] = go_s[...]
-        for k in range(4):
-            sm_ref[k] = sm_s[rank ^ k]
-
-
-def chunk_qkv(rank, me, count, gq_s, go_s, sm_s, keep_ref, gsend_ref):
-    part = go_s.shape[0]
-    rows = part // count
-    small = 16 // count
-    wide = gq_s.shape[1]
-    step = rows + small
-
-    def store(target, p, nat, place):
-        for k in range(4):
-            at = pl.ds(pl.multiple_of((rank ^ k) * part + nat * rows, 8), rows)
-            target[place, k * step:k * step + rows] = gq_s[at].astype(target.dtype)
-        out = go_s[at_rows(nat, rows)]
-        third = rows // 3
-        target[place, 4 * step:4 * step + rows] = out[:, 0:wide].astype(target.dtype)
-        tail = out[:, wide:]
-        packed = jnp.concatenate([tail[i * third:(i + 1) * third] for i in range(3)], 1)
-        target[place, 4 * step + rows:4 * step + rows + third] = packed.astype(target.dtype)
-
+    for k in range(4):
+        sm_ref[k, :, 0:part] = sm_s[rank ^ k].astype(bf16)
+        sm_ref[k, :, part:] = jnp.zeros((16, sm_ref.shape[2] - part), bf16)
+
+
+def cut_qkv_body(keep_ref, got_ref, sm_ref, low_ref, n1, n2, n3):
+    total = keep_ref[0].astype(f32) + got_ref[0].astype(f32)
+    low_ref[...] = total.astype(bf16)
+    rows = n1.shape[0] - 16
+    for k, ref in ((1, n1), (2, n2), (3, n3)):
+        ref[0:rows] = total[k * rows:(k + 1) * rows].astype(bf16)
+        ref[rows:] = sm_ref[k]
+
+
+def split_qkv_body(keep_ref, got_ref, kept_ref, send_ref):
+    half = kept_ref.shape[0]
+    for p in range(half):
+        kept_ref[p] = (keep_ref[p].astype(f32) + got_ref[p].astype(f32)).astype(bf16)
+        send_ref[p] = (keep_ref[half + p].astype(f32) + got_ref[half + p].astype(f32)).astype(bf16)
+
+
+def grow_feed_body(a_ref, b_ref, out_ref):
+    count = a_ref.shape[0]
     for p in range(count):
-        target, place = (keep_ref, p) if p < count // 2 else (gsend_ref, p - count // 2)
-        nat = chunk_at(rank, me, count, p)
-        store(target, p, nat, place)
-        for k in range(4):
-            sm = sm_s[rank ^ k]
-            row = jnp.zeros((small, part), f32)
-            for c in range(count):
-                row = jnp.where(nat == c, sm[c * small:(c + 1) * small], row)
-            target[place, k * step + rows:k * step + rows + small, 0:part] = row.astype(target.dtype)
-            target[place, k * step + rows:k * step + rows + small, part:] = jnp.zeros(
-                (small, wide - part), target.dtype)
+        out_ref[p] = a_ref[p]
+        out_ref[count + p] = b_ref[p]
+
+
+def join_qkv_body(low_ref, sm_ref, b1, b2, b3, out_ref):
+    rows = b1.shape[0] - 16
+    pieces = low_ref.shape[0]
+    total = sm_ref[0].astype(f32)
+    out_ref[0:rows] = low_ref[0:rows]
+    for k, b in ((1, b1), (2, b2), (3, b3)):
+        out_ref[k * rows:(k + 1) * rows] = b[0:rows]
+        total = total + b[rows:].astype(f32)
+    out_ref[4 * rows:pieces] = low_ref[4 * rows:]
+    out_ref[pieces:] = total.astype(bf16)
+
+
+def grow_qkv_body(a_ref, b_ref, out_ref):
+    n = a_ref.shape[0] - 16
+    out_ref[0:n] = a_ref[0:n]
+    out_ref[n:2 * n] = b_ref[0:n]
+    out_ref[2 * n:] = (a_ref[n:].astype(f32) + b_ref[n:].astype(f32)).astype(bf16)
 
 
 def last_body(sin_ref, par_ref, grad_a, grad_b, keep_ref, recv_ref, yrecv_ref, tok_ref):
@@ -416,57 +457,35 @@
         up_ref[:, pl.ds(pl.multiple_of((rank ^ k) * hidden, hidden), hidden)] = g_ref[0, lo:lo + up_rows].astype(f32)
 
 
-def place_qkv_body(count, start, rank_ref, g_ref, *refs):
-    rank, me = rank_ref[0], rank_ref[1]
-    if start:
-        sm_in, _, _, qkv_ref, out_ref = refs[:5]
-        small_refs, stage_s, sm_s = refs[5:-2], refs[-2], refs[-1]
+def place_qkv_body(ends, rank_ref, g_ref, *refs):
+    rank = rank_ref[0]
+    if ends:
+        sm_a, sm_b, _, _, qkv_ref, out_ref = refs[:6]
+        small_refs, stage_s = refs[6:-1], refs[-1]
     else:
-        qkv_ref, out_ref, sm_s, stage_s = refs
-    step = pl.program_id(0)
+        qkv_ref, out_ref, stage_s = refs
     rows, third = out_ref.shape[0], out_ref.shape[0] // 3
     width = out_ref.shape[1]
     part = width // 4
-    wide = g_ref.shape[2]
-    small = 16 // count
-    if start:
-        @pl.when(step == 0)
-        def _():
-            sm_s[...] = sm_in[...]
-    stage_s[...] = g_ref[0, 0:4 * rows].astype(f32)
+    wide = g_ref.shape[1]
+    stage_s[...] = g_ref[0:4 * rows].astype(f32)
     for j in range(4):
         block = stage_s[at_rows(rank ^ j, rows)]
         for i in range(3):
             qkv_ref[:, i * width + j * part:i * width + (j + 1) * part] = block[:, i * part:(i + 1) * part]
-    sm_s[chunk_at(rank, me, count, step + start)] = g_ref[0, 4 * rows:4 * rows + small, 0:part].astype(f32)
-    lo = 4 * rows + small
-    out_ref[:, 0:wide] = g_ref[0, lo:lo + rows].astype(f32)
-    packed = g_ref[0, lo + rows:lo + rows + third].astype(f32)
+    out_ref[:, 0:wide] = g_ref[4 * rows:5 * rows].astype(f32)
+    packed = g_ref[5 * rows:5 * rows + third].astype(f32)
     out_ref[:, wide:] = jnp.concatenate([packed[:, i * part:(i + 1) * part] for i in range(3)], 0)
-    if start:
-        @pl.when(step == pl.num_programs(0) - 1)
+    if ends:
+        @pl.when(pl.program_id(0) == 0)
         def _():
-            rows_of = [sm_s[i // small, i % small:i % small + 1] for i in range(16)]
+            total = (sm_a[...].astype(f32) + sm_b[...].astype(f32))[:, 0:part]
             table_ref = small_refs[0]
-            for i in range(table_ref.shape[0]):
-                table_ref[i:i + 1] = rows_of[i]
+            table_ref[...] = total[0:table_ref.shape[0]]
             for ref, i in zip(small_refs[1:7], (5, 6, 9, 7, 8, 10)):
-                ref[...] = rows_of[i].reshape(part)
+                ref[...] = total[i:i + 1].reshape(part)
             for i in range(4):
-                small_refs[7][i * part:(i + 1) * part] = rows_of[11 + i].reshape(part)
-
-
-def join_qkv_body(low_ref, b1, b2, b3, out_ref):
-    step = b1.shape[0]
-    small = (low_ref.shape[0] - out_ref.shape[0]) // 3
-    rows = step - small
-    total = low_ref[rows:step].astype(f32)
-    out_ref[0:rows] = low_ref[0:rows]
-    for k, b in enumerate((b1, b2, b3)):
-        out_ref[(k + 1) * rows:(k + 2) * rows] = b[0:rows]
-        total = total + b[rows:step].astype(f32)
-    out_ref[4 * rows:4 * rows + small] = total.astype(bf16)
-    out_ref[4 * rows + small:] = low_ref[4 * step:]
+                small_refs[7][i * part:(i + 1) * part] = total[11 + i:12 + i].reshape(part)
 
 
 def qkv_blocks_body(rank_ref, w_ref, own_ref, near_ref, far_ref, stage_s):
@@ -509,10 +528,13 @@
     return block, by_core(block), far, by_core(far)
 
 
-def scatter_sum(send, keep, far, rows):
-    recv = by_core(send)
-    half = rows // 2
-    onward = [(far[i:i + half] + recv[rows + i:rows + i + half].astype(f32)).astype(bf16) for i in (0, half)]
+def scatter_sum(near, both, keep, far, *first):
+    recv_far = by_core(both)
+    recv = by_core(near)
+    if first:
+        recv_far = after(recv_far, *first)
+    half = far.shape[0] // 2
+    onward = [(far[i:i + half] + recv_far[i:i + half].astype(f32)).astype(bf16) for i in (0, half)]
     return keep, recv, [by_row(o) for o in onward], onward
 
 
@@ -576,7 +598,7 @@
     smem = pl.BlockSpec(memory_space=pltpu.SMEM)
     vmem = pl.BlockSpec(memory_space=pltpu.VMEM)
 
-    def call(body, micros, outs, scratch, *args, ranked=True, aliases=None, wide=False):
+    def call(body, micros, outs, scratch, *args, ranked=True, aliases=None, wide=False, limit=8):
         specs = [smem] * ranked + [vmem] * (len(args) - ranked)
         return pl.pallas_call(
             body,
@@ -585,9 +607,12 @@
             out_specs=[vmem] * len(outs),
             scratch_shapes=[pltpu.VMEM(s, d) for s, d in scratch],
             input_output_aliases=aliases or {},
-            compiler_params=pltpu.CompilerParams(vmem_limit_bytes=None if wide else 8 * 2**20),
+            compiler_params=pltpu.CompilerParams(vmem_limit_bytes=None if wide else limit * 2**20),
             cost_estimate=pl.CostEstimate(flops=int(micros * 1.1e9), bytes_accessed=0, transcendentals=0),
         )(*args)
+
+    ur = part // replicas
+    pieces = 5 * ur + ur // 3 + 8 * packed
 
     def placed(body, values, start, shapes, blocks_of, extra, scratch, aliases, *first):
         def at_chunk(p, s):
@@ -601,8 +626,10 @@
             out_shape=[jax.ShapeDtypeStruct(s, f32) for s in shapes],
             grid_spec=pltpu.PrefetchScalarGridSpec(
                 num_scalar_prefetch=1, grid=(replicas // 2,),
-                in_specs=[pl.BlockSpec((1,) + values.shape[1:], lambda p, s: (p, 0, 0))]
-                + [whole(e.shape) if e.ndim == 3 else pl.BlockSpec(memory_space=pl.ANY) for e in extra],
+                in_specs=[pl.BlockSpec((1,) + values.shape[1:], lambda p, s: (p, 0, 0)) if values.ndim == 3
+                          else pl.BlockSpec((pieces, values.shape[1]), lambda p, s: (p, 0))]
+                + [pl.BlockSpec((16, e.shape[1]), lambda p, s, at=e.shape[0] // 16 - 1: (at, 0))
+                   if e.dtype == bf16 else pl.BlockSpec(memory_space=pl.ANY) for e in extra],
                 out_specs=[pl.BlockSpec(b, at_chunk) if b else whole(s) for s, b in zip(shapes, blocks_of)],
                 scratch_shapes=[pltpu.VMEM(s, f32) for s in scratch]),
             input_output_aliases=aliases,
@@ -636,14 +663,16 @@
 
     heads = part // HD
     half_f, half_b, row_f, row_b = ((2 * rows, width), f32), ((2 * rows, width), bf16), ((rows, width), f32), ((rows, width), bf16)
-    send, keep, far, qkv, ctx, lse, wq_full = call(
-        front_body, 4,
-        [half_b, row_f, row_f, ((seq, 3 * part), bf16), ((seq, part), bf16), ((8, seq), f32), ((width, 3 * part), bf16)],
-        [((seq, 128), f32), ((3 * heads, seq, HD), bf16), ((heads, seq, HD), bf16), ((heads, seq, 1), f32)],
-        place, segc, segr, nrm, *wq, out_weight)
+    near, both, keep, far, qkv, ctx, lse, wq_full = call(
+        front_body, 0,
+        [row_b, row_b, row_f, row_f, ((seq, 3 * part), bf16), ((seq, part), bf16), ((8, seq), f32),
+         ((width, 3 * part), bf16)],
+        [((seq, 128), f32), ((3 * heads, seq, HD), bf16), ((heads, seq, HD), bf16), ((heads, seq, 1), f32),
+         ((seq, seq), f32)],
+        place, segc, segr, nrm, *wq, out_weight, limit=20)
     half = rows // 2
     hrow_f, hrow_b = ((half, width), f32), ((half, width), bf16)
-    keep, recv, (first, second), _ = scatter_sum(after(send, far_u), keep, far, rows)
+    keep, recv, (first, second), _ = scatter_sum(near, both, keep, far, far_u)
     def middle(start, part_far):
         return call(functools.partial(mid_body, start), 1, [hrow_f, hrow_b], [], sin, par, keep, recv, part_far,
                     ranked=False)
@@ -653,11 +682,11 @@
     mid_b, nrm_b = middle(half, after(second, pair_u, near_a))
     mids = mid_a, mid_b
     n2 = gather_halves(nrm_a, nrm_b, near_a)
-    send, keep, far, act, pg = call(
-        feed_body, 5, [half_b, row_f, row_f, ((seq, hidden), bf16), ((seq, hidden), bf16)],
+    near, both, keep, far, act, pg = call(
+        feed_body, 5, [row_b, row_b, row_f, row_f, ((seq, hidden), bf16), ((seq, hidden), bf16)],
         [((width, hidden), bf16)],
         place, *n2, cotangent, *group, own_u, pair_u, up_bias, down_weight)
-    keep, recv, fars, onward = scatter_sum(send, keep, far, rows)
+    keep, recv, fars, onward = scatter_sum(near, both, keep, far)
     feed_rows = hidden // replicas + 4 * (part // replicas)
     if packed:
         grads = [((replicas // 2, feed_rows, width), bf16)] * 2
@@ -688,39 +717,30 @@
         gkeep, gsend = split_step(gkeep, got)
         got = plane_swap(gsend, replicas, phase)
 
-    small = max(16, replicas)
-    step = part // replicas + small // replicas
-    qkv_rows = 4 * step + part // replicas + part // replicas // 3
     if packed:
-        grads = [((replicas // 2, qkv_rows, 3 * part), bf16)] * 2
+        grads = [((replicas // 2, pieces, 3 * part), bf16)] * 2
     else:
         grads = [((width, 3 * part), f32), ((part, width), f32)]
     dctx, delta, grad_out, dqkv = call(
         functools.partial(attn_back_one_body, range(heads)), 9,
         [((seq, part), bf16), ((8, seq), f32), ((part, width), f32), ((seq, 3 * part), bf16)],
-        [((seq, 128), f32), ((seq, HD), f32)],
-        place, segc, segr, *branches, qkv, ctx, lse, out_weight)
+        [((seq, 128), f32), ((seq, HD), f32), ((seq, seq), f32)],
+        place, segc, segr, *branches, qkv, ctx, lse, out_weight, limit=20)
     if phases > 1:
         gkeep, gsend = split_step(gkeep, after(got, delta))
         got = plane_swap(gsend, replicas, phases - 1)
-    send, keep, far, qkeep, qsend, smalls = call(
-        functools.partial(attn_back_two_body, replicas), 5,
-        [half_b, row_f, row_f] + grads + [((4, 16, part), f32)],
-        [((width, 3 * part), f32), ((4, 16, part), f32)],
-        after(place, gsend), dqkv, grad_out, nrm_late, unit, inv, ids, par, *smalls_mid, up_b,
-        wq_full)
+    send, keep, far, qkeep, qsend = call(
+        functools.partial(attn_back_two_body, replicas), 3, [half_b, row_f, row_f] + grads, [((width, 3 * part), f32)],
+        after(place, gsend), dqkv, grad_out, nrm_late, wq_full)
     if not packed:
         qs = qkeep.reshape(4, replicas, -1, 3 * part)[rank ^ jnp.arange(4)][:, nat].transpose(1, 0, 2, 3)
-        sm = jnp.pad(smalls, ((0, 0), (0, small - 16), (0, 2 * part)))
-        sm = sm.reshape(4, replicas, -1, 3 * part)[:, nat].transpose(1, 0, 2, 3)
         os = qsend.reshape(replicas, -1, width)[nat]
         both = jnp.concatenate([
-            jnp.concatenate([qs, sm], 2).reshape(replicas, -1, 3 * part), os[:, :, :3 * part],
-            os[:, :, 3 * part:].reshape(replicas, -1, 3 * part)], 1)
+            qs.reshape(replicas, -1, 3 * part), os[:, :, :3 * part], os[:, :, 3 * part:].reshape(replicas, -1, 3 * part)], 1)
         both = both.astype(bf16)
         qkeep, qsend = both[:replicas // 2], both[replicas // 2:]
     qgot = plane_swap(qsend, replicas, 0)
-    lo, ur = hidden // replicas, part // replicas
+    lo = hidden // replicas
 
     last_phase = phases - 1
     now = {"turn": qkeep, "feed": got, "qkv": qgot}
@@ -740,36 +760,57 @@
         now["turn"] = now["feed_all"]
 
     def feed_join(phase):
-        now["feed_all"] = jnp.concatenate([now["feed_all"], after(now["feed"], now["turn"])], 0)
+        held, got = now["feed_all"], after(now["feed"], now["turn"])
+        now["feed_all"], = call(grow_feed_body, 4, [((2 * held.shape[0],) + held.shape[1:], bf16)], [], held, got,
+                                ranked=False)
         now["feed"] = plane_swap(now["feed_all"], replicas, phase)
         now["turn"] = now["feed_all"]
 
     def qkv_split(phase):
-        now["qkeep"], qsend = split_step(now.get("qkeep", qkeep), after(now["qkv"], now["turn"]))
+        kept, got = now.get("qkeep", qkeep), after(now["qkv"], now["turn"])
+        shape = (kept.shape[0] // 2,) + kept.shape[1:]
+        now["qkeep"], qsend = call(split_qkv_body, 0, [(shape, bf16)] * 2, [], kept, got, ranked=False)
         now["qkv"] = plane_swap(qsend, replicas, phase)
         now["turn"] = qsend
 
+    def small_sums():
+        now["small"], = call(
+            small_body, 0, [((4, 16, 3 * part), bf16)], [((4, 16, part), f32)], after(place, now["turn"]), send, keep, far,
+            unit, inv, ids, par, *smalls_mid, up_b)
+        now["turn"] = now["small"]
+
     def qkv_swap():
-        low = (now.get("qkeep", qkeep).astype(f32) + after(now["qkv"], now["turn"]).astype(f32))[0].astype(bf16)
-        now["quads"] = swap_piece(lambda k: low[k * step:(k + 1) * step])
+        kept, got = now.get("qkeep", qkeep), after(now["qkv"], now["turn"])
+        if packed:
+            low, *cuts = call(cut_qkv_body, 1, [((pieces, 3 * part), bf16)] + [((ur + 16, 3 * part), bf16)] * 3, [],
+                              kept, got, now["small"], ranked=False)
+        else:
+            low = (kept.astype(f32) + got.astype(f32))[0].astype(bf16)
+            cuts = [jnp.concatenate([low[k * ur:(k + 1) * ur], now["small"][k]], 0) for k in (1, 2, 3)]
+        now["quads"] = swap_piece(lambda k: cuts[k - 1])
         now["low"], now["turn"] = low, now["quads"][0]
 
     def qkv_first():
-        low = now["low"]
+        low, small = now["low"], now["small"]
         quads = [after(s, now["turn"]) for s in now["quads"]]
         if packed:
-            joined, = call(join_qkv_body, 0, [((qkv_rows - 3 * (small // replicas), 3 * part), bf16)], [], low, *quads,
-                           ranked=False)
+            now["qkv_all"], = call(join_qkv_body, 1, [((pieces + 16, 3 * part), bf16)], [], low, small, *quads,
+                                   ranked=False)
         else:
-            quads = [low[:step]] + quads
-            own_small = sum(q[ur:].astype(f32) for q in quads).astype(bf16)
-            joined = jnp.concatenate([q[:ur] for q in quads] + [own_small, low[4 * step:]], 0)
-        now["qkv_all"] = joined[None]
+            total = small[0].astype(f32) + sum(q[ur:].astype(f32) for q in quads)
+            now["qkv_all"] = jnp.concatenate(
+                [low[:ur]] + [q[:ur] for q in quads] + [low[4 * ur:], total.astype(bf16)], 0)
         now["qkv"] = plane_swap(now["qkv_all"], replicas, last_phase)
         now["turn"] = now["qkv_all"]
 
     def qkv_join(phase):
-        now["qkv_all"] = jnp.concatenate([now["qkv_all"], after(now["qkv"], now["turn"])], 0)
+        held, got = now["qkv_all"], after(now["qkv"], now["turn"])
+        if packed:
+            now["qkv_all"], = call(grow_qkv_body, 1, [((2 * held.shape[0] - 16, 3 * part), bf16)], [], held, got,
+                                   ranked=False)
+        else:
+            total = held[-16:].astype(f32) + got[-16:].astype(f32)
+            now["qkv_all"] = jnp.concatenate([held[:-16], got[:-16], total.astype(bf16)], 0)
         now["qkv"] = plane_swap(now["qkv_all"], replicas, phase)
         now["turn"] = now["qkv_all"]
 
@@ -806,17 +847,16 @@
     def qkv_place():
         if packed:
             now["qfilled"] = placed(
-                functools.partial(place_qkv_body, replicas, 0), now["qkv_all"], 0,
-                qkv_shapes[0] + [sm_shape], qkv_shapes[1] + [None], [], [stage], {}, now["turn"])
+                functools.partial(place_qkv_body, False), now["qkv_all"], 0, *qkv_shapes, [], [stage], {}, now["turn"])
             now["turn"] = now["qfilled"][0]
 
     feed_shapes = [(hidden, width), (part, 4 * hidden)], [(lo, width), (ur, 4 * hidden)]
     qkv_shapes = [(part, 12 * part), (part, width)], [(ur, 12 * part), (ur, width)]
-    stage, sm_shape = (4 * ur, 3 * part), (replicas, 16 // replicas, part)
+    stage = 4 * ur, 3 * part
     feed_joins = [functools.partial(feed_join, p) for p in reversed(range(last_phase))]
     qkv_joins = [functools.partial(qkv_join, p) for p in reversed(range(last_phase))]
     splits = [functools.partial(qkv_split, p) for p in range(1, phases)]
-    for run in ([feed_swap, tokens_onward, out_start, feed_first] + splits[:1] + [tokens_end] + splits[1:]
+    for run in ([feed_swap] + splits[:1] + [tokens_onward, feed_first, out_start, small_sums, tokens_end] + splits[1:]
                 + feed_joins[:-1] + [qkv_swap, out_onward, qkv_first] + feed_joins[-1:] + [feed_place]
                 + qkv_joins + [out_end, qkv_place]):
         run()
@@ -830,21 +870,20 @@
         shapes, split = qkv_shapes
         vectors = [pass_table.T.shape] + [(part,)] * 6 + [(hidden,)]
         final_qkv, final_out, table, g1, b1, ob, g2, b2, db, ub = placed(
-            functools.partial(place_qkv_body, replicas, replicas // 2), after(qgot, final_down), replicas // 2, shapes + vectors,
-            split + [None] * 8, [filled[2], filled[0], filled[1]], [stage, sm_shape], {3: 0, 4: 1})
+            functools.partial(place_qkv_body, True), after(qgot, final_down), replicas // 2, shapes + vectors,
+            split + [None] * 8, [qkv_all, qgot, *filled], [stage], {4: 0, 5: 1})
     else:
         back_at = jnp.argsort(nat)
         feed_all = jnp.concatenate([feed_all, got], 0)[back_at].astype(f32)
-        qkv_all = jnp.concatenate([qkv_all, qgot], 0)[back_at].astype(f32)
+        mine = (qkv_all[-16:].astype(f32) + qgot[-16:].astype(f32))[:, :part]
+        qkv_all = jnp.concatenate([qkv_all[:-16], qgot[:-16]], 0).reshape(replicas, pieces, -1)[back_at].astype(f32)
         final_down = feed_all[:, :lo].reshape(hidden, width)
         final_up = feed_all[:, lo:].reshape(replicas, 4, ur, hidden)[:, rank ^ jnp.arange(4)]
         final_up = final_up.transpose(0, 2, 1, 3).reshape(part, 4 * hidden)
         final_qkv = qkv_all[:, :4 * ur].reshape(replicas, 4, ur, 3, part)[:, rank ^ jnp.arange(4)]
         final_qkv = final_qkv.transpose(0, 2, 3, 1, 4).reshape(part, 12 * part)
-        hi = 4 * ur + small // replicas
-        mine = qkv_all[:, 4 * ur:hi, :part].reshape(small, part)
         final_out = jnp.concatenate(
-            [qkv_all[:, hi:hi + ur].reshape(part, 3 * part), qkv_all[:, hi + ur:].reshape(part, part)], 1)
+            [qkv_all[:, 4 * ur:5 * ur].reshape(part, 3 * part), qkv_all[:, 5 * ur:].reshape(part, part)], 1)
         table, g1, b1, ob, g2, b2, db = mine[0:5], mine[5], mine[6], mine[9], mine[7], mine[8], mine[10]
         ub = mine[11:15].reshape(hidden)
     return (output, tokens_grad, table.T, g1, b1, final_qkv, final_out, ob, g2, b2, final_up, ub, final_down, db)

time: 194 us -> 192 us (0.990)
  waiting for transfers between devices: 102 us -> 94.1 us
  starting transfers between devices: 33.3 us -> 39.7 us
    ppermute x15, waiting for transfers between devices: 46.9 us -> 42.8 us  [by_row(): return lax.ppermute(value, 'shard', ROWY)]
    ppermute x20 -> x22, starting transfers between devices: 2.89 us -> 6.34 us  [by_core(): return lax.ppermute(value, 'shard', CORE)]
    ppermute x20 -> x22, waiting for transfers between devices: 7.37 us -> 4.16 us  [by_core(): return lax.ppermute(value, 'shard', CORE)]
    ppermute x12, starting transfers between devices: 10.8 us -> 13.7 us  [plane_swap(): return lax.ppermute(value, ('replica', 'shard'), plane_pairs(count, phase))]
    pallas_call x16 -> x24, Pallas kernels: 44.2 us -> 43.3 us  [call(): pl.pallas_call(body, out_shape=[jax.ShapeDtypeStruct(s, d) for s, d in ou...]
  transfers between devices with their start and end apart: 50 -> 52, of which waited for: 29 -> 26; matrix products, arithmetic and copies ran while one was open for 1% -> 1% of each run, Pallas kernels for 23% -> 23%
where the time goes in v2:
time: 192 us
  waiting for transfers between devices  94.1 us (49%)
  Pallas kernels  53.3 us (28%)
  starting transfers between devices  39.7 us (21%)
  other arithmetic  1.92 us (1%)
    pallas_call x24, Pallas kernels, call(): pl.pallas_call(body, out_shape=[jax.ShapeDtypeStruct(s, d) for s, d in ou...  43.3 us
    ppermute x12, waiting for transfers between devices, plane_swap(): return lax.ppermute(value, ('replica', 'shard'), plane_pairs(count, phase))  42.9 us
    ppermute x15, waiting for transfers between devices, by_row(): return lax.ppermute(value, 'shard', ROWY)  42.8 us
    ppermute x15, starting transfers between devices, by_row(): return lax.ppermute(value, 'shard', ROWY)  15.7 us
    ppermute x12, starting transfers between devices, plane_swap(): return lax.ppermute(value, ('replica', 'shard'), plane_pairs(count, phase))  13.7 us
    pallas_call x4, Pallas kernels, placed(): pl.pallas_call(body, out_shape=[jax.ShapeDtypeStruct(s, f32) for s in sha...  10 us
    ppermute x22, starting transfers between devices, by_core(): return lax.ppermute(value, 'shard', CORE)  6.34 us
    ppermute x22, waiting for transfers between devices, by_core(): return lax.ppermute(value, 'shard', CORE)  4.16 us
  transfers between devices with their start and end apart: 52, of which 26 were waited for; matrix products, arithmetic and copies ran while one was open for 1% of the time, Pallas kernels for 23%

profile of v2, /device:TPU:0, one launch (start us, length us, event | category | flops | bytes accessed | tf_op | source)
XLA Modules:
  0.0 191.5 jit_solution(4551190833045740617)
XLA Ops:
  2.7 3.0 %collective-permute-start.1 = (bf16[272,768]{1,0:T(8,128)(2,1)}, bf16[272,768]{1,0:T(8,128)(2,1)}, u32[]{:S(2)}, u32[]{:S(2)}) collective-permute-start(bf16[272,768]{1,0:T(8,128)(2,1)} %shard_map.263.x0), channel_id=1, source_target_pairs={{0,2},{1,3},{2,0},{3,1},{4,6},{5,7},{6,4},{7,5},{8,10},{9,11},{10,... | collective-permute-start | bytes 1253384 | tf_op jit(solution)/shard_map/ppermute | solution.py:523
  8.4 8.1 %collective-permute-done.1.x2 = bf16[272,768]{1,0:T(8,128)(2,1)} collective-permute-done((bf16[272,768]{1,0:T(8,128)(2,1)}, bf16[272,768]{1,0:T(8,128)(2,1)}, u32[]{:S(2)}, u32[]{:S(2)}) %collective-permute-start.1) | collective-permute-done | bytes 417824 | tf_op jit(solution)/shard_map/ppermute | solution.py:523
  18.8 2.5 %shard_map.266 = (f32[1024,1]{1,0:T(8,128)S(1)}, f32[8,1024]{1,0:T(8,128)S(1)}, f32[256,768]{1,0:T(8,128)S(1)}, f32[16,768]{1,0:T(8,128)S(1)}, bf16[1024,768]{1,...) custom-call(s32[3]{0:T(128)S(1)} %pad_add_fusion.rank_ref, ...), custom_call_target="tpu_custom_call" | custom-call | tf_op jit(solution)/shard_map/pallas_call | solution.py:603
  21.3 5.6 %collective-permute-done.4.w2 = bf16[384,576]{1,0:T(8,128)(2,1)S(1)} collective-permute-done((bf16[384,576]{1,0:T(8,128)(2,1)S(1)}, bf16[384,576]{1,0:T(8,128)(2,1)S(1)}, u32[]{:S(2)}, u32[]{:S(2)}) %collective-permute-start.4) | collective-permute-done | bytes 442400 | tf_op jit(solution)/shard_map/ppermute | solution.py:523
  28.5 8.4 %shard_map.267 = (bf16[256,768]{1,0:T(8,128)(2,1)S(1)}, bf16[256,768]{1,0:T(8,128)(2,1)S(1)}, f32[256,768]{1,0:T(8,128)S(1)}, f32[256,768]{1,0:T(8,128)S(1)}, bf...) custom-call(s32[3]{0:T(128)S(1)} %pad_add_fusion.rank_ref, ...), custom_call_target="tpu_custom_call" | custom-call | tf_op jit(solution)/shard_map/pallas_call | solution.py:603
  37.5 3.4 %collective-permute-done.8.g2 = bf16[448,768]{1,0:T(8,128)(2,1)S(1)} collective-permute-done((bf16[448,768]{1,0:T(8,128)(2,1)S(1)}, bf16[448,768]{1,0:T(8,128)(2,1)S(1)}, u32[]{:S(2)}, u32[]{:S(2)}) %collective-permute-start.8) | collective-permute-done | bytes 688160 | tf_op jit(solution)/shard_map/ppermute | solution.py:523
  44.7 4.1 %collective-permute-done.9.yrecv_ref = bf16[128,768]{1,0:T(8,128)(2,1)S(1)} collective-permute-done((bf16[128,768]{1,0:T(8,128)(2,1)S(1)}, bf16[128,768]{1,0:T(8,128)(2,1)S(1)}, u32[]{:S(2)}, u32[]{:S(2)}) %collective-permute-start.9) | collective-permute-done | bytes 196640 | tf_op jit(solution)/shard_map/ppermute | solution.py:523
  49.8 2.2 %collective-permute-done.11.pair_ref = bf16[192,768]{1,0:T(8,128)(2,1)S(1)} collective-permute-done((bf16[192,768]{1,0:T(8,128)(2,1)S(1)}, bf16[192,768]{1,0:T(8,128)(2,1)S(1)}, u32[]{:S(2)}, u32[]{:S(2)}) %collective-permute-start.11) | collective-permute-done | bytes 294944 | tf_op jit(solution)/shard_map/ppermute | solution.py:661
  54.4 5.4 %collective-permute-done.14.n2 = bf16[128,768]{1,0:T(8,128)(2,1)S(1)} collective-permute-done((bf16[128,768]{1,0:T(8,128)(2,1)S(1)}, bf16[128,768]{1,0:T(8,128)(2,1)S(1)}, u32[]{:S(2)}, u32[]{:S(2)}) %collective-permute-start.14) | collective-permute-done | bytes 196640 | tf_op jit(solution)/shard_map/ppermute | solution.py:523
  59.8 3.4 %collective-permute-done.15.m2 = bf16[128,768]{1,0:T(8,128)(2,1)S(1)} collective-permute-done((bf16[128,768]{1,0:T(8,128)(2,1)S(1)}, bf16[128,768]{1,0:T(8,128)(2,1)S(1)}, u32[]{:S(2)}, u32[]{:S(2)}) %collective-permute-start.15) | collective-permute-done | bytes 196640 | tf_op jit(solution)/shard_map/ppermute | solution.py:523
  64.6 5.3 %shard_map.270 = (bf16[256,768]{1,0:T(8,128)(2,1)S(1)}, bf16[256,768]{1,0:T(8,128)(2,1)S(1)}, f32[256,768]{1,0:T(8,128)S(1)}, f32[256,768]{1,0:T(8,128)S(1)}, bf...) custom-call(s32[3]{0:T(128)S(1)} %pad_add_fusion.rank_ref, bf16[128,768]{1,0:T(8,128)(2,1)S(1)} %get-tuple-element.145.n0, ...), custom_call_target="tpu_custom_call" | custom-call | flops 5500000256 | tf_op jit(solution)/shard_map/pallas_call | solution.py:603
  73.9 3.8 %shard_map.271 = (f32[8,768]{1,0:T(8,128)S(1)}, bf16[4,192,768]{2,1,0:T(8,128)(2,1)S(1)}, bf16[4,192,768]{2,1,0:T(8,128)(2,1)S(1)}) custom-call(s32[3]{0:T(128)S(1)} %pad_add_fusion.rank_ref, bf16[128,768]{1,0:T(8,128)(2,1)S(1)} %get-tuple-element.145.n0, bf16[128,768]{1,0:T(8,128)(2,1)S(1)} %get-tuple-element.148.m0, ...), custom_call_target="tpu_custom_call" | custom-call | flops 8800000000 | tf_op jit(solution)/shard_map/pallas_call | solution.py:603
  80.6 3.2 %collective-permute-done.23.yrecv_ref = bf16[128,768]{1,0:T(8,128)(2,1)S(1)} collective-permute-done((bf16[128,768]{1,0:T(8,128)(2,1)S(1)}, bf16[128,768]{1,0:T(8,128)(2,1)S(1)}, u32[]{:S(2)}, u32[]{:S(2)}) %collective-permute-start.23) | collective-permute-done | bytes 196640 | tf_op jit(solution)/shard_map/ppermute | solution.py:523
  85.3 2.7 %collective-permute-done.30.f2 = bf16[128,768]{1,0:T(8,128)(2,1)S(1)} collective-permute-done((bf16[128,768]{1,0:T(8,128)(2,1)S(1)}, bf16[128,768]{1,0:T(8,128)(2,1)S(1)}, u32[]{:S(2)}, u32[]{:S(2)}) %collective-permute-start.30) | collective-permute-done | bytes 196640 | tf_op jit(solution)/shard_map/ppermute | solution.py:523
  88.0 3.4 %collective-permute-done.29.g2 = bf16[128,768]{1,0:T(8,128)(2,1)S(1)} collective-permute-done((bf16[128,768]{1,0:T(8,128)(2,1)S(1)}, bf16[128,768]{1,0:T(8,128)(2,1)S(1)}, u32[]{:S(2)}, u32[]{:S(2)}) %collective-permute-start.29) | collective-permute-done | bytes 196640 | tf_op jit(solution)/shard_map/ppermute | solution.py:523
  91.4 2.5 %collective-permute-done.21 = bf16[4,192,768]{2,1,0:T(8,128)(2,1)S(1)} collective-permute-done((bf16[4,192,768]{2,1,0:T(8,128)(2,1)S(1)}, bf16[4,192,768]{2,1,0:T(8,128)(2,1)S(1)}, u32[]{:S(2)}, u32[]{:S(2)}) %collective-permute-start.21) | collective-permute-done | bytes 1179680 | tf_op jit(solution)/shard_map/ppermute | solution.py:577
  95.9 8.3 %shard_map.274 = (bf16[1024,192]{1,0:T(8,128)(2,1)}, f32[8,1024]{1,0:T(8,128)}, f32[192,768]{1,0:T(8,128)S(1)}, bf16[1024,576]{1,0:T(8,128)(2,1)S(1)}) custom-call(s32[3]{0:T(128)S(1)} %pad_add_fusion.rank_ref, f32[1024,1]{1,0:T(8,128)S(1)} %get-tuple-element.131.segc_ref, f32[8,1024]{1,0:T(8,128)S(1)} %get-tuple-element.132.segr_ref, ...), custom_call_target="tpu_custom_call" | custom-call | flops 9900000256 | tf_op jit(solution)/shard_map/pallas_call | solution.py:603
  104.4 2.6 %collective-permute-start.26 = (bf16[1,192,768]{2,1,0:T(8,128)(2,1)S(1)}, bf16[1,192,768]{2,1,0:T(8,128)(2,1)S(1)}, u32[]{:S(2)}, u32[]{:S(2)}) collective-permute-start(bf16[1,192,768]{2,1,0:T(8,128)(2,1)S(1)} %slice.110), channel_id=1, source_target_pairs={{0,16},{1,17},{2,18},{3,19},{4,20},{5,21},{6,22},{7,23},{8,24},{9,... | collective-permute-start | bytes 884744 | tf_op jit(solution)/shard_map/ppermute | solution.py:577
  107.1 3.3 %shard_map.275 = (bf16[512,768]{1,0:T(8,128)(2,1)S(1)}, f32[256,768]{1,0:T(8,128)S(1)}, f32[256,768]{1,0:T(8,128)S(1)}, bf16[4,136,576]{2,1,0:T(8,128)(2,1)S(1)}, bf16[4,136,576]{2,1,0:T(8,128)(2,1)S(1)}) custom-call(s32[3]{0:T(128)S(1)} %pad_add_fusion.rank_ref, bf16[1024,576]{1,0:T(8,128)(2,1)S(1)} %get-tuple-element.168.dqkv_s, ...), custom_call_target="tpu_custom_call" | custom-call | flops 3300000000 | tf_op jit(solution)/shard_map/pallas_call | solution.py:603
  110.6 8.0 %collective-permute-done.26 = bf16[1,192,768]{2,1,0:T(8,128)(2,1)S(1)} collective-permute-done((bf16[1,192,768]{2,1,0:T(8,128)(2,1)S(1)}, bf16[1,192,768]{2,1,0:T(8,128)(2,1)S(1)}, u32[]{:S(2)}, u32[]{:S(2)}) %collective-permute-start.26) | collective-permute-done | bytes 294944 | tf_op jit(solution)/shard_map/ppermute | solution.py:577
  128.0 2.2 %collective-permute-start.38 = (bf16[512,768]{1,0:T(8,128)(2,1)S(1)}, bf16[512,768]{1,0:T(8,128)(2,1)S(1)}, u32[]{:S(2)}, u32[]{:S(2)}) collective-permute-start(bf16[512,768]{1,0:T(8,128)(2,1)S(1)} %get-tuple-element.185), channel_id=1, source_target_pairs={{0,1},{1,0},{2,3},{3,2},{4,5},{5,4},{6,7},{7,6},{8,9},{9,8},{10,11... | collective-permute-start | bytes 2359304 | tf_op jit(solution)/shard_map/ppermute | solution.py:519
  130.1 2.6 %shard_map.278.sm_ref = bf16[4,16,576]{2,1,0:T(8,128)(2,1)S(1)} custom-call(s32[3]{0:T(128)S(1)} %pad_add_fusion.rank_ref, bf16[512,768]{1,0:T(8,128)(2,1)S(1)} %get-tuple-element.175.send_ref, f32[256,768]{1,0:T(8,128)S(1)} %get-tuple-element.189.keep_ref, f32[256,768]{1,0:T(8,128)S(1)} %get-tuple-element.174.far_ref, ...), custom_call_target="tpu_custom_call" | custom-call | tf_op jit(solution)/shard_map/pallas_call | solution.py:603
  134.4 3.4 %collective-permute-start.41 = (bf16[1,136,576]{2,1,0:T(8,128)(2,1)S(1)}, bf16[1,136,576]{2,1,0:T(8,128)(2,1)S(1)}, u32[]{:S(2)}, u32[]{:S(2)}) collective-permute-start(bf16[1,136,576]{2,1,0:T(8,128)(2,1)S(1)} %get-tuple-element.199), channel_id=1, source_target_pairs={{0,16},{1,17},{2,18},{3,19},{4,20},{5,21},{6,22},{7,23},{8,24},{9,... | collective-permute-start | bytes 470024 | tf_op jit(solution)/shard_map/ppermute | solution.py:577
  137.8 2.0 %collective-permute-done.42.b_ref = bf16[1,192,768]{2,1,0:T(8,128)(2,1)S(1)} collective-permute-done((bf16[1,192,768]{2,1,0:T(8,128)(2,1)S(1)}, bf16[1,192,768]{2,1,0:T(8,128)(2,1)S(1)}, u32[]{:S(2)}, u32[]{:S(2)}) %collective-permute-start.42) | collective-permute-done | bytes 294944 | tf_op jit(solution)/shard_map/ppermute | solution.py:577
  140.3 7.1 %collective-permute-done.41.got_ref = bf16[1,136,576]{2,1,0:T(8,128)(2,1)S(1)} collective-permute-done((bf16[1,136,576]{2,1,0:T(8,128)(2,1)S(1)}, bf16[1,136,576]{2,1,0:T(8,128)(2,1)S(1)}, u32[]{:S(2)}, u32[]{:S(2)}) %collective-permute-start.41) | collective-permute-done | bytes 156704 | tf_op jit(solution)/shard_map/ppermute | solution.py:577
  155.8 2.5 %shard_map.285 = (f32[768,768]{1,0:T(8,128)}, f32[192,3072]{1,0:T(8,128)}) custom-call(s32[3]{0:T(128)S(1)} %pad_add_fusion.rank_ref, bf16[4,192,768]{2,1,0:T(8,128)(2,1)S(1)} %shard_map.284.g_ref), custom_call_target="tpu_custom_call" | custom-call | flops 2200000000 | tf_op jit(solution)/shard_map/pallas_call | solution.py:624
  158.3 7.4 %collective-permute-done.47.b_ref = bf16[152,576]{1,0:T(8,128)(2,1)S(1)} collective-permute-done((bf16[152,576]{1,0:T(8,128)(2,1)S(1)}, bf16[152,576]{1,0:T(8,128)(2,1)S(1)}, u32[]{:S(2)}, u32[]{:S(2)}) %collective-permute-start.47) | collective-permute-done | bytes 175136 | tf_op jit(solution)/shard_map/ppermute | solution.py:577
  167.3 10.1 %collective-permute-done.49.b_ref = bf16[288,576]{1,0:T(8,128)(2,1)S(1)} collective-permute-done((bf16[288,576]{1,0:T(8,128)(2,1)S(1)}, bf16[288,576]{1,0:T(8,128)(2,1)S(1)}, u32[]{:S(2)}, u32[]{:S(2)}) %collective-permute-start.49) | collective-permute-done | bytes 331808 | tf_op jit(solution)/shard_map/ppermute | solution.py:577
  179.2 2.4 %shard_map.288 = (f32[192,2304]{1,0:T(8,128)}, f32[192,768]{1,0:T(8,128)}) custom-call(s32[3]{0:T(128)S(1)} %pad_add_fusion.rank_ref, bf16[560,576]{1,0:T(8,128)(2,1)S(1)} %shard_map.287.g_ref.refs_0_), custom_call_target="tpu_custom_call" | custom-call | flops 2200000000 | tf_op jit(solution)/shard_map/pallas_call | solution.py:624
  181.6 2.5 %shard_map.289 = (f32[768,768]{1,0:T(8,128)}, f32[192,3072]{1,0:T(8,128)}) custom-call(s32[3]{0:T(128)S(1)} %pad_add_fusion.rank_ref, bf16[4,192,768]{2,1,0:T(8,128)(2,1)S(1)} %collective-permute-done.51.g_ref, f32[768,768]{1,0:T(8,128)} %get-tuple-element.212.refs_0_, ...), custom_call_target="tpu_custom_call", output_to_operand_aliasing={{0}: (2, {}), {1}: (3, {})} | custom-call | flops 2200000000 | tf_op jit(solution)/shard_map/pallas_call | solution.py:624
  184.1 4.6 %collective-permute-done.50.g_ref.refs_1_ = bf16[560,576]{1,0:T(8,128)(2,1)S(1)} collective-permute-done((bf16[560,576]{1,0:T(8,128)(2,1)S(1)}, bf16[560,576]{1,0:T(8,128)(2,1)S(1)}, u32[]{:S(2)}, u32[]{:S(2)}) %collective-permute-start.50) | collective-permute-done | bytes 645152 | tf_op jit(solution)/shard_map/ppermute | solution.py:577
  188.7 2.6 %shard_map.290 = (f32[192,2304]{1,0:T(8,128)}, f32[192,768]{1,0:T(8,128)}, f32[5,192]{1,0:T(8,128)}, f32[192]{0:T(256)}, f32[192]{0:T(256)}, /*index=5*/f32[192]...) custom-call(s32[3]{0:T(128)S(1)} %pad_add_fusion.rank_ref, ...), custom_call_target="tpu_custom_call", output_to_operand_aliasing={{0}: (4, {}), {1}: (5, {})} | custom-call | flops 2200000000 | tf_op jit(solution)/shard_map/pallas_call | solution.py:624
  (135 shorter events, 51.7 us)
Async XLA Ops:
  2.7 13.8 %collective-permute-start.1 = (bf16[272,768]{1,0:T(8,128)(2,1)}, bf16[272,768]{1,0:T(8,128)(2,1)}, u32[]{:S(2)}, u32[]{:S(2)}) collective-permute-start(bf16[272,768]{1,0:T(8,128)(2,1)} %shard_map.263.x0), channel_id=1, source_target_pairs={{0,2},{1,3},{2,0},{3,1},{4,6},{5,7},{6,4},{7,5},{8,10},{9,11},{10,... | collective-permute-start | bytes 1253384 | tf_op jit(solution)/shard_map/ppermute | solution.py:523
  6.6 20.4 %collective-permute-start.4 = (bf16[384,576]{1,0:T(8,128)(2,1)S(1)}, bf16[384,576]{1,0:T(8,128)(2,1)S(1)}, u32[]{:S(2)}, u32[]{:S(2)}) collective-permute-start(bf16[384,576]{1,0:T(8,128)(2,1)S(1)} %get-tuple-element.135), channel_id=1, source_target_pairs={{0,2},{1,3},{2,0},{3,1},{4,6},{5,7},{6,4},{7,5},{8,10},{9,11},{10,... | collective-permute-start | bytes 1327112 | tf_op jit(solution)/shard_map/ppermute | solution.py:523
  6.7 12.1 %collective-permute-start = (bf16[272,768]{1,0:T(8,128)(2,1)}, bf16[272,768]{1,0:T(8,128)(2,1)S(1)}, u32[]{:S(2)}, u32[]{:S(2)}) collective-permute-start(bf16[272,768]{1,0:T(8,128)(2,1)} %shard_map.263.x0), channel_id=1, source_target_pairs={{0,1},{1,0},{2,3},{3,2},{4,5},{5,4},{6,7},{7,6},{8,9},{9,8},{10,11... | collective-permute-start | bytes 1253384 | tf_op jit(solution)/shard_map/ppermute | solution.py:519
  16.5 24.3 %collective-permute-start.8 = (bf16[448,768]{1,0:T(8,128)(2,1)S(1)}, bf16[448,768]{1,0:T(8,128)(2,1)S(1)}, u32[]{:S(2)}, u32[]{:S(2)}) collective-permute-start(bf16[448,768]{1,0:T(8,128)(2,1)S(1)} %get-tuple-element.142), channel_id=1, source_target_pairs={{0,2},{1,3},{2,0},{3,1},{4,6},{5,7},{6,4},{7,5},{8,10},{9,11},{10,... | collective-permute-start | bytes 2064392 | tf_op jit(solution)/shard_map/ppermute | solution.py:523
  18.5 8.5 %collective-permute-start.3 = (bf16[192,576]{1,0:T(8,128)(2,1)S(1)}, bf16[192,576]{1,0:T(8,128)(2,1)S(1)}, u32[]{:S(2)}, u32[]{:S(2)}) collective-permute-start(bf16[192,576]{1,0:T(8,128)(2,1)S(1)} %get-tuple-element.134), channel_id=1, source_target_pairs={{0,1},{1,0},{2,3},{3,2},{4,5},{5,4},{6,7},{7,6},{8,9},{9,8},{10,11... | collective-permute-start | bytes 663560 | tf_op jit(solution)/shard_map/ppermute | solution.py:519
  40.9 7.9 %collective-permute-start.9 = (bf16[128,768]{1,0:T(8,128)(2,1)S(1)}, bf16[128,768]{1,0:T(8,128)(2,1)S(1)}, u32[]{:S(2)}, u32[]{:S(2)}) collective-permute-start(bf16[128,768]{1,0:T(8,128)(2,1)S(1)} %get-tuple-element.237), channel_id=1, source_target_pairs={{0,2},{1,3},{2,0},{3,1},{4,6},{5,7},{6,4},{7,5},{8,10},{9,11},{10,... | collective-permute-start | bytes 589832 | tf_op jit(solution)/shard_map/ppermute | solution.py:523
  42.7 9.3 %collective-permute-start.11 = (bf16[192,768]{1,0:T(8,128)(2,1)S(1)}, bf16[192,768]{1,0:T(8,128)(2,1)S(1)}, u32[]{:S(2)}, u32[]{:S(2)}) collective-permute-start(bf16[192,768]{1,0:T(8,128)(2,1)S(1)} %slice.104), channel_id=1, source_target_pairs={{0,4},{1,5},{2,6},{3,7},{4,1},{5,0},{6,3},{7,2},{8,12},{9,13},{10,... | collective-permute-start | bytes 884744 | tf_op jit(solution)/shard_map/ppermute | solution.py:661
  44.2 8.0 %collective-permute-start.10 = (bf16[128,768]{1,0:T(8,128)(2,1)S(1)}, bf16[128,768]{1,0:T(8,128)(2,1)S(1)}, u32[]{:S(2)}, u32[]{:S(2)}) collective-permute-start(bf16[128,768]{1,0:T(8,128)(2,1)S(1)} %get-tuple-element.236), channel_id=1, source_target_pairs={{0,2},{1,3},{2,0},{3,1},{4,6},{5,7},{6,4},{7,5},{8,10},{9,11},{10,... | collective-permute-start | bytes 589832 | tf_op jit(solution)/shard_map/ppermute | solution.py:523
  49.2 13.9 %collective-permute-start.18 = (bf16[448,768]{1,0:T(8,128)(2,1)S(1)}, bf16[448,768]{1,0:T(8,128)(2,1)S(1)}, u32[]{:S(2)}, u32[]{:S(2)}) collective-permute-start(bf16[448,768]{1,0:T(8,128)(2,1)S(1)} %get-tuple-element.149), channel_id=1, source_target_pairs={{0,1},{1,0},{2,3},{3,2},{4,5},{5,4},{6,7},{7,6},{8,9},{9,8},{10,11... | collective-permute-start | bytes 2064392 | tf_op jit(solution)/shard_map/ppermute | solution.py:519
  49.7 13.5 %collective-permute-start.19 = (bf16[448,768]{1,0:T(8,128)(2,1)S(1)}, bf16[448,768]{1,0:T(8,128)(2,1)S(1)}, u32[]{:S(2)}, u32[]{:S(2)}) collective-permute-start(bf16[448,768]{1,0:T(8,128)(2,1)S(1)} %collective-permute-done.8.g2), channel_id=1, source_target_pairs={{0,1},{1,0},{2,3},{3,2},{4,5},{5,4},{6,7},{7,6},{8,9},{9,8},{10,11... | collective-permute-start | bytes 2064392 | tf_op jit(solution)/shard_map/ppermute | solution.py:519
  52.5 10.7 %collective-permute-start.15 = (bf16[128,768]{1,0:T(8,128)(2,1)S(1)}, bf16[128,768]{1,0:T(8,128)(2,1)S(1)}, u32[]{:S(2)}, u32[]{:S(2)}) collective-permute-start(bf16[128,768]{1,0:T(8,128)(2,1)S(1)} %get-tuple-element.148.m0), channel_id=1, source_target_pairs={{0,2},{1,3},{2,0},{3,1},{4,6},{5,7},{6,4},{7,5},{8,10},{9,11},{10,... | collective-permute-start | bytes 589832 | tf_op jit(solution)/shard_map/ppermute | solution.py:523
  54.4 8.8 %collective-permute-start.13 = (bf16[128,768]{1,0:T(8,128)(2,1)S(1)}, bf16[128,768]{1,0:T(8,128)(2,1)S(1)}, u32[]{:S(2)}, u32[]{:S(2)}) collective-permute-start(bf16[128,768]{1,0:T(8,128)(2,1)S(1)} %get-tuple-element.148.m0), channel_id=1, source_target_pairs={{0,1},{1,0},{2,3},{3,2},{4,5},{5,4},{6,7},{7,6},{8,9},{9,8},{10,11... | collective-permute-start | bytes 589832 | tf_op jit(solution)/shard_map/ppermute | solution.py:519
  72.2 11.6 %collective-permute-start.23 = (bf16[128,768]{1,0:T(8,128)(2,1)S(1)}, bf16[128,768]{1,0:T(8,128)(2,1)S(1)}, u32[]{:S(2)}, u32[]{:S(2)}) collective-permute-start(bf16[128,768]{1,0:T(8,128)(2,1)S(1)} %get-tuple-element.235), channel_id=1, source_target_pairs={{0,2},{1,3},{2,0},{3,1},{4,6},{5,7},{6,4},{7,5},{8,10},{9,11},{10,... | collective-permute-start | bytes 589832 | tf_op jit(solution)/shard_map/ppermute | solution.py:523
  77.6 16.3 %collective-permute-start.21 = (bf16[4,192,768]{2,1,0:T(8,128)(2,1)S(1)}, bf16[4,192,768]{2,1,0:T(8,128)(2,1)S(1)}, u32[]{:S(2)}, u32[]{:S(2)}) collective-permute-start(bf16[4,192,768]{2,1,0:T(8,128)(2,1)S(1)} %get-tuple-element.156), channel_id=1, source_target_pairs={{0,4},{1,9},{2,6},{3,11},{4,0},{5,13},{6,2},{7,15},{8,12},{9,1},{1... | collective-permute-start | bytes 3538952 | tf_op jit(solution)/shard_map/ppermute | solution.py:577
  80.2 7.8 %collective-permute-start.30 = (bf16[128,768]{1,0:T(8,128)(2,1)S(1)}, bf16[128,768]{1,0:T(8,128)(2,1)S(1)}, u32[]{:S(2)}, u32[]{:S(2)}) collective-permute-start(bf16[128,768]{1,0:T(8,128)(2,1)S(1)} %get-tuple-element.164.f0), channel_id=1, source_target_pairs={{0,2},{1,3},{2,0},{3,1},{4,6},{5,7},{6,4},{7,5},{8,10},{9,11},{10,... | collective-permute-start | bytes 589832 | tf_op jit(solution)/shard_map/ppermute | solution.py:523
  84.8 11.1 %collective-permute-start.28 = (bf16[128,768]{1,0:T(8,128)(2,1)S(1)}, bf16[128,768]{1,0:T(8,128)(2,1)S(1)}, u32[]{:S(2)}, u32[]{:S(2)}) collective-permute-start(bf16[128,768]{1,0:T(8,128)(2,1)S(1)} %get-tuple-element.164.f0), channel_id=1, source_target_pairs={{0,1},{1,0},{2,3},{3,2},{4,5},{5,4},{6,7},{7,6},{8,9},{9,8},{10,11... | collective-permute-start | bytes 589832 | tf_op jit(solution)/shard_map/ppermute | solution.py:519
  88.0 7.9 %collective-permute-start.32 = (bf16[128,768]{1,0:T(8,128)(2,1)S(1)}, bf16[128,768]{1,0:T(8,128)(2,1)S(1)}, u32[]{:S(2)}, u32[]{:S(2)}) collective-permute-start(bf16[128,768]{1,0:T(8,128)(2,1)S(1)} %collective-permute-done.30.f2), channel_id=1, source_target_pairs={{0,1},{1,0},{2,3},{3,2},{4,5},{5,4},{6,7},{7,6},{8,9},{9,8},{10,11... | collective-permute-start | bytes 589832 | tf_op jit(solution)/shard_map/ppermute | solution.py:519
  94.2 10.0 %collective-permute-start.25 = (bf16[2,192,768]{2,1,0:T(8,128)(2,1)S(1)}, bf16[2,192,768]{2,1,0:T(8,128)(2,1)S(1)}, u32[]{:S(2)}, u32[]{:S(2)}) collective-permute-start(bf16[2,192,768]{2,1,0:T(8,128)(2,1)S(1)} %slice.108), channel_id=1, source_target_pairs={{0,8},{1,5},{2,10},{3,7},{4,12},{5,1},{6,14},{7,3},{8,0},{9,13},{1... | collective-permute-start | bytes 1769480 | tf_op jit(solution)/shard_map/ppermute | solution.py:577
  104.4 14.1 %collective-permute-start.26 = (bf16[1,192,768]{2,1,0:T(8,128)(2,1)S(1)}, bf16[1,192,768]{2,1,0:T(8,128)(2,1)S(1)}, u32[]{:S(2)}, u32[]{:S(2)}) collective-permute-start(bf16[1,192,768]{2,1,0:T(8,128)(2,1)S(1)} %slice.110), channel_id=1, source_target_pairs={{0,16},{1,17},{2,18},{3,19},{4,20},{5,21},{6,22},{7,23},{8,24},{9,... | collective-permute-start | bytes 884744 | tf_op jit(solution)/shard_map/ppermute | solution.py:577
  110.4 12.9 %collective-permute-start.34 = (bf16[512,768]{1,0:T(8,128)(2,1)S(1)}, bf16[512,768]{1,0:T(8,128)(2,1)S(1)}, u32[]{:S(2)}, u32[]{:S(2)}) collective-permute-start(bf16[512,768]{1,0:T(8,128)(2,1)S(1)} %get-tuple-element.175.send_ref), channel_id=1, source_target_pairs={{0,1},{1,0},{2,3},{3,2},{4,5},{5,4},{6,7},{7,6},{8,9},{9,8},{10,11... | collective-permute-start | bytes 2359304 | tf_op jit(solution)/shard_map/ppermute | solution.py:519
  110.5 11.1 %collective-permute-start.35 = (bf16[4,136,576]{2,1,0:T(8,128)(2,1)S(1)}, bf16[4,136,576]{2,1,0:T(8,128)(2,1)S(1)}, u32[]{:S(2)}, u32[]{:S(2)}) collective-permute-start(bf16[4,136,576]{2,1,0:T(8,128)(2,1)S(1)} %get-tuple-element.176), channel_id=1, source_target_pairs={{0,4},{1,9},{2,6},{3,11},{4,0},{5,13},{6,2},{7,15},{8,12},{9,1},{1... | collective-permute-start | bytes 1880072 | tf_op jit(solution)/shard_map/ppermute | solution.py:577
  121.8 12.6 %collective-permute-start.39 = (bf16[2,136,576]{2,1,0:T(8,128)(2,1)S(1)}, bf16[2,136,576]{2,1,0:T(8,128)(2,1)S(1)}, u32[]{:S(2)}, u32[]{:S(2)}) collective-permute-start(bf16[2,136,576]{2,1,0:T(8,128)(2,1)S(1)} %get-tuple-element.178), channel_id=1, source_target_pairs={{0,8},{1,5},{2,10},{3,7},{4,12},{5,1},{6,14},{7,3},{8,0},{9,13},{1... | collective-permute-start | bytes 940040 | tf_op jit(solution)/shard_map/ppermute | solution.py:577
  123.4 9.6 %collective-permute-start.40 = (bf16[256,768]{1,0:T(8,128)(2,1)S(1)}, bf16[256,768]{1,0:T(8,128)(2,1)S(1)}, u32[]{:S(2)}, u32[]{:S(2)}) collective-permute-start(bf16[256,768]{1,0:T(8,128)(2,1)S(1)} %add_convert_fusion.3), channel_id=1, source_target_pairs={{0,2},{1,3},{2,0},{3,1},{4,6},{5,7},{6,4},{7,5},{8,10},{9,11},{10,... | collective-permute-start | bytes 1179656 | tf_op jit(solution)/shard_map/ppermute | solution.py:523
  124.1 15.7 %collective-permute-start.42 = (bf16[1,192,768]{2,1,0:T(8,128)(2,1)S(1)}, bf16[1,192,768]{2,1,0:T(8,128)(2,1)S(1)}, u32[]{:S(2)}, u32[]{:S(2)}) collective-permute-start(bf16[1,192,768]{2,1,0:T(8,128)(2,1)S(1)} %maximum_bitcast_fusion.a_ref), channel_id=1, source_target_pairs={{0,16},{1,17},{2,18},{3,19},{4,20},{5,21},{6,22},{7,23},{8,24},{9,... | collective-permute-start | bytes 884744 | tf_op jit(solution)/shard_map/ppermute | solution.py:577
  128.0 22.5 %collective-permute-start.38 = (bf16[512,768]{1,0:T(8,128)(2,1)S(1)}, bf16[512,768]{1,0:T(8,128)(2,1)S(1)}, u32[]{:S(2)}, u32[]{:S(2)}) collective-permute-start(bf16[512,768]{1,0:T(8,128)(2,1)S(1)} %get-tuple-element.185), channel_id=1, source_target_pairs={{0,1},{1,0},{2,3},{3,2},{4,5},{5,4},{6,7},{7,6},{8,9},{9,8},{10,11... | collective-permute-start | bytes 2359304 | tf_op jit(solution)/shard_map/ppermute | solution.py:519
  134.4 12.9 %collective-permute-start.41 = (bf16[1,136,576]{2,1,0:T(8,128)(2,1)S(1)}, bf16[1,136,576]{2,1,0:T(8,128)(2,1)S(1)}, u32[]{:S(2)}, u32[]{:S(2)}) collective-permute-start(bf16[1,136,576]{2,1,0:T(8,128)(2,1)S(1)} %get-tuple-element.199), channel_id=1, source_target_pairs={{0,16},{1,17},{2,18},{3,19},{4,20},{5,21},{6,22},{7,23},{8,24},{9,... | collective-permute-start | bytes 470024 | tf_op jit(solution)/shard_map/ppermute | solution.py:577
  139.9 14.9 %collective-permute-start.48 = (bf16[2,192,768]{2,1,0:T(8,128)(2,1)S(1)}, bf16[2,192,768]{2,1,0:T(8,128)(2,1)S(1)}, u32[]{:S(2)}, u32[]{:S(2)}) collective-permute-start(bf16[2,192,768]{2,1,0:T(8,128)(2,1)S(1)} %shard_map.281.a_ref), channel_id=1, source_target_pairs={{0,8},{1,5},{2,10},{3,7},{4,12},{5,1},{6,14},{7,3},{8,0},{9,13},{1... | collective-permute-start | bytes 1769480 | tf_op jit(solution)/shard_map/ppermute | solution.py:577
  154.0 11.7 %collective-permute-start.47 = (bf16[152,576]{1,0:T(8,128)(2,1)S(1)}, bf16[152,576]{1,0:T(8,128)(2,1)S(1)}, u32[]{:S(2)}, u32[]{:S(2)}) collective-permute-start(bf16[152,576]{1,0:T(8,128)(2,1)S(1)} %shard_map.283.a_ref), channel_id=1, source_target_pairs={{0,16},{1,17},{2,18},{3,19},{4,20},{5,21},{6,22},{7,23},{8,24},{9,... | collective-permute-start | bytes 525320 | tf_op jit(solution)/shard_map/ppermute | solution.py:577
  154.8 26.8 %collective-permute-start.51 = (bf16[4,192,768]{2,1,0:T(8,128)(2,1)S(1)}, bf16[4,192,768]{2,1,0:T(8,128)(2,1)S(1)}, u32[]{:S(2)}, u32[]{:S(2)}) collective-permute-start(bf16[4,192,768]{2,1,0:T(8,128)(2,1)S(1)} %shard_map.284.g_ref), channel_id=1, source_target_pairs={{0,4},{1,9},{2,6},{3,11},{4,0},{5,13},{6,2},{7,15},{8,12},{9,1},{1... | collective-permute-start | bytes 3538952 | tf_op jit(solution)/shard_map/ppermute | solution.py:577
  165.7 11.6 %collective-permute-start.49 = (bf16[288,576]{1,0:T(8,128)(2,1)S(1)}, bf16[288,576]{1,0:T(8,128)(2,1)S(1)}, u32[]{:S(2)}, u32[]{:S(2)}) collective-permute-start(bf16[288,576]{1,0:T(8,128)(2,1)S(1)} %shard_map.286.a_ref), channel_id=1, source_target_pairs={{0,8},{1,5},{2,10},{3,7},{4,12},{5,1},{6,14},{7,3},{8,0},{9,13},{1... | collective-permute-start | bytes 995336 | tf_op jit(solution)/shard_map/ppermute | solution.py:577
  165.8 12.4 %collective-permute-start.44 = (bf16[256,768]{1,0:T(8,128)(2,1)S(1)}, bf16[256,768]{1,0:T(8,128)(2,1)S(1)}, u32[]{:S(2)}, u32[]{:S(2)}) collective-permute-start(bf16[256,768]{1,0:T(8,128)(2,1)S(1)} %add_convert_fusion.2), channel_id=1, source_target_pairs={{0,2},{1,3},{2,0},{3,1},{4,6},{5,7},{6,4},{7,5},{8,10},{9,11},{10,... | collective-permute-start | bytes 1179656 | tf_op jit(solution)/shard_map/ppermute | solution.py:523
  177.4 11.3 %collective-permute-start.50 = (bf16[560,576]{1,0:T(8,128)(2,1)S(1)}, bf16[560,576]{1,0:T(8,128)(2,1)S(1)}, u32[]{:S(2)}, u32[]{:S(2)}) collective-permute-start(bf16[560,576]{1,0:T(8,128)(2,1)S(1)} %shard_map.287.g_ref.refs_0_), channel_id=1, source_target_pairs={{0,4},{1,9},{2,6},{3,11},{4,0},{5,13},{6,2},{7,15},{8,12},{9,1},{1... | collective-permute-start | bytes 1935368 | tf_op jit(solution)/shard_map/ppermute | solution.py:577
  (29 other events, 200.1 us)

commit v3 on v2

--- a/solution.py
+++ b/solution.py
@@ -94,8 +94,14 @@
     rank = rank_ref[0]
     rows, width = keep_ref.shape
     part = width // 4
-    for k, w in enumerate((w0[...], w1[...], w2[0:part], w3[...])):
-        wq_ref[at_rows(rank ^ k, part)] = w
+    fold = w0.shape[0]
+    rest = part - fold
+    for k, w in enumerate((w0, w1, w2, w3)):
+        base = (rank ^ k) * part
+        wq_ref[pl.ds(pl.multiple_of(base, rest), fold)] = w[0:fold, 0:3 * part]
+        for i in range(3):
+            wq_ref[pl.ds(pl.multiple_of(base + fold, rest), rest), i * part:(i + 1) * part] = w[
+                i * rest:(i + 1) * rest, 3 * part:]
     qkv_ref[...] = jnp.dot(nrm_ref[...], wq_ref[...], preferred_element_type=f32).astype(bf16)
     heads = part // HD
     total_rows = nrm_ref.shape[0]
@@ -349,20 +355,19 @@
 
 def chunk_qkv(rank, me, count, gq_s, go_s, keep_ref, gsend_ref):
     part = go_s.shape[0]
-    rows, third = part // count, part // count // 3
+    rows = part // count
     wide = gq_s.shape[1]
     for p in range(count):
         target, place = (keep_ref, p) if p < count // 2 else (gsend_ref, p - count // 2)
         nat = chunk_at(rank, me, count, p)
         for k in range(4):
-            at = pl.ds(pl.multiple_of((rank ^ k) * part + nat * rows, 8), rows)
-            target[place, k * rows:(k + 1) * rows] = gq_s[at].astype(target.dtype)
-        out = go_s[at_rows(nat, rows)]
-        target[place, 4 * rows:5 * rows] = out[:, 0:wide].astype(target.dtype)
-        tail = out[:, wide:]
-        packed = jnp.concatenate([tail[i * third:(i + 1) * third] for i in range(3)], 1)
-        target[place, 5 * rows:5 * rows + third] = packed.astype(target.dtype)
-        target[place, 5 * rows + third:] = jnp.zeros((target.shape[1] - 5 * rows - third, wide), target.dtype)
+            block = gq_s[pl.ds(pl.multiple_of((rank ^ k) * part + nat * rows, 8), rows)].astype(bf16)
+            if k < 3:
+                target[place, k * rows:(k + 1) * rows, 0:wide] = block
+            else:
+                for i in range(3):
+                    target[place, i * rows:(i + 1) * rows, wide:] = block[:, i * part:(i + 1) * part]
+        target[place, 3 * rows:4 * rows] = go_s[at_rows(nat, rows)].astype(bf16)
 
 
 def small_body(rank_ref, send_ref, keep_ref, far_ref, unit_ref, inv_ref, ids_ref, par_ref, smid_ref, smid2_ref, upb_ref,
@@ -400,10 +405,14 @@
 def cut_qkv_body(keep_ref, got_ref, sm_ref, low_ref, n1, n2, n3):
     total = keep_ref[0].astype(f32) + got_ref[0].astype(f32)
     low_ref[...] = total.astype(bf16)
-    rows = n1.shape[0] - 16
-    for k, ref in ((1, n1), (2, n2), (3, n3)):
-        ref[0:rows] = total[k * rows:(k + 1) * rows].astype(bf16)
+    rows, wide = n1.shape[0] - 16, n1.shape[1]
+    part = wide // 3
+    for k, ref in ((1, n1), (2, n2)):
+        ref[0:rows] = total[k * rows:(k + 1) * rows, 0:wide].astype(bf16)
         ref[rows:] = sm_ref[k]
+    for i in range(3):
+        n3[0:rows, i * part:(i + 1) * part] = total[i * rows:(i + 1) * rows, wide:].astype(bf16)
+    n3[rows:] = sm_ref[3]
 
 
 def split_qkv_body(keep_ref, got_ref, kept_ref, send_ref):
@@ -421,15 +430,20 @@
 
 
 def join_qkv_body(low_ref, sm_ref, b1, b2, b3, out_ref):
-    rows = b1.shape[0] - 16
+    rows, wide = b1.shape[0] - 16, b1.shape[1]
+    part = wide // 3
     pieces = low_ref.shape[0]
     total = sm_ref[0].astype(f32)
-    out_ref[0:rows] = low_ref[0:rows]
-    for k, b in ((1, b1), (2, b2), (3, b3)):
-        out_ref[k * rows:(k + 1) * rows] = b[0:rows]
+    out_ref[0:rows, 0:wide] = low_ref[0:rows, 0:wide]
+    for k, b in ((1, b1), (2, b2)):
+        out_ref[k * rows:(k + 1) * rows, 0:wide] = b[0:rows]
+    for i in range(3):
+        out_ref[i * rows:(i + 1) * rows, wide:] = b3[0:rows, i * part:(i + 1) * part]
+    for b in (b1, b2, b3):
         total = total + b[rows:].astype(f32)
-    out_ref[4 * rows:pieces] = low_ref[4 * rows:]
-    out_ref[pieces:] = total.astype(bf16)
+    out_ref[3 * rows:pieces] = low_ref[3 * rows:]
+    out_ref[pieces:, 0:wide] = total.astype(bf16)
+    out_ref[pieces:, wide:] = jnp.zeros((16, part), bf16)
 
 
 def grow_qkv_body(a_ref, b_ref, out_ref):
@@ -464,18 +478,17 @@
         small_refs, stage_s = refs[6:-1], refs[-1]
     else:
         qkv_ref, out_ref, stage_s = refs
-    rows, third = out_ref.shape[0], out_ref.shape[0] // 3
-    width = out_ref.shape[1]
+    rows, width = out_ref.shape
     part = width // 4
-    wide = g_ref.shape[1]
-    stage_s[...] = g_ref[0:4 * rows].astype(f32)
+    wide = 3 * part
+    stage_s[0:3 * rows] = g_ref[0:3 * rows, 0:wide].astype(f32)
+    for i in range(3):
+        stage_s[3 * rows:, i * part:(i + 1) * part] = g_ref[i * rows:(i + 1) * rows, wide:].astype(f32)
     for j in range(4):
         block = stage_s[at_rows(rank ^ j, rows)]
         for i in range(3):
             qkv_ref[:, i * width + j * part:i * width + (j + 1) * part] = block[:, i * part:(i + 1) * part]
-    out_ref[:, 0:wide] = g_ref[4 * rows:5 * rows].astype(f32)
-    packed = g_ref[5 * rows:5 * rows + third].astype(f32)
-    out_ref[:, wide:] = jnp.concatenate([packed[:, i * part:(i + 1) * part] for i in range(3)], 0)
+    out_ref[...] = g_ref[3 * rows:4 * rows].astype(f32)
     if ends:
         @pl.when(pl.program_id(0) == 0)
         def _():
@@ -491,13 +504,17 @@
 def qkv_blocks_body(rank_ref, w_ref, own_ref, near_ref, far_ref, stage_s):
     rank = rank_ref[0]
     part = w_ref.shape[0]
+    fold = own_ref.shape[0]
+    rest = part - fold
     for t in range(4):
-        stage_s[t] = jnp.concatenate(
-            [w_ref[:, (4 * i + t) * part:(4 * i + t + 1) * part] for i in range(3)], 1)
+        for i in range(3):
+            at = slice((4 * i + t) * part, (4 * i + t + 1) * part)
+            stage_s[t, :, i * part:(i + 1) * part] = w_ref[0:fold, at]
+            stage_s[t, i * rest:(i + 1) * rest, 3 * part:] = w_ref[fold:, at]
     own_ref[...] = stage_s[rank]
     near_ref[...] = stage_s[rank ^ 1]
-    far_ref[0:part] = stage_s[rank ^ 2]
-    far_ref[part:] = stage_s[rank ^ 3]
+    far_ref[0:fold] = stage_s[rank ^ 2]
+    far_ref[fold:] = stage_s[rank ^ 3]
 
 
 def up_blocks_body(rank_ref, w_ref, cot_ref, own_ref, near_ref, far_ref):
@@ -612,7 +629,7 @@
         )(*args)
 
     ur = part // replicas
-    pieces = 5 * ur + ur // 3 + 8 * packed
+    pieces, wide_cols = (4 * ur, width) if packed else (5 * ur + ur // 3, 3 * part)
 
     def placed(body, values, start, shapes, blocks_of, extra, scratch, aliases, *first):
         def at_chunk(p, s):
@@ -640,9 +657,10 @@
     block, = call(pack_body, 1, [((rows + 16, width), bf16)], [], tokens, pass_ids, pass_table.T, norm1_gain, norm1_bias,
                   out_bias, norm2_gain, norm2_bias, down_bias, ranked=False, wide=True)
     x1, x2 = by_core(block), by_row(block)
+    fold = part * 3 // 4
     own_q, near_q, far_q = call(
-        qkv_blocks_body, 0, [((part, 3 * part), bf16), ((part, 3 * part), bf16), ((2 * part, 3 * part), bf16)],
-        [((4, part, 3 * part), bf16)], place, after(qkv_weight, block))
+        qkv_blocks_body, 0, [((fold, width), bf16), ((fold, width), bf16), ((2 * fold, width), bf16)],
+        [((4, fold, width), bf16)], place, after(qkv_weight, block))
     far_q = by_row(far_q)
     own_u, near_u, far_u = call(
         up_blocks_body, 0,
@@ -655,7 +673,7 @@
         [((seq, 1), f32), ((8, seq), f32), ((rows, width), f32), ((16, width), f32), ((seq, width), bf16),
          ((seq, width), bf16), ((seq, width), bf16), ((seq, 1), f32), ((8, rows), f32)], [], place, seg_ids, *blocks)
     far_q = after(far_q, ids)
-    wq = own_q, by_core(near_q), far_q, by_core(far_q[part:])
+    wq = own_q, by_core(near_q), far_q, by_core(far_q[fold:])
     far_u = by_row(far_u)
     group = by_core(near_u), far_u, by_core(far_u)
     pair_u = lax.ppermute(far_u[rows:], ("replica", "shard"), [
@@ -718,7 +736,7 @@
         got = plane_swap(gsend, replicas, phase)
 
     if packed:
-        grads = [((replicas // 2, pieces, 3 * part), bf16)] * 2
+        grads = [((replicas // 2, pieces, wide_cols), bf16)] * 2
     else:
         grads = [((width, 3 * part), f32), ((part, width), f32)]
     dctx, delta, grad_out, dqkv = call(
@@ -782,7 +800,7 @@
     def qkv_swap():
         kept, got = now.get("qkeep", qkeep), after(now["qkv"], now["turn"])
         if packed:
-            low, *cuts = call(cut_qkv_body, 1, [((pieces, 3 * part), bf16)] + [((ur + 16, 3 * part), bf16)] * 3, [],
+            low, *cuts = call(cut_qkv_body, 1, [((pieces, wide_cols), bf16)] + [((ur + 16, 3 * part), bf16)] * 3, [],
                               kept, got, now["small"], ranked=False)
         else:
             low = (kept.astype(f32) + got.astype(f32))[0].astype(bf16)
@@ -794,7 +812,7 @@
         low, small = now["low"], now["small"]
         quads = [after(s, now["turn"]) for s in now["quads"]]
         if packed:
-            now["qkv_all"], = call(join_qkv_body, 1, [((pieces + 16, 3 * part), bf16)], [], low, small, *quads,
+            now["qkv_all"], = call(join_qkv_body, 1, [((pieces + 16, wide_cols), bf16)], [], low, small, *quads,
                                    ranked=False)
         else:
             total = small[0].astype(f32) + sum(q[ur:].astype(f32) for q in quads)
@@ -806,7 +824,7 @@
     def qkv_join(phase):
         held, got = now["qkv_all"], after(now["qkv"], now["turn"])
         if packed:
-            now["qkv_all"], = call(grow_qkv_body, 1, [((2 * held.shape[0] - 16, 3 * part), bf16)], [], held, got,
+            now["qkv_all"], = call(grow_qkv_body, 1, [((2 * held.shape[0] - 16, wide_cols), bf16)], [], held, got,
                                    ranked=False)
         else:
             total = held[-16:].astype(f32) + got[-16:].astype(f32)

time: 192 us -> 186 us (0.969)
  waiting for transfers between devices: 94.1 us -> 82 us
  starting transfers between devices: 39.7 us -> 45.6 us
    ppermute x12, waiting for transfers between devices: 42.9 us -> 30.7 us  [plane_swap(): return lax.ppermute(value, ('replica', 'shard'), plane_pairs(count, phase))]
    ppermute x12, starting transfers between devices: 13.7 us -> 21.4 us  [plane_swap(): return lax.ppermute(value, ('replica', 'shard'), plane_pairs(count, phase))]
  transfers between devices with their start and end apart: 52 -> 52, of which waited for: 26 -> 25; matrix products, arithmetic and copies ran while one was open for 1% -> 1% of each run, Pallas kernels for 23% -> 24%
where the time goes in v3:
time: 186 us
  waiting for transfers between devices  82 us (44%)
  Pallas kernels  53.7 us (29%)
  starting transfers between devices  45.6 us (25%)
  other arithmetic  1.88 us (1%)
    pallas_call x24, Pallas kernels, call(): pl.pallas_call(body, out_shape=[jax.ShapeDtypeStruct(s, d) for s, d in ou...  43.4 us
    ppermute x15, waiting for transfers between devices, by_row(): return lax.ppermute(value, 'shard', ROWY)  42.9 us
    ppermute x12, waiting for transfers between devices, plane_swap(): return lax.ppermute(value, ('replica', 'shard'), plane_pairs(count, phase))  30.7 us
    ppermute x12, starting transfers between devices, plane_swap(): return lax.ppermute(value, ('replica', 'shard'), plane_pairs(count, phase))  21.4 us
    ppermute x15, starting transfers between devices, by_row(): return lax.ppermute(value, 'shard', ROWY)  15.7 us
    pallas_call x4, Pallas kernels, placed(): pl.pallas_call(body, out_shape=[jax.ShapeDtypeStruct(s, f32) for s in sha...  10.3 us
    ppermute x22, starting transfers between devices, by_core(): return lax.ppermute(value, 'shard', CORE)  4.97 us
    ppermute x22, waiting for transfers between devices, by_core(): return lax.ppermute(value, 'shard', CORE)  4.12 us
  transfers between devices with their start and end apart: 52, of which 25 were waited for; matrix products, arithmetic and copies ran while one was open for 1% of the time, Pallas kernels for 24%

profile of v3, /device:TPU:0, one launch (start us, length us, event | category | flops | bytes accessed | tf_op | source)
XLA Modules:
  0.0 185.7 jit_solution(5159693276098442147)
XLA Ops:
  2.7 3.0 %collective-permute-start.1 = (bf16[272,768]{1,0:T(8,128)(2,1)}, bf16[272,768]{1,0:T(8,128)(2,1)}, u32[]{:S(2)}, u32[]{:S(2)}) collective-permute-start(bf16[272,768]{1,0:T(8,128)(2,1)} %shard_map.263.x0), channel_id=1, source_target_pairs={{0,2},{1,3},{2,0},{3,1},{4,6},{5,7},{6,4},{7,5},{8,10},{9,11},{10,... | collective-permute-start | bytes 1253384 | tf_op jit(solution)/shard_map/ppermute | solution.py:540
  8.4 8.1 %collective-permute-done.1.x2 = bf16[272,768]{1,0:T(8,128)(2,1)} collective-permute-done((bf16[272,768]{1,0:T(8,128)(2,1)}, bf16[272,768]{1,0:T(8,128)(2,1)}, u32[]{:S(2)}, u32[]{:S(2)}) %collective-permute-start.1) | collective-permute-done | bytes 417824 | tf_op jit(solution)/shard_map/ppermute | solution.py:540
  18.8 2.5 %shard_map.266 = (f32[1024,1]{1,0:T(8,128)S(1)}, f32[8,1024]{1,0:T(8,128)S(1)}, f32[256,768]{1,0:T(8,128)S(1)}, f32[16,768]{1,0:T(8,128)S(1)}, bf16[1024,768]{1,...) custom-call(s32[3]{0:T(128)S(1)} %pad_add_fusion.rank_ref, ...), custom_call_target="tpu_custom_call" | custom-call | tf_op jit(solution)/shard_map/pallas_call | solution.py:620
  21.3 4.6 %collective-permute-done.4.w2 = bf16[288,768]{1,0:T(8,128)(2,1)S(1)} collective-permute-done((bf16[288,768]{1,0:T(8,128)(2,1)S(1)}, bf16[288,768]{1,0:T(8,128)(2,1)S(1)}, u32[]{:S(2)}, u32[]{:S(2)}) %collective-permute-start.4) | collective-permute-done | bytes 442400 | tf_op jit(solution)/shard_map/ppermute | solution.py:540
  27.4 8.4 %shard_map.267 = (bf16[256,768]{1,0:T(8,128)(2,1)S(1)}, bf16[256,768]{1,0:T(8,128)(2,1)S(1)}, f32[256,768]{1,0:T(8,128)S(1)}, f32[256,768]{1,0:T(8,128)S(1)}, bf...) custom-call(s32[3]{0:T(128)S(1)} %pad_add_fusion.rank_ref, ...), custom_call_target="tpu_custom_call" | custom-call | tf_op jit(solution)/shard_map/pallas_call | solution.py:620
  36.5 3.3 %collective-permute-done.8.g2 = bf16[448,768]{1,0:T(8,128)(2,1)S(1)} collective-permute-done((bf16[448,768]{1,0:T(8,128)(2,1)S(1)}, bf16[448,768]{1,0:T(8,128)(2,1)S(1)}, u32[]{:S(2)}, u32[]{:S(2)}) %collective-permute-start.8) | collective-permute-done | bytes 688160 | tf_op jit(solution)/shard_map/ppermute | solution.py:540
  43.7 4.1 %collective-permute-done.9.yrecv_ref = bf16[128,768]{1,0:T(8,128)(2,1)S(1)} collective-permute-done((bf16[128,768]{1,0:T(8,128)(2,1)S(1)}, bf16[128,768]{1,0:T(8,128)(2,1)S(1)}, u32[]{:S(2)}, u32[]{:S(2)}) %collective-permute-start.9) | collective-permute-done | bytes 196640 | tf_op jit(solution)/shard_map/ppermute | solution.py:540
  48.8 2.2 %collective-permute-done.11.pair_ref = bf16[192,768]{1,0:T(8,128)(2,1)S(1)} collective-permute-done((bf16[192,768]{1,0:T(8,128)(2,1)S(1)}, bf16[192,768]{1,0:T(8,128)(2,1)S(1)}, u32[]{:S(2)}, u32[]{:S(2)}) %collective-permute-start.11) | collective-permute-done | bytes 294944 | tf_op jit(solution)/shard_map/ppermute | solution.py:679
  53.3 5.4 %collective-permute-done.14.n2 = bf16[128,768]{1,0:T(8,128)(2,1)S(1)} collective-permute-done((bf16[128,768]{1,0:T(8,128)(2,1)S(1)}, bf16[128,768]{1,0:T(8,128)(2,1)S(1)}, u32[]{:S(2)}, u32[]{:S(2)}) %collective-permute-start.14) | collective-permute-done | bytes 196640 | tf_op jit(solution)/shard_map/ppermute | solution.py:540
  58.7 3.4 %collective-permute-done.15.m2 = bf16[128,768]{1,0:T(8,128)(2,1)S(1)} collective-permute-done((bf16[128,768]{1,0:T(8,128)(2,1)S(1)}, bf16[128,768]{1,0:T(8,128)(2,1)S(1)}, u32[]{:S(2)}, u32[]{:S(2)}) %collective-permute-start.15) | collective-permute-done | bytes 196640 | tf_op jit(solution)/shard_map/ppermute | solution.py:540
  63.5 5.3 %shard_map.270 = (bf16[256,768]{1,0:T(8,128)(2,1)S(1)}, bf16[256,768]{1,0:T(8,128)(2,1)S(1)}, f32[256,768]{1,0:T(8,128)S(1)}, f32[256,768]{1,0:T(8,128)S(1)}, bf...) custom-call(s32[3]{0:T(128)S(1)} %pad_add_fusion.rank_ref, bf16[128,768]{1,0:T(8,128)(2,1)S(1)} %get-tuple-element.145.n0, ...), custom_call_target="tpu_custom_call" | custom-call | flops 5500000256 | tf_op jit(solution)/shard_map/pallas_call | solution.py:620
  72.8 3.8 %shard_map.271 = (f32[8,768]{1,0:T(8,128)S(1)}, bf16[4,192,768]{2,1,0:T(8,128)(2,1)S(1)}, bf16[4,192,768]{2,1,0:T(8,128)(2,1)S(1)}) custom-call(s32[3]{0:T(128)S(1)} %pad_add_fusion.rank_ref, bf16[128,768]{1,0:T(8,128)(2,1)S(1)} %get-tuple-element.145.n0, bf16[128,768]{1,0:T(8,128)(2,1)S(1)} %get-tuple-element.148.m0, ...), custom_call_target="tpu_custom_call" | custom-call | flops 8800000000 | tf_op jit(solution)/shard_map/pallas_call | solution.py:620
  79.5 3.2 %collective-permute-done.23.yrecv_ref = bf16[128,768]{1,0:T(8,128)(2,1)S(1)} collective-permute-done((bf16[128,768]{1,0:T(8,128)(2,1)S(1)}, bf16[128,768]{1,0:T(8,128)(2,1)S(1)}, u32[]{:S(2)}, u32[]{:S(2)}) %collective-permute-start.23) | collective-permute-done | bytes 196640 | tf_op jit(solution)/shard_map/ppermute | solution.py:540
  84.2 2.7 %collective-permute-done.30.f2 = bf16[128,768]{1,0:T(8,128)(2,1)S(1)} collective-permute-done((bf16[128,768]{1,0:T(8,128)(2,1)S(1)}, bf16[128,768]{1,0:T(8,128)(2,1)S(1)}, u32[]{:S(2)}, u32[]{:S(2)}) %collective-permute-start.30) | collective-permute-done | bytes 196640 | tf_op jit(solution)/shard_map/ppermute | solution.py:540
  87.0 3.4 %collective-permute-done.29.g2 = bf16[128,768]{1,0:T(8,128)(2,1)S(1)} collective-permute-done((bf16[128,768]{1,0:T(8,128)(2,1)S(1)}, bf16[128,768]{1,0:T(8,128)(2,1)S(1)}, u32[]{:S(2)}, u32[]{:S(2)}) %collective-permute-start.29) | collective-permute-done | bytes 196640 | tf_op jit(solution)/shard_map/ppermute | solution.py:540
  90.4 2.5 %collective-permute-done.21 = bf16[4,192,768]{2,1,0:T(8,128)(2,1)S(1)} collective-permute-done((bf16[4,192,768]{2,1,0:T(8,128)(2,1)S(1)}, bf16[4,192,768]{2,1,0:T(8,128)(2,1)S(1)}, u32[]{:S(2)}, u32[]{:S(2)}) %collective-permute-start.21) | collective-permute-done | bytes 1179680 | tf_op jit(solution)/shard_map/ppermute | solution.py:594
  94.8 8.3 %shard_map.274 = (bf16[1024,192]{1,0:T(8,128)(2,1)}, f32[8,1024]{1,0:T(8,128)}, f32[192,768]{1,0:T(8,128)S(1)}, bf16[1024,576]{1,0:T(8,128)(2,1)S(1)}) custom-call(s32[3]{0:T(128)S(1)} %pad_add_fusion.rank_ref, f32[1024,1]{1,0:T(8,128)S(1)} %get-tuple-element.131.segc_ref, f32[8,1024]{1,0:T(8,128)S(1)} %get-tuple-element.132.segr_ref, ...), custom_call_target="tpu_custom_call" | custom-call | flops 9900000256 | tf_op jit(solution)/shard_map/pallas_call | solution.py:620
  103.4 2.7 %collective-permute-start.26 = (bf16[1,192,768]{2,1,0:T(8,128)(2,1)S(1)}, bf16[1,192,768]{2,1,0:T(8,128)(2,1)S(1)}, u32[]{:S(2)}, u32[]{:S(2)}) collective-permute-start(bf16[1,192,768]{2,1,0:T(8,128)(2,1)S(1)} %slice.110), channel_id=1, source_target_pairs={{0,16},{1,17},{2,18},{3,19},{4,20},{5,21},{6,22},{7,23},{8,24},{9,... | collective-permute-start | bytes 884744 | tf_op jit(solution)/shard_map/ppermute | solution.py:594
  106.0 3.4 %shard_map.275 = (bf16[512,768]{1,0:T(8,128)(2,1)S(1)}, f32[256,768]{1,0:T(8,128)S(1)}, f32[256,768]{1,0:T(8,128)S(1)}, bf16[4,96,768]{2,1,0:T(8,128)(2,1)S(1)}, bf16[4,96,768]{2,1,0:T(8,128)(2,1)S(1)}) custom-call(s32[3]{0:T(128)S(1)} %pad_add_fusion.rank_ref, bf16[1024,576]{1,0:T(8,128)(2,1)S(1)} %get-tuple-element.168.dqkv_s, ...), custom_call_target="tpu_custom_call" | custom-call | flops 3300000000 | tf_op jit(solution)/shard_map/pallas_call | solution.py:620
  109.6 7.9 %collective-permute-done.26 = bf16[1,192,768]{2,1,0:T(8,128)(2,1)S(1)} collective-permute-done((bf16[1,192,768]{2,1,0:T(8,128)(2,1)S(1)}, bf16[1,192,768]{2,1,0:T(8,128)(2,1)S(1)}, u32[]{:S(2)}, u32[]{:S(2)}) %collective-permute-start.26) | collective-permute-done | bytes 294944 | tf_op jit(solution)/shard_map/ppermute | solution.py:594
  122.3 2.3 %collective-permute-start.42 = (bf16[1,192,768]{2,1,0:T(8,128)(2,1)S(1)}, bf16[1,192,768]{2,1,0:T(8,128)(2,1)S(1)}, u32[]{:S(2)}, u32[]{:S(2)}) collective-permute-start(bf16[1,192,768]{2,1,0:T(8,128)(2,1)S(1)} %maximum_bitcast_fusion.a_ref), channel_id=1, source_target_pairs={{0,16},{1,17},{2,18},{3,19},{4,20},{5,21},{6,22},{7,23},{8,24},{9,... | collective-permute-start | bytes 884744 | tf_op jit(solution)/shard_map/ppermute | solution.py:594
  127.5 2.6 %shard_map.278.sm_ref = bf16[4,16,576]{2,1,0:T(8,128)(2,1)S(1)} custom-call(s32[3]{0:T(128)S(1)} %pad_add_fusion.rank_ref, bf16[512,768]{1,0:T(8,128)(2,1)S(1)} %get-tuple-element.175.send_ref, f32[256,768]{1,0:T(8,128)S(1)} %get-tuple-element.189.keep_ref, f32[256,768]{1,0:T(8,128)S(1)} %get-tuple-element.174.far_ref, ...), custom_call_target="tpu_custom_call" | custom-call | tf_op jit(solution)/shard_map/pallas_call | solution.py:620
  132.5 4.9 %collective-permute-start.41 = (bf16[1,96,768]{2,1,0:T(8,128)(2,1)S(1)}, bf16[1,96,768]{2,1,0:T(8,128)(2,1)S(1)}, u32[]{:S(2)}, u32[]{:S(2)}) collective-permute-start(bf16[1,96,768]{2,1,0:T(8,128)(2,1)S(1)} %get-tuple-element.199), channel_id=1, source_target_pairs={{0,16},{1,17},{2,18},{3,19},{4,20},{5,21},{6,22},{7,23},{8,24},{9,... | collective-permute-start | bytes 442376 | tf_op jit(solution)/shard_map/ppermute | solution.py:594
  138.2 4.7 %collective-permute-start.48 = (bf16[2,192,768]{2,1,0:T(8,128)(2,1)S(1)}, bf16[2,192,768]{2,1,0:T(8,128)(2,1)S(1)}, u32[]{:S(2)}, u32[]{:S(2)}) collective-permute-start(bf16[2,192,768]{2,1,0:T(8,128)(2,1)S(1)} %shard_map.281.a_ref), channel_id=1, source_target_pairs={{0,8},{1,5},{2,10},{3,7},{4,12},{5,1},{6,14},{7,3},{8,0},{9,13},{1... | collective-permute-start | bytes 1769480 | tf_op jit(solution)/shard_map/ppermute | solution.py:594
  147.7 2.0 %collective-permute-done.46.b3 = bf16[40,576]{1,0:T(8,128)(2,1)S(1)} collective-permute-done((bf16[40,576]{1,0:T(8,128)(2,1)S(1)}, bf16[40,576]{1,0:T(8,128)(2,1)S(1)}, u32[]{:S(2)}, u32[]{:S(2)}) %collective-permute-start.46) | collective-permute-done | bytes 46112 | tf_op jit(solution)/shard_map/ppermute | solution.py:767
  153.6 2.5 %shard_map.285 = (f32[768,768]{1,0:T(8,128)}, f32[192,3072]{1,0:T(8,128)}) custom-call(s32[3]{0:T(128)S(1)} %pad_add_fusion.rank_ref, bf16[4,192,768]{2,1,0:T(8,128)(2,1)S(1)} %shard_map.284.g_ref), custom_call_target="tpu_custom_call" | custom-call | flops 2200000000 | tf_op jit(solution)/shard_map/pallas_call | solution.py:641
  156.1 5.8 %collective-permute-done.47.b_ref = bf16[112,768]{1,0:T(8,128)(2,1)S(1)} collective-permute-done((bf16[112,768]{1,0:T(8,128)(2,1)S(1)}, bf16[112,768]{1,0:T(8,128)(2,1)S(1)}, u32[]{:S(2)}, u32[]{:S(2)}) %collective-permute-start.47) | collective-permute-done | bytes 172064 | tf_op jit(solution)/shard_map/ppermute | solution.py:594
  163.5 9.0 %collective-permute-done.49.b_ref = bf16[208,768]{1,0:T(8,128)(2,1)S(1)} collective-permute-done((bf16[208,768]{1,0:T(8,128)(2,1)S(1)}, bf16[208,768]{1,0:T(8,128)(2,1)S(1)}, u32[]{:S(2)}, u32[]{:S(2)}) %collective-permute-start.49) | collective-permute-done | bytes 319520 | tf_op jit(solution)/shard_map/ppermute | solution.py:594
  174.7 2.6 %shard_map.288 = (f32[192,2304]{1,0:T(8,128)}, f32[192,768]{1,0:T(8,128)}) custom-call(s32[3]{0:T(128)S(1)} %pad_add_fusion.rank_ref, bf16[400,768]{1,0:T(8,128)(2,1)S(1)} %shard_map.287.g_ref.refs_0_), custom_call_target="tpu_custom_call" | custom-call | flops 2200000000 | tf_op jit(solution)/shard_map/pallas_call | solution.py:641
  177.2 2.5 %shard_map.289 = (f32[768,768]{1,0:T(8,128)}, f32[192,3072]{1,0:T(8,128)}) custom-call(s32[3]{0:T(128)S(1)} %pad_add_fusion.rank_ref, bf16[4,192,768]{2,1,0:T(8,128)(2,1)S(1)} %collective-permute-done.51.g_ref, f32[768,768]{1,0:T(8,128)} %get-tuple-element.212.refs_0_, ...), custom_call_target="tpu_custom_call", output_to_operand_aliasing={{0}: (2, {}), {1}: (3, {})} | custom-call | flops 2200000000 | tf_op jit(solution)/shard_map/pallas_call | solution.py:641
  179.7 3.0 %collective-permute-done.50.g_ref.refs_1_ = bf16[400,768]{1,0:T(8,128)(2,1)S(1)} collective-permute-done((bf16[400,768]{1,0:T(8,128)(2,1)S(1)}, bf16[400,768]{1,0:T(8,128)(2,1)S(1)}, u32[]{:S(2)}, u32[]{:S(2)}) %collective-permute-start.50) | collective-permute-done | bytes 614432 | tf_op jit(solution)/shard_map/ppermute | solution.py:594
  182.7 2.7 %shard_map.290 = (f32[192,2304]{1,0:T(8,128)}, f32[192,768]{1,0:T(8,128)}, f32[5,192]{1,0:T(8,128)}, f32[192]{0:T(256)}, f32[192]{0:T(256)}, /*index=5*/f32[192]...) custom-call(s32[3]{0:T(128)S(1)} %pad_add_fusion.rank_ref, ...), custom_call_target="tpu_custom_call", output_to_operand_aliasing={{0}: (4, {}), {1}: (5, {})} | custom-call | flops 2200000000 | tf_op jit(solution)/shard_map/pallas_call | solution.py:641
  (135 shorter events, 51.6 us)
Async XLA Ops:
  2.7 13.8 %collective-permute-start.1 = (bf16[272,768]{1,0:T(8,128)(2,1)}, bf16[272,768]{1,0:T(8,128)(2,1)}, u32[]{:S(2)}, u32[]{:S(2)}) collective-permute-start(bf16[272,768]{1,0:T(8,128)(2,1)} %shard_map.263.x0), channel_id=1, source_target_pairs={{0,2},{1,3},{2,0},{3,1},{4,6},{5,7},{6,4},{7,5},{8,10},{9,11},{10,... | collective-permute-start | bytes 1253384 | tf_op jit(solution)/shard_map/ppermute | solution.py:540
  6.6 19.3 %collective-permute-start.4 = (bf16[288,768]{1,0:T(8,128)(2,1)S(1)}, bf16[288,768]{1,0:T(8,128)(2,1)S(1)}, u32[]{:S(2)}, u32[]{:S(2)}) collective-permute-start(bf16[288,768]{1,0:T(8,128)(2,1)S(1)} %get-tuple-element.135), channel_id=1, source_target_pairs={{0,2},{1,3},{2,0},{3,1},{4,6},{5,7},{6,4},{7,5},{8,10},{9,11},{10,... | collective-permute-start | bytes 1327112 | tf_op jit(solution)/shard_map/ppermute | solution.py:540
  6.6 12.1 %collective-permute-start = (bf16[272,768]{1,0:T(8,128)(2,1)}, bf16[272,768]{1,0:T(8,128)(2,1)S(1)}, u32[]{:S(2)}, u32[]{:S(2)}) collective-permute-start(bf16[272,768]{1,0:T(8,128)(2,1)} %shard_map.263.x0), channel_id=1, source_target_pairs={{0,1},{1,0},{2,3},{3,2},{4,5},{5,4},{6,7},{7,6},{8,9},{9,8},{10,11... | collective-permute-start | bytes 1253384 | tf_op jit(solution)/shard_map/ppermute | solution.py:536
  16.5 23.3 %collective-permute-start.8 = (bf16[448,768]{1,0:T(8,128)(2,1)S(1)}, bf16[448,768]{1,0:T(8,128)(2,1)S(1)}, u32[]{:S(2)}, u32[]{:S(2)}) collective-permute-start(bf16[448,768]{1,0:T(8,128)(2,1)S(1)} %get-tuple-element.142), channel_id=1, source_target_pairs={{0,2},{1,3},{2,0},{3,1},{4,6},{5,7},{6,4},{7,5},{8,10},{9,11},{10,... | collective-permute-start | bytes 2064392 | tf_op jit(solution)/shard_map/ppermute | solution.py:540
  39.9 7.9 %collective-permute-start.9 = (bf16[128,768]{1,0:T(8,128)(2,1)S(1)}, bf16[128,768]{1,0:T(8,128)(2,1)S(1)}, u32[]{:S(2)}, u32[]{:S(2)}) collective-permute-start(bf16[128,768]{1,0:T(8,128)(2,1)S(1)} %get-tuple-element.237), channel_id=1, source_target_pairs={{0,2},{1,3},{2,0},{3,1},{4,6},{5,7},{6,4},{7,5},{8,10},{9,11},{10,... | collective-permute-start | bytes 589832 | tf_op jit(solution)/shard_map/ppermute | solution.py:540
  41.6 9.3 %collective-permute-start.11 = (bf16[192,768]{1,0:T(8,128)(2,1)S(1)}, bf16[192,768]{1,0:T(8,128)(2,1)S(1)}, u32[]{:S(2)}, u32[]{:S(2)}) collective-permute-start(bf16[192,768]{1,0:T(8,128)(2,1)S(1)} %slice.104), channel_id=1, source_target_pairs={{0,4},{1,5},{2,6},{3,7},{4,1},{5,0},{6,3},{7,2},{8,12},{9,13},{10,... | collective-permute-start | bytes 884744 | tf_op jit(solution)/shard_map/ppermute | solution.py:679
  43.2 8.0 %collective-permute-start.10 = (bf16[128,768]{1,0:T(8,128)(2,1)S(1)}, bf16[128,768]{1,0:T(8,128)(2,1)S(1)}, u32[]{:S(2)}, u32[]{:S(2)}) collective-permute-start(bf16[128,768]{1,0:T(8,128)(2,1)S(1)} %get-tuple-element.236), channel_id=1, source_target_pairs={{0,2},{1,3},{2,0},{3,1},{4,6},{5,7},{6,4},{7,5},{8,10},{9,11},{10,... | collective-permute-start | bytes 589832 | tf_op jit(solution)/shard_map/ppermute | solution.py:540
  48.2 13.9 %collective-permute-start.18 = (bf16[448,768]{1,0:T(8,128)(2,1)S(1)}, bf16[448,768]{1,0:T(8,128)(2,1)S(1)}, u32[]{:S(2)}, u32[]{:S(2)}) collective-permute-start(bf16[448,768]{1,0:T(8,128)(2,1)S(1)} %get-tuple-element.149), channel_id=1, source_target_pairs={{0,1},{1,0},{2,3},{3,2},{4,5},{5,4},{6,7},{7,6},{8,9},{9,8},{10,11... | collective-permute-start | bytes 2064392 | tf_op jit(solution)/shard_map/ppermute | solution.py:536
  48.6 13.5 %collective-permute-start.19 = (bf16[448,768]{1,0:T(8,128)(2,1)S(1)}, bf16[448,768]{1,0:T(8,128)(2,1)S(1)}, u32[]{:S(2)}, u32[]{:S(2)}) collective-permute-start(bf16[448,768]{1,0:T(8,128)(2,1)S(1)} %collective-permute-done.8.g2), channel_id=1, source_target_pairs={{0,1},{1,0},{2,3},{3,2},{4,5},{5,4},{6,7},{7,6},{8,9},{9,8},{10,11... | collective-permute-start | bytes 2064392 | tf_op jit(solution)/shard_map/ppermute | solution.py:536
  51.4 10.6 %collective-permute-start.15 = (bf16[128,768]{1,0:T(8,128)(2,1)S(1)}, bf16[128,768]{1,0:T(8,128)(2,1)S(1)}, u32[]{:S(2)}, u32[]{:S(2)}) collective-permute-start(bf16[128,768]{1,0:T(8,128)(2,1)S(1)} %get-tuple-element.148.m0), channel_id=1, source_target_pairs={{0,2},{1,3},{2,0},{3,1},{4,6},{5,7},{6,4},{7,5},{8,10},{9,11},{10,... | collective-permute-start | bytes 589832 | tf_op jit(solution)/shard_map/ppermute | solution.py:540
  53.3 8.8 %collective-permute-start.13 = (bf16[128,768]{1,0:T(8,128)(2,1)S(1)}, bf16[128,768]{1,0:T(8,128)(2,1)S(1)}, u32[]{:S(2)}, u32[]{:S(2)}) collective-permute-start(bf16[128,768]{1,0:T(8,128)(2,1)S(1)} %get-tuple-element.148.m0), channel_id=1, source_target_pairs={{0,1},{1,0},{2,3},{3,2},{4,5},{5,4},{6,7},{7,6},{8,9},{9,8},{10,11... | collective-permute-start | bytes 589832 | tf_op jit(solution)/shard_map/ppermute | solution.py:536
  70.7 7.8 %collective-permute-start.27 = (bf16[128,768]{1,0:T(8,128)(2,1)S(1)}, bf16[128,768]{1,0:T(8,128)(2,1)S(1)}, u32[]{:S(2)}, u32[]{:S(2)}) collective-permute-start(bf16[128,768]{1,0:T(8,128)(2,1)S(1)} %get-tuple-element.234), channel_id=1, source_target_pairs={{0,2},{1,3},{2,0},{3,1},{4,6},{5,7},{6,4},{7,5},{8,10},{9,11},{10,... | collective-permute-start | bytes 589832 | tf_op jit(solution)/shard_map/ppermute | solution.py:540
  71.2 11.6 %collective-permute-start.23 = (bf16[128,768]{1,0:T(8,128)(2,1)S(1)}, bf16[128,768]{1,0:T(8,128)(2,1)S(1)}, u32[]{:S(2)}, u32[]{:S(2)}) collective-permute-start(bf16[128,768]{1,0:T(8,128)(2,1)S(1)} %get-tuple-element.235), channel_id=1, source_target_pairs={{0,2},{1,3},{2,0},{3,1},{4,6},{5,7},{6,4},{7,5},{8,10},{9,11},{10,... | collective-permute-start | bytes 589832 | tf_op jit(solution)/shard_map/ppermute | solution.py:540
  76.6 16.3 %collective-permute-start.21 = (bf16[4,192,768]{2,1,0:T(8,128)(2,1)S(1)}, bf16[4,192,768]{2,1,0:T(8,128)(2,1)S(1)}, u32[]{:S(2)}, u32[]{:S(2)}) collective-permute-start(bf16[4,192,768]{2,1,0:T(8,128)(2,1)S(1)} %get-tuple-element.156), channel_id=1, source_target_pairs={{0,4},{1,9},{2,6},{3,11},{4,0},{5,13},{6,2},{7,15},{8,12},{9,1},{1... | collective-permute-start | bytes 3538952 | tf_op jit(solution)/shard_map/ppermute | solution.py:594
  79.1 7.8 %collective-permute-start.30 = (bf16[128,768]{1,0:T(8,128)(2,1)S(1)}, bf16[128,768]{1,0:T(8,128)(2,1)S(1)}, u32[]{:S(2)}, u32[]{:S(2)}) collective-permute-start(bf16[128,768]{1,0:T(8,128)(2,1)S(1)} %get-tuple-element.164.f0), channel_id=1, source_target_pairs={{0,2},{1,3},{2,0},{3,1},{4,6},{5,7},{6,4},{7,5},{8,10},{9,11},{10,... | collective-permute-start | bytes 589832 | tf_op jit(solution)/shard_map/ppermute | solution.py:540
  83.7 11.1 %collective-permute-start.28 = (bf16[128,768]{1,0:T(8,128)(2,1)S(1)}, bf16[128,768]{1,0:T(8,128)(2,1)S(1)}, u32[]{:S(2)}, u32[]{:S(2)}) collective-permute-start(bf16[128,768]{1,0:T(8,128)(2,1)S(1)} %get-tuple-element.164.f0), channel_id=1, source_target_pairs={{0,1},{1,0},{2,3},{3,2},{4,5},{5,4},{6,7},{7,6},{8,9},{9,8},{10,11... | collective-permute-start | bytes 589832 | tf_op jit(solution)/shard_map/ppermute | solution.py:536
  87.0 7.9 %collective-permute-start.32 = (bf16[128,768]{1,0:T(8,128)(2,1)S(1)}, bf16[128,768]{1,0:T(8,128)(2,1)S(1)}, u32[]{:S(2)}, u32[]{:S(2)}) collective-permute-start(bf16[128,768]{1,0:T(8,128)(2,1)S(1)} %collective-permute-done.30.f2), channel_id=1, source_target_pairs={{0,1},{1,0},{2,3},{3,2},{4,5},{5,4},{6,7},{7,6},{8,9},{9,8},{10,11... | collective-permute-start | bytes 589832 | tf_op jit(solution)/shard_map/ppermute | solution.py:536
  93.2 10.0 %collective-permute-start.25 = (bf16[2,192,768]{2,1,0:T(8,128)(2,1)S(1)}, bf16[2,192,768]{2,1,0:T(8,128)(2,1)S(1)}, u32[]{:S(2)}, u32[]{:S(2)}) collective-permute-start(bf16[2,192,768]{2,1,0:T(8,128)(2,1)S(1)} %slice.108), channel_id=1, source_target_pairs={{0,8},{1,5},{2,10},{3,7},{4,12},{5,1},{6,14},{7,3},{8,0},{9,13},{1... | collective-permute-start | bytes 1769480 | tf_op jit(solution)/shard_map/ppermute | solution.py:594
  103.4 14.1 %collective-permute-start.26 = (bf16[1,192,768]{2,1,0:T(8,128)(2,1)S(1)}, bf16[1,192,768]{2,1,0:T(8,128)(2,1)S(1)}, u32[]{:S(2)}, u32[]{:S(2)}) collective-permute-start(bf16[1,192,768]{2,1,0:T(8,128)(2,1)S(1)} %slice.110), channel_id=1, source_target_pairs={{0,16},{1,17},{2,18},{3,19},{4,20},{5,21},{6,22},{7,23},{8,24},{9,... | collective-permute-start | bytes 884744 | tf_op jit(solution)/shard_map/ppermute | solution.py:594
  109.4 11.7 %collective-permute-start.34 = (bf16[512,768]{1,0:T(8,128)(2,1)S(1)}, bf16[512,768]{1,0:T(8,128)(2,1)S(1)}, u32[]{:S(2)}, u32[]{:S(2)}) collective-permute-start(bf16[512,768]{1,0:T(8,128)(2,1)S(1)} %get-tuple-element.175.send_ref), channel_id=1, source_target_pairs={{0,1},{1,0},{2,3},{3,2},{4,5},{5,4},{6,7},{7,6},{8,9},{9,8},{10,11... | collective-permute-start | bytes 2359304 | tf_op jit(solution)/shard_map/ppermute | solution.py:536
  109.5 10.1 %collective-permute-start.35 = (bf16[4,96,768]{2,1,0:T(8,128)(2,1)S(1)}, bf16[4,96,768]{2,1,0:T(8,128)(2,1)S(1)}, u32[]{:S(2)}, u32[]{:S(2)}) collective-permute-start(bf16[4,96,768]{2,1,0:T(8,128)(2,1)S(1)} %get-tuple-element.176), channel_id=1, source_target_pairs={{0,4},{1,9},{2,6},{3,11},{4,0},{5,13},{6,2},{7,15},{8,12},{9,1},{1... | collective-permute-start | bytes 1769480 | tf_op jit(solution)/shard_map/ppermute | solution.py:594
  119.7 12.7 %collective-permute-start.39 = (bf16[2,96,768]{2,1,0:T(8,128)(2,1)S(1)}, bf16[2,96,768]{2,1,0:T(8,128)(2,1)S(1)}, u32[]{:S(2)}, u32[]{:S(2)}) collective-permute-start(bf16[2,96,768]{2,1,0:T(8,128)(2,1)S(1)} %get-tuple-element.178), channel_id=1, source_target_pairs={{0,8},{1,5},{2,10},{3,7},{4,12},{5,1},{6,14},{7,3},{8,0},{9,13},{1... | collective-permute-start | bytes 884744 | tf_op jit(solution)/shard_map/ppermute | solution.py:594
  121.3 9.8 %collective-permute-start.40 = (bf16[256,768]{1,0:T(8,128)(2,1)S(1)}, bf16[256,768]{1,0:T(8,128)(2,1)S(1)}, u32[]{:S(2)}, u32[]{:S(2)}) collective-permute-start(bf16[256,768]{1,0:T(8,128)(2,1)S(1)} %add_convert_fusion.3), channel_id=1, source_target_pairs={{0,2},{1,3},{2,0},{3,1},{4,6},{5,7},{6,4},{7,5},{8,10},{9,11},{10,... | collective-permute-start | bytes 1179656 | tf_op jit(solution)/shard_map/ppermute | solution.py:540
  122.3 15.9 %collective-permute-start.42 = (bf16[1,192,768]{2,1,0:T(8,128)(2,1)S(1)}, bf16[1,192,768]{2,1,0:T(8,128)(2,1)S(1)}, u32[]{:S(2)}, u32[]{:S(2)}) collective-permute-start(bf16[1,192,768]{2,1,0:T(8,128)(2,1)S(1)} %maximum_bitcast_fusion.a_ref), channel_id=1, source_target_pairs={{0,16},{1,17},{2,18},{3,19},{4,20},{5,21},{6,22},{7,23},{8,24},{9,... | collective-permute-start | bytes 884744 | tf_op jit(solution)/shard_map/ppermute | solution.py:594
  126.6 21.0 %collective-permute-start.38 = (bf16[512,768]{1,0:T(8,128)(2,1)S(1)}, bf16[512,768]{1,0:T(8,128)(2,1)S(1)}, u32[]{:S(2)}, u32[]{:S(2)}) collective-permute-start(bf16[512,768]{1,0:T(8,128)(2,1)S(1)} %get-tuple-element.185), channel_id=1, source_target_pairs={{0,1},{1,0},{2,3},{3,2},{4,5},{5,4},{6,7},{7,6},{8,9},{9,8},{10,11... | collective-permute-start | bytes 2359304 | tf_op jit(solution)/shard_map/ppermute | solution.py:536
  132.5 12.3 %collective-permute-start.41 = (bf16[1,96,768]{2,1,0:T(8,128)(2,1)S(1)}, bf16[1,96,768]{2,1,0:T(8,128)(2,1)S(1)}, u32[]{:S(2)}, u32[]{:S(2)}) collective-permute-start(bf16[1,96,768]{2,1,0:T(8,128)(2,1)S(1)} %get-tuple-element.199), channel_id=1, source_target_pairs={{0,16},{1,17},{2,18},{3,19},{4,20},{5,21},{6,22},{7,23},{8,24},{9,... | collective-permute-start | bytes 442376 | tf_op jit(solution)/shard_map/ppermute | solution.py:594
  138.2 14.0 %collective-permute-start.48 = (bf16[2,192,768]{2,1,0:T(8,128)(2,1)S(1)}, bf16[2,192,768]{2,1,0:T(8,128)(2,1)S(1)}, u32[]{:S(2)}, u32[]{:S(2)}) collective-permute-start(bf16[2,192,768]{2,1,0:T(8,128)(2,1)S(1)} %shard_map.281.a_ref), channel_id=1, source_target_pairs={{0,8},{1,5},{2,10},{3,7},{4,12},{5,1},{6,14},{7,3},{8,0},{9,13},{1... | collective-permute-start | bytes 1769480 | tf_op jit(solution)/shard_map/ppermute | solution.py:594
  151.2 10.7 %collective-permute-start.47 = (bf16[112,768]{1,0:T(8,128)(2,1)S(1)}, bf16[112,768]{1,0:T(8,128)(2,1)S(1)}, u32[]{:S(2)}, u32[]{:S(2)}) collective-permute-start(bf16[112,768]{1,0:T(8,128)(2,1)S(1)} %shard_map.283.a_ref), channel_id=1, source_target_pairs={{0,16},{1,17},{2,18},{3,19},{4,20},{5,21},{6,22},{7,23},{8,24},{9,... | collective-permute-start | bytes 516104 | tf_op jit(solution)/shard_map/ppermute | solution.py:594
  152.3 24.9 %collective-permute-start.51 = (bf16[4,192,768]{2,1,0:T(8,128)(2,1)S(1)}, bf16[4,192,768]{2,1,0:T(8,128)(2,1)S(1)}, u32[]{:S(2)}, u32[]{:S(2)}) collective-permute-start(bf16[4,192,768]{2,1,0:T(8,128)(2,1)S(1)} %shard_map.284.g_ref), channel_id=1, source_target_pairs={{0,4},{1,9},{2,6},{3,11},{4,0},{5,13},{6,2},{7,15},{8,12},{9,1},{1... | collective-permute-start | bytes 3538952 | tf_op jit(solution)/shard_map/ppermute | solution.py:594
  161.9 10.5 %collective-permute-start.49 = (bf16[208,768]{1,0:T(8,128)(2,1)S(1)}, bf16[208,768]{1,0:T(8,128)(2,1)S(1)}, u32[]{:S(2)}, u32[]{:S(2)}) collective-permute-start(bf16[208,768]{1,0:T(8,128)(2,1)S(1)} %shard_map.286.a_ref), channel_id=1, source_target_pairs={{0,8},{1,5},{2,10},{3,7},{4,12},{5,1},{6,14},{7,3},{8,0},{9,13},{1... | collective-permute-start | bytes 958472 | tf_op jit(solution)/shard_map/ppermute | solution.py:594
  162.0 11.7 %collective-permute-start.44 = (bf16[256,768]{1,0:T(8,128)(2,1)S(1)}, bf16[256,768]{1,0:T(8,128)(2,1)S(1)}, u32[]{:S(2)}, u32[]{:S(2)}) collective-permute-start(bf16[256,768]{1,0:T(8,128)(2,1)S(1)} %add_convert_fusion.2), channel_id=1, source_target_pairs={{0,2},{1,3},{2,0},{3,1},{4,6},{5,7},{6,4},{7,5},{8,10},{9,11},{10,... | collective-permute-start | bytes 1179656 | tf_op jit(solution)/shard_map/ppermute | solution.py:540
  172.5 10.2 %collective-permute-start.50 = (bf16[400,768]{1,0:T(8,128)(2,1)S(1)}, bf16[400,768]{1,0:T(8,128)(2,1)S(1)}, u32[]{:S(2)}, u32[]{:S(2)}) collective-permute-start(bf16[400,768]{1,0:T(8,128)(2,1)S(1)} %shard_map.287.g_ref.refs_0_), channel_id=1, source_target_pairs={{0,4},{1,9},{2,6},{3,11},{4,0},{5,13},{6,2},{7,15},{8,12},{9,1},{1... | collective-permute-start | bytes 1843208 | tf_op jit(solution)/shard_map/ppermute | solution.py:594
  (29 other events, 196.4 us)
